TPU v7x, 256 devices: a whole 4x4x8 slice. The times are simulated.
256 devices in a mesh: gx: 32 (over z_hi, x, y), gy: 8 (over z_lo, core).
Axes of the slice: x: 4, y: 4, z: 8 (z_hi: 2, z_lo: 4; z = z_hi * 4 + z_lo), core: 2. Of those that a mesh axis runs over, the one named last changes fastest.
Arguments:
- motion: float32 [3, 64, 96, 1024], P(None, 'gx', None, 'gy'), may hold values from -6 to 6
- stress: float32 [6, 64, 96, 1024], P(None, 'gx', None, 'gy'), may hold values from -6 to 6
- buoyancy: float32 [64, 96, 1024], P('gx', None, 'gy'), may hold values from 0.5 to 1.5
- lame_first: float32 [64, 96, 1024], P('gx', None, 'gy'), may hold values from 0.5 to 1.5
- lame_shear: float32 [64, 96, 1024], P('gx', None, 'gy'), may hold values from 0.5 to 1.5
- surface: float32 [512, 8192], P('gx', 'gy'), may hold values from -2 to 2
- momentum: float32 [2, 512, 8192], P(None, 'gx', 'gy'), may hold values from -3 to 3
- bathymetry: float32 [512, 8192], P('gx', 'gy'), may hold values from 2 to 4
- wet_mask: int32 [512, 8192], P('gx', 'gy'), may hold values 0 or 1
Outputs:
- final_motion: float32 [3, 64, 96, 1024], P(None, 'gx', None, 'gy')
- final_stress: float32 [6, 64, 96, 1024], P(None, 'gx', None, 'gy')
- final_surface: float32 [512, 8192], P('gx', 'gy')
- final_momentum: float32 [2, 512, 8192], P(None, 'gx', 'gy')
Inputs may be any that keep to these rules, and one draw needn't show every extreme that they name: `wet_mask`: 1 marks a wet ocean cell, 0 a dry one.
All inputs are finite; a program needn't handle non-finite values. No bound on the sum of `wet_mask` on one device may be relied on, other than what follows from the above.
Results may differ from a plain program's by a relative error of at most 0.0001.
Values sent between devices are 32-bit elements; how exact they have to be, the bound alone decides.
No kernel may reach another device: no remote copies, remote signals or barrier semaphores. Data moves between devices by JAX's collectives and lax.ppermute only.
A program may use at most 64 MiB of HBM per device.

v0:
```python
import jax
import jax.numpy as jnp
from jax import lax
from jax.sharding import PartitionSpec as P

RATIO = 8
STEPS = 4
NSUB = 4


SOLID_STEP = 0.2
WAVE_STEP = 0.1
VISCOSITY = 0.05
UPLIFT_GAIN = 0.25
LOAD_GAIN = 8.0


def padded(shard, sides, width):
    for axis, dim in sides:
        size, length = (lax.axis_size(axis), shard.shape[dim])
        up = [(i, (i + 1) % size) for i in range(size - 1)]
        down = [(j, i) for i, j in up]
        last = lax.slice_in_dim(shard, length - width, length, axis=dim)
        first = lax.slice_in_dim(shard, 0, width, axis=dim)
        before = lax.ppermute(last, axis, up)
        after = lax.ppermute(first, axis, down)
        shard = jnp.concatenate([before, shard, after], axis=dim)
    return shard


def from_behind(shard, axis, by):
    size = lax.axis_size(axis)
    pairs = [(i, i + by) for i in range(size) if 0 <= i + by < size]
    return lax.ppermute(shard, axis, pairs)


def middle(quantity):
    return quantity[1:-1, :, 1:-1]


def ahead_x(quantity):
    return quantity[2:, :, 1:-1]


def behind_x(quantity):
    return quantity[:-2, :, 1:-1]


def ahead_y(quantity):
    return quantity[1:-1, :, 2:]


def behind_y(quantity):
    return quantity[1:-1, :, :-2]


def ahead_z(quantity):
    return jnp.concatenate([quantity[:, 1:], jnp.zeros_like(quantity[:, :1])], axis=1)


def behind_z(quantity):
    return jnp.concatenate([jnp.zeros_like(quantity[:, :1]), quantity[:, :-1]], axis=1)


def advance_velocity(motion, stress, buoyancy):
    stress_xx, stress_yy, stress_zz = (stress[0], stress[1], stress[2])
    stress_xy, stress_xz, stress_yz = (stress[3], stress[4], stress[5])
    mid_xy = middle(stress_xy)
    mid_xz = middle(stress_xz)
    mid_yz = middle(stress_yz)
    mid_zz = middle(stress_zz)
    step_rate = SOLID_STEP * buoyancy
    force_x = (
        ahead_x(stress_xx)
        - middle(stress_xx)
        + (mid_xy - behind_y(stress_xy))
        + (mid_xz - behind_z(mid_xz))
    )
    force_y = (
        mid_xy
        - behind_x(stress_xy)
        + (ahead_y(stress_yy) - middle(stress_yy))
        + (mid_yz - behind_z(mid_yz))
    )
    force_z = (
        mid_xz - behind_x(stress_xz) + (mid_yz - behind_y(stress_yz)) + (ahead_z(mid_zz) - mid_zz)
    )
    return jnp.stack(
        [
            motion[0] + step_rate * force_x,
            motion[1] + step_rate * force_y,
            motion[2] + step_rate * force_z,
        ]
    )


def advance_stress(stress, motion, lame_first, lame_shear):
    speed_x, speed_y, speed_z = (motion[0], motion[1], motion[2])
    centre_x = middle(speed_x)
    centre_y = middle(speed_y)
    centre_z = middle(speed_z)
    strain_x = centre_x - behind_x(speed_x)
    strain_y = centre_y - behind_y(speed_y)
    strain_z = centre_z - behind_z(centre_z)
    stiffness = lame_first + 2.0 * lame_shear
    normal_xx = stress[0] + SOLID_STEP * (stiffness * strain_x + lame_first * (strain_y + strain_z))
    normal_yy = stress[1] + SOLID_STEP * (stiffness * strain_y + lame_first * (strain_x + strain_z))
    normal_zz = stress[2] + SOLID_STEP * (stiffness * strain_z + lame_first * (strain_x + strain_y))
    shear_rate = SOLID_STEP * lame_shear
    shear_xy = stress[3] + shear_rate * (
        ahead_y(speed_x) - centre_x + (ahead_x(speed_y) - centre_y)
    )
    shear_xz = stress[4] + shear_rate * (
        ahead_z(centre_x) - centre_x + (ahead_x(speed_z) - centre_z)
    )
    shear_yz = stress[5] + shear_rate * (
        ahead_z(centre_y) - centre_y + (ahead_y(speed_z) - centre_z)
    )
    return jnp.stack([normal_xx, normal_yy, normal_zz, shear_xy, shear_xz, shear_yz])


def apply_load(stress, seafloor_load):
    return stress.at[2, :, 0, :].set(-LOAD_GAIN * seafloor_load)


def interior(quantity):
    return quantity[1:-1, 1:-1]


def wave_substep(ocean_state, seabed):
    height, flow_x, flow_y = (ocean_state[0], ocean_state[1], ocean_state[2])
    depth_in = seabed[0, 1:-1, 1:-1]
    wet_full = seabed[1]
    wet_in = wet_full[1:-1, 1:-1]
    extent_x, extent_y = height.shape
    height_new = height[1:, 1:] - WAVE_STEP * wet_in[1:, 1:] * (
        flow_x[1:, 1:] - flow_x[:-1, 1:] + (flow_y[1:, 1:] - flow_y[1:, :-1])
    )
    centre = height_new[:-1, :-1]
    east_side = height_new[1:, :-1]
    north_side = height_new[:-1, 1:]
    face_x = wet_full[:-1, :] * wet_full[1:, :]
    face_y = wet_full[:, :-1] * wet_full[:, 1:]
    flow_cx = interior(flow_x)
    spread_x = (
        face_x[3 : extent_x + 1, 2:extent_y] * (flow_x[2:, 1:-1] - flow_cx)
        + face_x[1 : extent_x - 1, 2:extent_y] * (flow_x[:-2, 1:-1] - flow_cx)
        + face_x[2:extent_x, 3 : extent_y + 1] * (flow_x[1:-1, 2:] - flow_cx)
        + face_x[2:extent_x, 1 : extent_y - 1] * (flow_x[1:-1, :-2] - flow_cx)
    )
    flow_cy = interior(flow_y)
    spread_y = (
        face_y[3 : extent_x + 1, 2:extent_y] * (flow_y[2:, 1:-1] - flow_cy)
        + face_y[1 : extent_x - 1, 2:extent_y] * (flow_y[:-2, 1:-1] - flow_cy)
        + face_y[2:extent_x, 3 : extent_y + 1] * (flow_y[1:-1, 2:] - flow_cy)
        + face_y[2:extent_x, 1 : extent_y - 1] * (flow_y[1:-1, :-2] - flow_cy)
    )
    depth_c = interior(depth_in)
    depth_east = depth_in[2:, 1:-1]
    depth_north = depth_in[1:-1, 2:]
    new_flow_x = face_x[2:extent_x, 2:extent_y] * (
        flow_cx
        - WAVE_STEP * 0.5 * (depth_c + depth_east + centre + east_side) * (east_side - centre)
        + VISCOSITY * spread_x
    )
    new_flow_y = face_y[2:extent_x, 2:extent_y] * (
        flow_cy
        - WAVE_STEP * 0.5 * (depth_c + depth_north + centre + north_side) * (north_side - centre)
        + VISCOSITY * spread_y
    )
    return jnp.stack([centre, new_flow_x, new_flow_y])


def upsample(coarse):
    count_x, count_y = coarse.shape
    spread_out = jnp.broadcast_to(coarse[:, None, :, None], (count_x, RATIO, count_y, RATIO))
    return spread_out.reshape(count_x * RATIO, count_y * RATIO)


def block_average(fine_grid):
    count_x, count_y = fine_grid.shape
    return jnp.mean(
        fine_grid.reshape(count_x // RATIO, RATIO, count_y // RATIO, RATIO), axis=(1, 3)
    )


def body(motion, stress, buoyancy, lame_first, lame_shear, surface, momentum, bathymetry, wet_mask):
    half_rows = motion.shape[1] // 2
    wet_float = wet_mask.astype(jnp.float32)
    seabed = jnp.stack([bathymetry, wet_float])
    seabed_ext = padded(seabed, (("gx", 1), ("gy", 2)), 2)
    ocean_state = jnp.concatenate([surface[None], momentum], axis=0)
    for coupling_step in range(STEPS):
        top_speed = motion[2, :, 0, :]
        incoming = from_behind(top_speed[half_rows:], "gx", 1)
        uplift = jnp.concatenate([incoming, top_speed[:half_rows]], axis=0)
        lifted = ocean_state[0] + UPLIFT_GAIN * wet_float * upsample(uplift)
        ocean_state = ocean_state.at[0].set(lifted)
        for substep in range(NSUB):
            ocean_ext = padded(ocean_state, (("gx", 1), ("gy", 2)), 1)
            ocean_state = wave_substep(ocean_ext, seabed_ext)
        averaged = block_average(wet_float * ocean_state[0])
        returned = from_behind(averaged[:half_rows], "gx", -1)
        seafloor_load = jnp.concatenate([averaged[half_rows:], returned], axis=0)
        stress_ext = padded(stress, (("gx", 1), ("gy", 3)), 1)
        motion = advance_velocity(motion, stress_ext, buoyancy)
        motion_ext = padded(motion, (("gx", 1), ("gy", 3)), 1)
        stress = advance_stress(stress, motion_ext, lame_first, lame_shear)
        stress = apply_load(stress, seafloor_load)
    return (motion, stress, ocean_state[0], ocean_state[1:])


def solution(mesh):
    return jax.shard_map(
        body,
        mesh=mesh,
        in_specs=(
            P(None, "gx", None, "gy"),
            P(None, "gx", None, "gy"),
            P("gx", None, "gy"),
            P("gx", None, "gy"),
            P("gx", None, "gy"),
            P("gx", "gy"),
            P(None, "gx", "gy"),
            P("gx", "gy"),
            P("gx", "gy"),
        ),
        out_specs=(
            P(None, "gx", None, "gy"),
            P(None, "gx", None, "gy"),
            P("gx", "gy"),
            P(None, "gx", "gy"),
        ),
        check_vma=False,
    )
```

profile of v0, /device:TPU:192, one launch (start us, length us, event | category | flops | bytes accessed | tf_op | source)
XLA Modules:
  0.0 767.6 jit_solution(17684907863241918610)
XLA Ops:
  6.7 8.3 %collective-permute-done.8 = f32[1,128]{1,0:T(1,128)S(1)} collective-permute-done((f32[1,128]{1,0:T(1,128)S(1)}, f32[1,128]{1,0:T(1,128)S(1)}, u32[]{:S(2)}, u32[]{:S(2)}) %collective-permute-start.8) | collective-permute-done | bytes 544 | tf_op jit(solution)/shard_map/ppermute | solution.py:34
  21.7 10.3 %collective-permute-start.14 = (f32[2,2,1024]{2,1,0:T(2,128)S(1)}, f32[2,2,1024]{2,1,0:T(2,128)S(1)}, u32[]{:S(2)}, u32[]{:S(2)}) collective-permute-start(f32[2,2,1024]{2,1,0:T(2,128)S(1)} %get-tuple-element.320), channel_id=1, source_target_pairs={{8,0},{16,8},{24,16},{32,24},{40,32},{48,40},{56,48},{64,56},{72,6... | collective-permute-start | bytes 49160 | tf_op jit(solution)/shard_map/ppermute | solution.py:26
  41.4 4.3 collective-permute-done.13
  54.1 7.8 %collective-permute-start.18 = (f32[3,1,1024]{2,1,0:T(1,128)S(1)}, f32[3,1,1024]{2,1,0:T(1,128)S(1)}, u32[]{:S(2)}, u32[]{:S(2)}) collective-permute-start(f32[3,1,1024]{2,1,0:T(1,128)S(1)} %get-tuple-element.314), channel_id=1, source_target_pairs={{8,0},{16,8},{24,16},{32,24},{40,32},{48,40},{56,48},{64,56},{72,6... | collective-permute-start | bytes 36872 | tf_op jit(solution)/shard_map/ppermute | solution.py:26
  63.8 11.9 %collective-permute-done.17 = f32[3,1,1024]{2,1,0:T(1,128)S(1)} collective-permute-done((f32[3,1,1024]{2,1,0:T(1,128)S(1)}, f32[3,1,1024]{2,1,0:T(1,128)S(1)}, u32[]{:S(2)}, u32[]{:S(2)}) %collective-permute-start.17) | collective-permute-done | bytes 12320 | tf_op jit(solution)/shard_map/ppermute | solution.py:25
  85.9 3.9 collective-permute-start.21
  90.9 10.0 %collective-permute-start.1 = (f32[6,1,96,128]{2,1,3,0:T(1,128)}, f32[6,1,96,128]{2,1,3,0:T(1,128)S(1)}, u32[]{:S(2)}, u32[]{:S(2)}) collective-permute-start(f32[6,1,96,128]{2,1,3,0:T(1,128)} %copy.84), channel_id=1, source_target_pairs={{8,0},{16,8},{24,16},{32,24},{40,32},{48,40},{56,48},{64,56},{72,6... | collective-permute-start | bytes 884744 | tf_op jit(solution)/shard_map/ppermute | solution.py:26
  112.3 10.3 %collective-permute-start.26 = (f32[3,1,1024]{2,1,0:T(1,128)S(1)}, f32[3,1,1024]{2,1,0:T(1,128)S(1)}, u32[]{:S(2)}, u32[]{:S(2)}) collective-permute-start(f32[3,1,1024]{2,1,0:T(1,128)S(1)} %get-tuple-element.310), channel_id=1, source_target_pairs={{8,0},{16,8},{24,16},{32,24},{40,32},{48,40},{56,48},{64,56},{72,6... | collective-permute-start | bytes 36872 | tf_op jit(solution)/shard_map/ppermute | solution.py:26
  125.9 11.2 %collective-permute-done.25 = f32[3,1,1024]{2,1,0:T(1,128)S(1)} collective-permute-done((f32[3,1,1024]{2,1,0:T(1,128)S(1)}, f32[3,1,1024]{2,1,0:T(1,128)S(1)}, u32[]{:S(2)}, u32[]{:S(2)}) %collective-permute-start.25) | collective-permute-done | bytes 12320 | tf_op jit(solution)/shard_map/ppermute | solution.py:25
  160.5 11.6 %collective-permute-done.38 = f32[1,128]{1,0:T(1,128)S(1)} collective-permute-done((f32[1,128]{1,0:T(1,128)S(1)}, f32[1,128]{1,0:T(1,128)S(1)}, u32[]{:S(2)}, u32[]{:S(2)}) %collective-permute-start.38) | collective-permute-done | bytes 544 | tf_op jit(solution)/shard_map/ppermute | solution.py:34
  177.0 3.9 collective-permute-start.39
  184.3 6.4 collective-permute-done.39
  206.5 11.5 %collective-permute-done.43 = f32[3,1,1024]{2,1,0:T(1,128)S(1)} collective-permute-done((f32[3,1,1024]{2,1,0:T(1,128)S(1)}, f32[3,1,1024]{2,1,0:T(1,128)S(1)}, u32[]{:S(2)}, u32[]{:S(2)}) %collective-permute-start.43) | collective-permute-done | bytes 12320 | tf_op jit(solution)/shard_map/ppermute | solution.py:25
  231.0 3.9 collective-permute-start.47
  235.3 9.4 %collective-permute-done.47 = f32[3,1,1024]{2,1,0:T(1,128)S(1)} collective-permute-done((f32[3,1,1024]{2,1,0:T(1,128)S(1)}, f32[3,1,1024]{2,1,0:T(1,128)S(1)}, u32[]{:S(2)}, u32[]{:S(2)}) %collective-permute-start.47) | collective-permute-done | bytes 12320 | tf_op jit(solution)/shard_map/ppermute | solution.py:25
  254.9 3.9 collective-permute-start.51
  259.9 10.0 %collective-permute-start.5 = (f32[3,1,96,128]{2,1,3,0:T(1,128)}, f32[3,1,96,128]{2,1,3,0:T(1,128)S(1)}, u32[]{:S(2)}, u32[]{:S(2)}) collective-permute-start(f32[3,1,96,128]{2,1,3,0:T(1,128)} %get-tuple-element.199), channel_id=1, source_target_pairs={{8,0},{16,8},{24,16},{32,24},{40,32},{48,40},{56,48},{64,56},{72,6... | collective-permute-start | bytes 442376 | tf_op jit(solution)/shard_map/ppermute | solution.py:26
  279.4 12.2 %collective-permute-done.4 = f32[3,1,96,128]{2,1,3,0:T(1,128)S(1)} collective-permute-done((f32[3,1,96,128]{2,1,3,0:T(1,128)}, f32[3,1,96,128]{2,1,3,0:T(1,128)S(1)}, u32[]{:S(2)}, u32[]{:S(2)}) %collective-permute-start.4) | collective-permute-done | bytes 147488 | tf_op jit(solution)/shard_map/ppermute | solution.py:25
  306.6 3.9 collective-permute-start.30
  311.0 11.7 %collective-permute-done.31 = f32[6,1,96,128]{2,1,3,0:T(1,128)S(1)} collective-permute-done((f32[6,1,96,128]{2,1,3,0:T(1,128)S(1)}, f32[6,1,96,128]{2,1,3,0:T(1,128)S(1)}, u32[]{:S(2)}, u32[]{:S(2)}) %collective-permute-start.31) | collective-permute-done | bytes 294944 | tf_op jit(solution)/shard_map/ppermute | solution.py:26
  322.7 12.5 %collective-permute-done.30 = f32[6,1,96,128]{2,1,3,0:T(1,128)S(1)} collective-permute-done((f32[6,1,96,128]{2,1,3,0:T(1,128)S(1)}, f32[6,1,96,128]{2,1,3,0:T(1,128)S(1)}, u32[]{:S(2)}, u32[]{:S(2)}) %collective-permute-start.30) | collective-permute-done | bytes 294944 | tf_op jit(solution)/shard_map/ppermute | solution.py:25
  348.2 11.6 %collective-permute-done.64 = f32[1,128]{1,0:T(1,128)S(1)} collective-permute-done((f32[1,128]{1,0:T(1,128)S(1)}, f32[1,128]{1,0:T(1,128)S(1)}, u32[]{:S(2)}, u32[]{:S(2)}) %collective-permute-start.64) | collective-permute-done | bytes 544 | tf_op jit(solution)/shard_map/ppermute | solution.py:34
  364.7 3.9 collective-permute-start.65
  371.6 6.8 collective-permute-done.65
  395.2 11.1 %collective-permute-done.69 = f32[3,1,1024]{2,1,0:T(1,128)S(1)} collective-permute-done((f32[3,1,1024]{2,1,0:T(1,128)S(1)}, f32[3,1,1024]{2,1,0:T(1,128)S(1)}, u32[]{:S(2)}, u32[]{:S(2)}) %collective-permute-start.69) | collective-permute-done | bytes 12320 | tf_op jit(solution)/shard_map/ppermute | solution.py:25
  418.6 3.9 collective-permute-start.73
  422.9 9.4 %collective-permute-done.73 = f32[3,1,1024]{2,1,0:T(1,128)S(1)} collective-permute-done((f32[3,1,1024]{2,1,0:T(1,128)S(1)}, f32[3,1,1024]{2,1,0:T(1,128)S(1)}, u32[]{:S(2)}, u32[]{:S(2)}) %collective-permute-start.73) | collective-permute-done | bytes 12320 | tf_op jit(solution)/shard_map/ppermute | solution.py:25
  445.2 3.9 collective-permute-start.77
  450.1 10.0 %collective-permute-start.35 = (f32[3,1,96,128]{2,1,3,0:T(1,128)}, f32[3,1,96,128]{2,1,3,0:T(1,128)S(1)}, u32[]{:S(2)}, u32[]{:S(2)}) collective-permute-start(f32[3,1,96,128]{2,1,3,0:T(1,128)} %get-tuple-element.197), channel_id=1, source_target_pairs={{8,0},{16,8},{24,16},{32,24},{40,32},{48,40},{56,48},{64,56},{72,6... | collective-permute-start | bytes 442376 | tf_op jit(solution)/shard_map/ppermute | solution.py:26
  469.7 11.9 %collective-permute-done.34 = f32[3,1,96,128]{2,1,3,0:T(1,128)S(1)} collective-permute-done((f32[3,1,96,128]{2,1,3,0:T(1,128)}, f32[3,1,96,128]{2,1,3,0:T(1,128)S(1)}, u32[]{:S(2)}, u32[]{:S(2)}) %collective-permute-start.34) | collective-permute-done | bytes 147488 | tf_op jit(solution)/shard_map/ppermute | solution.py:25
  502.5 12.0 %collective-permute-done.57 = f32[6,1,96,128]{2,1,3,0:T(1,128)S(1)} collective-permute-done((f32[6,1,96,128]{2,1,3,0:T(1,128)S(1)}, f32[6,1,96,128]{2,1,3,0:T(1,128)S(1)}, u32[]{:S(2)}, u32[]{:S(2)}) %collective-permute-start.57) | collective-permute-done | bytes 294944 | tf_op jit(solution)/shard_map/ppermute | solution.py:26
  514.5 12.5 %collective-permute-done.56 = f32[6,1,96,128]{2,1,3,0:T(1,128)S(1)} collective-permute-done((f32[6,1,96,128]{2,1,3,0:T(1,128)S(1)}, f32[6,1,96,128]{2,1,3,0:T(1,128)S(1)}, u32[]{:S(2)}, u32[]{:S(2)}) %collective-permute-start.56) | collective-permute-done | bytes 294944 | tf_op jit(solution)/shard_map/ppermute | solution.py:25
  540.7 11.0 %collective-permute-done.90 = f32[1,128]{1,0:T(1,128)S(1)} collective-permute-done((f32[1,128]{1,0:T(1,128)S(1)}, f32[1,128]{1,0:T(1,128)S(1)}, u32[]{:S(2)}, u32[]{:S(2)}) %collective-permute-start.90) | collective-permute-done | bytes 544 | tf_op jit(solution)/shard_map/ppermute | solution.py:34
  557.3 3.9 collective-permute-start.91
  562.9 8.2 %collective-permute-done.91 = f32[3,1,1024]{2,1,0:T(1,128)S(1)} collective-permute-done((f32[3,1,1024]{2,1,0:T(1,128)S(1)}, f32[3,1,1024]{2,1,0:T(1,128)S(1)}, u32[]{:S(2)}, u32[]{:S(2)}) %collective-permute-start.91) | collective-permute-done | bytes 12320 | tf_op jit(solution)/shard_map/ppermute | solution.py:25
  582.2 3.9 collective-permute-start.95
  586.1 10.0 %collective-permute-start.81 = (f32[1,128]{1,0:T(1,128)S(1)}, f32[1,128]{1,0:T(1,128)S(1)}, u32[]{:S(2)}, u32[]{:S(2)}) collective-permute-start(f32[1,128]{1,0:T(1,128)S(1)} %get-tuple-element.358), channel_id=1, source_target_pairs={{8,0},{16,8},{24,16},{32,24},{40,32},{48,40},{56,48},{64,56},{72,6... | collective-permute-start | bytes 1544 | tf_op jit(solution)/shard_map/ppermute | solution.py:34
  604.5 7.2 collective-permute-start.100
  614.0 11.4 %collective-permute-done.99 = f32[3,1,1024]{2,1,0:T(1,128)S(1)} collective-permute-done((f32[3,1,1024]{2,1,0:T(1,128)S(1)}, f32[3,1,1024]{2,1,0:T(1,128)S(1)}, u32[]{:S(2)}, u32[]{:S(2)}) %collective-permute-start.99) | collective-permute-done | bytes 12320 | tf_op jit(solution)/shard_map/ppermute | solution.py:25
  635.6 3.9 collective-permute-start.103
  640.6 8.8 %collective-permute-done.103 = f32[3,1,1024]{2,1,0:T(1,128)S(1)} collective-permute-done((f32[3,1,1024]{2,1,0:T(1,128)S(1)}, f32[3,1,1024]{2,1,0:T(1,128)S(1)}, u32[]{:S(2)}, u32[]{:S(2)}) %collective-permute-start.103) | collective-permute-done | bytes 12320 | tf_op jit(solution)/shard_map/ppermute | solution.py:25
  657.1 3.9 collective-permute-start.60
  664.5 12.5 %collective-permute-done.60 = f32[3,1,96,128]{2,1,3,0:T(1,128)} collective-permute-done((f32[3,1,96,128]{2,1,3,0:T(1,128)}, f32[3,1,96,128]{2,1,3,0:T(1,128)}, u32[]{:S(2)}, u32[]{:S(2)}) %collective-permute-start.60) | collective-permute-done | bytes 147488 | tf_op jit(solution)/shard_map/ppermute | solution.py:25
  695.8 3.9 collective-permute-start.82
  707.4 12.1 %collective-permute-done.82 = f32[6,1,96,128]{2,1,3,0:T(1,128)S(1)} collective-permute-done((f32[6,1,96,128]{2,1,3,0:T(1,128)}, f32[6,1,96,128]{2,1,3,0:T(1,128)S(1)}, u32[]{:S(2)}, u32[]{:S(2)}) %collective-permute-start.82) | collective-permute-done | bytes 294944 | tf_op jit(solution)/shard_map/ppermute | solution.py:25
  719.6 6.9 collective-permute-start.85
  736.7 3.9 collective-permute-start.86
  740.7 10.0 %collective-permute-start.107 = (f32[1,128]{1,0:T(1,128)S(1)}, f32[1,128]{1,0:T(1,128)S(1)}, u32[]{:S(2)}, u32[]{:S(2)}) collective-permute-start(f32[1,128]{1,0:T(1,128)S(1)} %get-tuple-element.356), channel_id=1, source_target_pairs={{8,0},{16,8},{24,16},{32,24},{40,32},{48,40},{56,48},{64,56},{72,6... | collective-permute-start | bytes 1544 | tf_op jit(solution)/shard_map/ppermute | solution.py:34
  (520 shorter events, 365.5 us)
Async XLA Ops:
  1.4 13.6 %collective-permute-start.8 = (f32[1,128]{1,0:T(1,128)S(1)}, f32[1,128]{1,0:T(1,128)S(1)}, u32[]{:S(2)}, u32[]{:S(2)}) collective-permute-start(f32[1,128]{1,0:T(1,128)S(1)} %get-tuple-element.280), channel_id=1, source_target_pairs={{0,8},{8,16},{16,24},{24,32},{32,40},{40,48},{48,56},{56,64},{64,7... | collective-permute-start | bytes 1544 | tf_op jit(solution)/shard_map/ppermute | solution.py:34
  15.8 18.1 %collective-permute-start.10 = (f32[3,1,1024]{2,1,0:T(1,128)S(1)}, f32[3,1,1024]{2,1,0:T(1,128)S(1)}, u32[]{:S(2)}, u32[]{:S(2)}) collective-permute-start(f32[3,1,1024]{2,1,0:T(1,128)S(1)} %get-tuple-element.318), channel_id=1, source_target_pairs={{8,0},{16,8},{24,16},{32,24},{40,32},{48,40},{56,48},{64,56},{72,6... | collective-permute-start | bytes 36872 | tf_op jit(solution)/shard_map/ppermute | solution.py:26
  17.9 16.0 %collective-permute-start.9 = (f32[3,1,1024]{2,1,0:T(1,128)S(1)}, f32[3,1,1024]{2,1,0:T(1,128)S(1)}, u32[]{:S(2)}, u32[]{:S(2)}) collective-permute-start(f32[3,1,1024]{2,1,0:T(1,128)S(1)} %get-tuple-element.317), channel_id=1, source_target_pairs={{0,8},{8,16},{16,24},{24,32},{32,40},{40,48},{48,56},{56,64},{64,7... | collective-permute-start | bytes 36872 | tf_op jit(solution)/shard_map/ppermute | solution.py:25
  21.7 19.8 %collective-permute-start.14 = (f32[2,2,1024]{2,1,0:T(2,128)S(1)}, f32[2,2,1024]{2,1,0:T(2,128)S(1)}, u32[]{:S(2)}, u32[]{:S(2)}) collective-permute-start(f32[2,2,1024]{2,1,0:T(2,128)S(1)} %get-tuple-element.320), channel_id=1, source_target_pairs={{8,0},{16,8},{24,16},{32,24},{40,32},{48,40},{56,48},{64,56},{72,6... | collective-permute-start | bytes 49160 | tf_op jit(solution)/shard_map/ppermute | solution.py:26
  32.0 13.8 %collective-permute-start.13 = (f32[2,2,1024]{2,1,0:T(2,128)S(1)}, f32[2,2,1024]{2,1,0:T(2,128)S(1)}, u32[]{:S(2)}, u32[]{:S(2)}) collective-permute-start(f32[2,2,1024]{2,1,0:T(2,128)S(1)} %get-tuple-element.319), channel_id=1, source_target_pairs={{0,8},{8,16},{16,24},{24,32},{32,40},{40,48},{48,56},{56,64},{64,7... | collective-permute-start | bytes 49160 | tf_op jit(solution)/shard_map/ppermute | solution.py:25
  61.9 13.8 %collective-permute-start.17 = (f32[3,1,1024]{2,1,0:T(1,128)S(1)}, f32[3,1,1024]{2,1,0:T(1,128)S(1)}, u32[]{:S(2)}, u32[]{:S(2)}) collective-permute-start(f32[3,1,1024]{2,1,0:T(1,128)S(1)} %get-tuple-element.313), channel_id=1, source_target_pairs={{0,8},{8,16},{16,24},{24,32},{32,40},{40,48},{48,56},{56,64},{64,7... | collective-permute-start | bytes 36872 | tf_op jit(solution)/shard_map/ppermute | solution.py:25
  84.0 17.0 %collective-permute-start.22 = (f32[3,1,1024]{2,1,0:T(1,128)S(1)}, f32[3,1,1024]{2,1,0:T(1,128)S(1)}, u32[]{:S(2)}, u32[]{:S(2)}) collective-permute-start(f32[3,1,1024]{2,1,0:T(1,128)S(1)} %get-tuple-element.312), channel_id=1, source_target_pairs={{8,0},{16,8},{24,16},{32,24},{40,32},{48,40},{56,48},{64,56},{72,6... | collective-permute-start | bytes 36872 | tf_op jit(solution)/shard_map/ppermute | solution.py:26
  85.9 15.0 %collective-permute-start.21 = (f32[3,1,1024]{2,1,0:T(1,128)S(1)}, f32[3,1,1024]{2,1,0:T(1,128)S(1)}, u32[]{:S(2)}, u32[]{:S(2)}) collective-permute-start(f32[3,1,1024]{2,1,0:T(1,128)S(1)} %get-tuple-element.311), channel_id=1, source_target_pairs={{0,8},{8,16},{16,24},{24,32},{32,40},{40,48},{48,56},{56,64},{64,7... | collective-permute-start | bytes 36872 | tf_op jit(solution)/shard_map/ppermute | solution.py:25
  90.9 54.8 %collective-permute-start.1 = (f32[6,1,96,128]{2,1,3,0:T(1,128)}, f32[6,1,96,128]{2,1,3,0:T(1,128)S(1)}, u32[]{:S(2)}, u32[]{:S(2)}) collective-permute-start(f32[6,1,96,128]{2,1,3,0:T(1,128)} %copy.84), channel_id=1, source_target_pairs={{8,0},{16,8},{24,16},{32,24},{40,32},{48,40},{56,48},{64,56},{72,6... | collective-permute-start | bytes 884744 | tf_op jit(solution)/shard_map/ppermute | solution.py:26
  107.7 38.1 %collective-permute-start = (f32[6,1,96,128]{2,1,3,0:T(1,128)}, f32[6,1,96,128]{2,1,3,0:T(1,128)S(1)}, u32[]{:S(2)}, u32[]{:S(2)}) collective-permute-start(f32[6,1,96,128]{2,1,3,0:T(1,128)} %copy.83), channel_id=1, source_target_pairs={{0,8},{8,16},{16,24},{24,32},{32,40},{40,48},{48,56},{56,64},{64,7... | collective-permute-start | bytes 884744 | tf_op jit(solution)/shard_map/ppermute | solution.py:25
  112.3 13.6 %collective-permute-start.26 = (f32[3,1,1024]{2,1,0:T(1,128)S(1)}, f32[3,1,1024]{2,1,0:T(1,128)S(1)}, u32[]{:S(2)}, u32[]{:S(2)}) collective-permute-start(f32[3,1,1024]{2,1,0:T(1,128)S(1)} %get-tuple-element.310), channel_id=1, source_target_pairs={{8,0},{16,8},{24,16},{32,24},{40,32},{48,40},{56,48},{64,56},{72,6... | collective-permute-start | bytes 36872 | tf_op jit(solution)/shard_map/ppermute | solution.py:26
  122.7 14.5 %collective-permute-start.25 = (f32[3,1,1024]{2,1,0:T(1,128)S(1)}, f32[3,1,1024]{2,1,0:T(1,128)S(1)}, u32[]{:S(2)}, u32[]{:S(2)}) collective-permute-start(f32[3,1,1024]{2,1,0:T(1,128)S(1)} %get-tuple-element.309), channel_id=1, source_target_pairs={{0,8},{8,16},{16,24},{24,32},{32,40},{40,48},{48,56},{56,64},{64,7... | collective-permute-start | bytes 36872 | tf_op jit(solution)/shard_map/ppermute | solution.py:25
  158.5 13.6 %collective-permute-start.38 = (f32[1,128]{1,0:T(1,128)S(1)}, f32[1,128]{1,0:T(1,128)S(1)}, u32[]{:S(2)}, u32[]{:S(2)}) collective-permute-start(f32[1,128]{1,0:T(1,128)S(1)} %bitcast.623), channel_id=1, source_target_pairs={{0,8},{8,16},{16,24},{24,32},{32,40},{40,48},{48,56},{56,64},{64,7... | collective-permute-start | bytes 1544 | tf_op jit(solution)/shard_map/ppermute | solution.py:34
  177.0 13.7 %collective-permute-start.39 = (f32[3,1,1024]{2,1,0:T(1,128)S(1)}, f32[3,1,1024]{2,1,0:T(1,128)S(1)}, u32[]{:S(2)}, u32[]{:S(2)}) collective-permute-start(f32[3,1,1024]{2,1,0:T(1,128)S(1)} %get-tuple-element.307), channel_id=1, source_target_pairs={{0,8},{8,16},{16,24},{24,32},{32,40},{40,48},{48,56},{56,64},{64,7... | collective-permute-start | bytes 36872 | tf_op jit(solution)/shard_map/ppermute | solution.py:25
  204.3 13.7 %collective-permute-start.43 = (f32[3,1,1024]{2,1,0:T(1,128)S(1)}, f32[3,1,1024]{2,1,0:T(1,128)S(1)}, u32[]{:S(2)}, u32[]{:S(2)}) collective-permute-start(f32[3,1,1024]{2,1,0:T(1,128)S(1)} %get-tuple-element.305), channel_id=1, source_target_pairs={{0,8},{8,16},{16,24},{24,32},{32,40},{40,48},{48,56},{56,64},{64,7... | collective-permute-start | bytes 36872 | tf_op jit(solution)/shard_map/ppermute | solution.py:25
  223.7 53.9 %collective-permute-start.29 = (f32[1,128]{1,0:T(1,128)S(1)}, f32[1,128]{1,0:T(1,128)S(1)}, u32[]{:S(2)}, u32[]{:S(2)}) collective-permute-start(f32[1,128]{1,0:T(1,128)S(1)} %get-tuple-element.362), channel_id=1, source_target_pairs={{8,0},{16,8},{24,16},{32,24},{40,32},{48,40},{56,48},{64,56},{72,6... | collective-permute-start | bytes 1544 | tf_op jit(solution)/shard_map/ppermute | solution.py:34
  231.0 13.7 %collective-permute-start.47 = (f32[3,1,1024]{2,1,0:T(1,128)S(1)}, f32[3,1,1024]{2,1,0:T(1,128)S(1)}, u32[]{:S(2)}, u32[]{:S(2)}) collective-permute-start(f32[3,1,1024]{2,1,0:T(1,128)S(1)} %get-tuple-element.303), channel_id=1, source_target_pairs={{0,8},{8,16},{16,24},{24,32},{32,40},{40,48},{48,56},{56,64},{64,7... | collective-permute-start | bytes 36872 | tf_op jit(solution)/shard_map/ppermute | solution.py:25
  253.0 18.9 %collective-permute-start.52 = (f32[3,1,1024]{2,1,0:T(1,128)S(1)}, f32[3,1,1024]{2,1,0:T(1,128)S(1)}, u32[]{:S(2)}, u32[]{:S(2)}) collective-permute-start(f32[3,1,1024]{2,1,0:T(1,128)S(1)} %get-tuple-element.302), channel_id=1, source_target_pairs={{8,0},{16,8},{24,16},{32,24},{40,32},{48,40},{56,48},{64,56},{72,6... | collective-permute-start | bytes 36872 | tf_op jit(solution)/shard_map/ppermute | solution.py:26
  254.9 17.0 %collective-permute-start.51 = (f32[3,1,1024]{2,1,0:T(1,128)S(1)}, f32[3,1,1024]{2,1,0:T(1,128)S(1)}, u32[]{:S(2)}, u32[]{:S(2)}) collective-permute-start(f32[3,1,1024]{2,1,0:T(1,128)S(1)} %get-tuple-element.301), channel_id=1, source_target_pairs={{0,8},{8,16},{16,24},{24,32},{32,40},{40,48},{48,56},{56,64},{64,7... | collective-permute-start | bytes 36872 | tf_op jit(solution)/shard_map/ppermute | solution.py:25
  259.9 19.5 %collective-permute-start.5 = (f32[3,1,96,128]{2,1,3,0:T(1,128)}, f32[3,1,96,128]{2,1,3,0:T(1,128)S(1)}, u32[]{:S(2)}, u32[]{:S(2)}) collective-permute-start(f32[3,1,96,128]{2,1,3,0:T(1,128)} %get-tuple-element.199), channel_id=1, source_target_pairs={{8,0},{16,8},{24,16},{32,24},{40,32},{48,40},{56,48},{64,56},{72,6... | collective-permute-start | bytes 442376 | tf_op jit(solution)/shard_map/ppermute | solution.py:26
  269.9 21.7 %collective-permute-start.4 = (f32[3,1,96,128]{2,1,3,0:T(1,128)}, f32[3,1,96,128]{2,1,3,0:T(1,128)S(1)}, u32[]{:S(2)}, u32[]{:S(2)}) collective-permute-start(f32[3,1,96,128]{2,1,3,0:T(1,128)} %get-tuple-element.198), channel_id=1, source_target_pairs={{0,8},{8,16},{16,24},{24,32},{32,40},{40,48},{48,56},{56,64},{64,7... | collective-permute-start | bytes 442376 | tf_op jit(solution)/shard_map/ppermute | solution.py:25
  304.7 18.0 %collective-permute-start.31 = (f32[6,1,96,128]{2,1,3,0:T(1,128)S(1)}, f32[6,1,96,128]{2,1,3,0:T(1,128)S(1)}, u32[]{:S(2)}, u32[]{:S(2)}) collective-permute-start(f32[6,1,96,128]{2,1,3,0:T(1,128)S(1)} %get-tuple-element.179), channel_id=1, source_target_pairs={{8,0},{16,8},{24,16},{32,24},{40,32},{48,40},{56,48},{64,56},{72,6... | collective-permute-start | bytes 884744 | tf_op jit(solution)/shard_map/ppermute | solution.py:26
  306.6 28.6 %collective-permute-start.30 = (f32[6,1,96,128]{2,1,3,0:T(1,128)S(1)}, f32[6,1,96,128]{2,1,3,0:T(1,128)S(1)}, u32[]{:S(2)}, u32[]{:S(2)}) collective-permute-start(f32[6,1,96,128]{2,1,3,0:T(1,128)S(1)} %get-tuple-element.178), channel_id=1, source_target_pairs={{0,8},{8,16},{16,24},{24,32},{32,40},{40,48},{48,56},{56,64},{64,7... | collective-permute-start | bytes 884744 | tf_op jit(solution)/shard_map/ppermute | solution.py:25
  346.2 13.6 %collective-permute-start.64 = (f32[1,128]{1,0:T(1,128)S(1)}, f32[1,128]{1,0:T(1,128)S(1)}, u32[]{:S(2)}, u32[]{:S(2)}) collective-permute-start(f32[1,128]{1,0:T(1,128)S(1)} %bitcast.624), channel_id=1, source_target_pairs={{0,8},{8,16},{16,24},{24,32},{32,40},{40,48},{48,56},{56,64},{64,7... | collective-permute-start | bytes 1544 | tf_op jit(solution)/shard_map/ppermute | solution.py:34
  364.7 13.7 %collective-permute-start.65 = (f32[3,1,1024]{2,1,0:T(1,128)S(1)}, f32[3,1,1024]{2,1,0:T(1,128)S(1)}, u32[]{:S(2)}, u32[]{:S(2)}) collective-permute-start(f32[3,1,1024]{2,1,0:T(1,128)S(1)} %get-tuple-element.299), channel_id=1, source_target_pairs={{0,8},{8,16},{16,24},{24,32},{32,40},{40,48},{48,56},{56,64},{64,7... | collective-permute-start | bytes 36872 | tf_op jit(solution)/shard_map/ppermute | solution.py:25
  392.6 13.7 %collective-permute-start.69 = (f32[3,1,1024]{2,1,0:T(1,128)S(1)}, f32[3,1,1024]{2,1,0:T(1,128)S(1)}, u32[]{:S(2)}, u32[]{:S(2)}) collective-permute-start(f32[3,1,1024]{2,1,0:T(1,128)S(1)} %get-tuple-element.297), channel_id=1, source_target_pairs={{0,8},{8,16},{16,24},{24,32},{32,40},{40,48},{48,56},{56,64},{64,7... | collective-permute-start | bytes 36872 | tf_op jit(solution)/shard_map/ppermute | solution.py:25
  412.0 55.9 %collective-permute-start.55 = (f32[1,128]{1,0:T(1,128)S(1)}, f32[1,128]{1,0:T(1,128)S(1)}, u32[]{:S(2)}, u32[]{:S(2)}) collective-permute-start(f32[1,128]{1,0:T(1,128)S(1)} %get-tuple-element.360), channel_id=1, source_target_pairs={{8,0},{16,8},{24,16},{32,24},{40,32},{48,40},{56,48},{64,56},{72,6... | collective-permute-start | bytes 1544 | tf_op jit(solution)/shard_map/ppermute | solution.py:34
  418.6 13.7 %collective-permute-start.73 = (f32[3,1,1024]{2,1,0:T(1,128)S(1)}, f32[3,1,1024]{2,1,0:T(1,128)S(1)}, u32[]{:S(2)}, u32[]{:S(2)}) collective-permute-start(f32[3,1,1024]{2,1,0:T(1,128)S(1)} %get-tuple-element.295), channel_id=1, source_target_pairs={{0,8},{8,16},{16,24},{24,32},{32,40},{40,48},{48,56},{56,64},{64,7... | collective-permute-start | bytes 36872 | tf_op jit(solution)/shard_map/ppermute | solution.py:25
  443.2 18.9 %collective-permute-start.78 = (f32[3,1,1024]{2,1,0:T(1,128)S(1)}, f32[3,1,1024]{2,1,0:T(1,128)S(1)}, u32[]{:S(2)}, u32[]{:S(2)}) collective-permute-start(f32[3,1,1024]{2,1,0:T(1,128)S(1)} %get-tuple-element.294), channel_id=1, source_target_pairs={{8,0},{16,8},{24,16},{32,24},{40,32},{48,40},{56,48},{64,56},{72,6... | collective-permute-start | bytes 36872 | tf_op jit(solution)/shard_map/ppermute | solution.py:26
  445.2 17.0 %collective-permute-start.77 = (f32[3,1,1024]{2,1,0:T(1,128)S(1)}, f32[3,1,1024]{2,1,0:T(1,128)S(1)}, u32[]{:S(2)}, u32[]{:S(2)}) collective-permute-start(f32[3,1,1024]{2,1,0:T(1,128)S(1)} %get-tuple-element.293), channel_id=1, source_target_pairs={{0,8},{8,16},{16,24},{24,32},{32,40},{40,48},{48,56},{56,64},{64,7... | collective-permute-start | bytes 36872 | tf_op jit(solution)/shard_map/ppermute | solution.py:25
  450.1 19.5 %collective-permute-start.35 = (f32[3,1,96,128]{2,1,3,0:T(1,128)}, f32[3,1,96,128]{2,1,3,0:T(1,128)S(1)}, u32[]{:S(2)}, u32[]{:S(2)}) collective-permute-start(f32[3,1,96,128]{2,1,3,0:T(1,128)} %get-tuple-element.197), channel_id=1, source_target_pairs={{8,0},{16,8},{24,16},{32,24},{40,32},{48,40},{56,48},{64,56},{72,6... | collective-permute-start | bytes 442376 | tf_op jit(solution)/shard_map/ppermute | solution.py:26
  460.2 21.3 %collective-permute-start.34 = (f32[3,1,96,128]{2,1,3,0:T(1,128)}, f32[3,1,96,128]{2,1,3,0:T(1,128)S(1)}, u32[]{:S(2)}, u32[]{:S(2)}) collective-permute-start(f32[3,1,96,128]{2,1,3,0:T(1,128)} %get-tuple-element.196), channel_id=1, source_target_pairs={{0,8},{8,16},{16,24},{24,32},{32,40},{40,48},{48,56},{56,64},{64,7... | collective-permute-start | bytes 442376 | tf_op jit(solution)/shard_map/ppermute | solution.py:25
  495.6 18.9 %collective-permute-start.57 = (f32[6,1,96,128]{2,1,3,0:T(1,128)S(1)}, f32[6,1,96,128]{2,1,3,0:T(1,128)S(1)}, u32[]{:S(2)}, u32[]{:S(2)}) collective-permute-start(f32[6,1,96,128]{2,1,3,0:T(1,128)S(1)} %get-tuple-element.175), channel_id=1, source_target_pairs={{8,0},{16,8},{24,16},{32,24},{40,32},{48,40},{56,48},{64,56},{72,6... | collective-permute-start | bytes 884744 | tf_op jit(solution)/shard_map/ppermute | solution.py:26
  497.6 29.5 %collective-permute-start.56 = (f32[6,1,96,128]{2,1,3,0:T(1,128)S(1)}, f32[6,1,96,128]{2,1,3,0:T(1,128)S(1)}, u32[]{:S(2)}, u32[]{:S(2)}) collective-permute-start(f32[6,1,96,128]{2,1,3,0:T(1,128)S(1)} %get-tuple-element.174), channel_id=1, source_target_pairs={{0,8},{8,16},{16,24},{24,32},{32,40},{40,48},{48,56},{56,64},{64,7... | collective-permute-start | bytes 884744 | tf_op jit(solution)/shard_map/ppermute | solution.py:25
  538.0 13.6 %collective-permute-start.90 = (f32[1,128]{1,0:T(1,128)S(1)}, f32[1,128]{1,0:T(1,128)S(1)}, u32[]{:S(2)}, u32[]{:S(2)}) collective-permute-start(f32[1,128]{1,0:T(1,128)S(1)} %bitcast.625), channel_id=1, source_target_pairs={{0,8},{8,16},{16,24},{24,32},{32,40},{40,48},{48,56},{56,64},{64,7... | collective-permute-start | bytes 1544 | tf_op jit(solution)/shard_map/ppermute | solution.py:34
  557.3 13.7 %collective-permute-start.91 = (f32[3,1,1024]{2,1,0:T(1,128)S(1)}, f32[3,1,1024]{2,1,0:T(1,128)S(1)}, u32[]{:S(2)}, u32[]{:S(2)}) collective-permute-start(f32[3,1,1024]{2,1,0:T(1,128)S(1)} %get-tuple-element.291), channel_id=1, source_target_pairs={{0,8},{8,16},{16,24},{24,32},{32,40},{40,48},{48,56},{56,64},{64,7... | collective-permute-start | bytes 36872 | tf_op jit(solution)/shard_map/ppermute | solution.py:25
  580.3 15.9 %collective-permute-start.96 = (f32[3,1,1024]{2,1,0:T(1,128)S(1)}, f32[3,1,1024]{2,1,0:T(1,128)S(1)}, u32[]{:S(2)}, u32[]{:S(2)}) collective-permute-start(f32[3,1,1024]{2,1,0:T(1,128)S(1)} %get-tuple-element.290), channel_id=1, source_target_pairs={{8,0},{16,8},{24,16},{32,24},{40,32},{48,40},{56,48},{64,56},{72,6... | collective-permute-start | bytes 36872 | tf_op jit(solution)/shard_map/ppermute | solution.py:26
  582.2 14.0 %collective-permute-start.95 = (f32[3,1,1024]{2,1,0:T(1,128)S(1)}, f32[3,1,1024]{2,1,0:T(1,128)S(1)}, u32[]{:S(2)}, u32[]{:S(2)}) collective-permute-start(f32[3,1,1024]{2,1,0:T(1,128)S(1)} %get-tuple-element.289), channel_id=1, source_target_pairs={{0,8},{8,16},{16,24},{24,32},{32,40},{40,48},{48,56},{56,64},{64,7... | collective-permute-start | bytes 36872 | tf_op jit(solution)/shard_map/ppermute | solution.py:25
  586.1 16.0 %collective-permute-start.81 = (f32[1,128]{1,0:T(1,128)S(1)}, f32[1,128]{1,0:T(1,128)S(1)}, u32[]{:S(2)}, u32[]{:S(2)}) collective-permute-start(f32[1,128]{1,0:T(1,128)S(1)} %get-tuple-element.358), channel_id=1, source_target_pairs={{8,0},{16,8},{24,16},{32,24},{40,32},{48,40},{56,48},{64,56},{72,6... | collective-permute-start | bytes 1544 | tf_op jit(solution)/shard_map/ppermute | solution.py:34
  611.7 13.7 %collective-permute-start.99 = (f32[3,1,1024]{2,1,0:T(1,128)S(1)}, f32[3,1,1024]{2,1,0:T(1,128)S(1)}, u32[]{:S(2)}, u32[]{:S(2)}) collective-permute-start(f32[3,1,1024]{2,1,0:T(1,128)S(1)} %get-tuple-element.287), channel_id=1, source_target_pairs={{0,8},{8,16},{16,24},{24,32},{32,40},{40,48},{48,56},{56,64},{64,7... | collective-permute-start | bytes 36872 | tf_op jit(solution)/shard_map/ppermute | solution.py:25
  635.6 13.8 %collective-permute-start.103 = (f32[3,1,1024]{2,1,0:T(1,128)S(1)}, f32[3,1,1024]{2,1,0:T(1,128)S(1)}, u32[]{:S(2)}, u32[]{:S(2)}) collective-permute-start(f32[3,1,1024]{2,1,0:T(1,128)S(1)} %get-tuple-element.285), channel_id=1, source_target_pairs={{0,8},{8,16},{16,24},{24,32},{32,40},{40,48},{48,56},{56,64},{64,7... | collective-permute-start | bytes 36872 | tf_op jit(solution)/shard_map/ppermute | solution.py:25
  649.6 11.4 %collective-permute-start.105 = (f32[3,18,1]{2,1,0:T(8,128)S(1)}, f32[3,18,1]{2,1,0:T(8,128)S(1)}, u32[]{:S(2)}, u32[]{:S(2)}) collective-permute-start(f32[3,18,1]{2,1,0:T(8,128)S(1)} %get-tuple-element.249), channel_id=1, source_target_pairs={{0,1},{1,2},{2,3},{3,4},{4,5},{5,6},{6,7},{8,9},{9,10},{10,11},{11... | collective-permute-start | bytes 656 | tf_op jit(solution)/shard_map/ppermute | solution.py:25
  657.1 19.9 %collective-permute-start.60 = (f32[3,1,96,128]{2,1,3,0:T(1,128)}, f32[3,1,96,128]{2,1,3,0:T(1,128)}, u32[]{:S(2)}, u32[]{:S(2)}) collective-permute-start(f32[3,1,96,128]{2,1,3,0:T(1,128)} %get-tuple-element.194), channel_id=1, source_target_pairs={{0,8},{8,16},{16,24},{24,32},{32,40},{40,48},{48,56},{56,64},{64,7... | collective-permute-start | bytes 442376 | tf_op jit(solution)/shard_map/ppermute | solution.py:25
  693.9 13.5 %collective-permute-start.83 = (f32[6,1,96,128]{2,1,3,0:T(1,128)}, f32[6,1,96,128]{2,1,3,0:T(1,128)S(1)}, u32[]{:S(2)}, u32[]{:S(2)}) collective-permute-start(f32[6,1,96,128]{2,1,3,0:T(1,128)} %get-tuple-element.171), channel_id=1, source_target_pairs={{8,0},{16,8},{24,16},{32,24},{40,32},{48,40},{56,48},{64,56},{72,6... | collective-permute-start | bytes 884744 | tf_op jit(solution)/shard_map/ppermute | solution.py:26
  695.8 23.8 %collective-permute-start.82 = (f32[6,1,96,128]{2,1,3,0:T(1,128)}, f32[6,1,96,128]{2,1,3,0:T(1,128)S(1)}, u32[]{:S(2)}, u32[]{:S(2)}) collective-permute-start(f32[6,1,96,128]{2,1,3,0:T(1,128)} %get-tuple-element.170), channel_id=1, source_target_pairs={{0,8},{8,16},{16,24},{24,32},{32,40},{40,48},{48,56},{56,64},{64,7... | collective-permute-start | bytes 884744 | tf_op jit(solution)/shard_map/ppermute | solution.py:25
  734.8 16.6 %collective-permute-start.87 = (f32[3,1,96,128]{2,1,3,0:T(1,128)S(1)}, f32[3,1,96,128]{2,1,3,0:T(1,128)S(1)}, u32[]{:S(2)}, u32[]{:S(2)}) collective-permute-start(f32[3,1,96,128]{2,1,3,0:T(1,128)S(1)} %get-tuple-element.193), channel_id=1, source_target_pairs={{8,0},{16,8},{24,16},{32,24},{40,32},{48,40},{56,48},{64,56},{72,6... | collective-permute-start | bytes 442376 | tf_op jit(solution)/shard_map/ppermute | solution.py:26
  736.7 17.0 %collective-permute-start.86 = (f32[3,1,96,128]{2,1,3,0:T(1,128)S(1)}, f32[3,1,96,128]{2,1,3,0:T(1,128)S(1)}, u32[]{:S(2)}, u32[]{:S(2)}) collective-permute-start(f32[3,1,96,128]{2,1,3,0:T(1,128)S(1)} %get-tuple-element.192), channel_id=1, source_target_pairs={{0,8},{8,16},{16,24},{24,32},{32,40},{40,48},{48,56},{56,64},{64,7... | collective-permute-start | bytes 442376 | tf_op jit(solution)/shard_map/ppermute | solution.py:25
  740.7 17.4 %collective-permute-start.107 = (f32[1,128]{1,0:T(1,128)S(1)}, f32[1,128]{1,0:T(1,128)S(1)}, u32[]{:S(2)}, u32[]{:S(2)}) collective-permute-start(f32[1,128]{1,0:T(1,128)S(1)} %get-tuple-element.356), channel_id=1, source_target_pairs={{8,0},{16,8},{24,16},{32,24},{40,32},{48,40},{56,48},{64,56},{72,6... | collective-permute-start | bytes 1544 | tf_op jit(solution)/shard_map/ppermute | solution.py:34
  (89 other events, 733.4 us)
where the time goes:
time: 780 us; the launch traced here: 768 us
  starting transfers between devices  354 us (45%)
  waiting for transfers between devices  296 us (38%)
  local copies, waits for them, and re-layouts  65.1 us (8%)
  other arithmetic  48.3 us (6%)
    ppermute x50, waiting for transfers between devices, padded(): before = lax.ppermute(last, axis, up)  206 us
    ppermute x50, starting transfers between devices, padded(): after = lax.ppermute(first, axis, down)  185 us
    ppermute x50, starting transfers between devices, padded(): before = lax.ppermute(last, axis, up)  136 us
    ppermute x50, waiting for transfers between devices, padded(): after = lax.ppermute(first, axis, down)  47.4 us
    ppermute x8, waiting for transfers between devices, from_behind(): return lax.ppermute(shard, axis, pairs)  42.5 us
    ppermute x8, starting transfers between devices, from_behind(): return lax.ppermute(shard, axis, pairs)  33.1 us
  transfers between devices with their start and end apart: 108, of which 49 were waited for; matrix products, arithmetic and copies ran while one was open for 6% of the time, Pallas kernels for 0%

commit v1 on v0

v1 whole, which is shorter than its diff:
```python
import functools

import jax
import jax.numpy as jnp
from jax import lax
from jax.experimental import pallas as pl
from jax.experimental.pallas import tpu as pltpu
from jax.sharding import PartitionSpec as P

STEPS = 4
NSUB = 4
SOLID_STEP = 0.2
WAVE_STEP = 0.1
VISCOSITY = 0.05
UPLIFT_GAIN = 0.25
LOAD_GAIN = 8.0

INTERPRET = False
LANES = 128
TILES = 9
OCEAN = 3 * TILES * 8


def iota(shape, dim):
    return lax.broadcasted_iota(jnp.int32, shape, dim)


def roll(value, shift, axis):
    shift = shift % value.shape[axis]
    return value if shift == 0 else pltpu.roll(value, shift, axis)


def prev_lane(value):
    return roll(value, 1, 1)


def next_lane(value):
    return roll(value, -1, 1)


def below(get, k):
    current = roll(get(k), 1, 0)
    other = roll(get(k - 1), 1, 0) if k > 0 else jnp.zeros_like(current)
    return jnp.where(iota(current.shape, 0) == 0, other, current)


def above(get, k, slabs):
    current = roll(get(k), -1, 0)
    other = roll(get(k + 1), -1, 0) if k < slabs - 1 else jnp.zeros_like(current)
    return jnp.where(iota(current.shape, 0) == 7, other, current)


def expander():
    shape = (LANES, LANES)
    return jnp.where(iota(shape, 0) == iota(shape, 1) >> 3, 1.0, 0.0)


def reducer():
    shape = (LANES, LANES)
    return jnp.where(iota(shape, 0) >> 3 == iota(shape, 1), 1.0 / 64.0, 0.0)


def exact_dot(left, right):
    return jnp.dot(
        left, right, precision=lax.Precision.HIGHEST, preferred_element_type=jnp.float32
    )


def upsampled(rows):
    lane, line = iota((8, LANES), 1), iota((8, LANES), 0)
    stack = []
    for row in rows:
        own = jnp.broadcast_to(row[:, :LANES], (8, LANES))
        halo = jnp.broadcast_to(row[:, LANES:], (8, LANES))
        tiles = own
        for t in range(1, 8):
            tiles = jnp.where(line == t, roll(own, -16 * t, 1), tiles)
        stack += [tiles, jnp.where(lane < 4, halo, roll(halo, 16, 1))]
    spread = exact_dot(jnp.concatenate(stack, axis=0), expander())
    return [spread[16 * i : 16 * i + 16] for i in range(len(rows))]


def block_means(sums):
    lane, line = iota((8, LANES), 1), iota((8, LANES), 0)
    stack = []
    for tiles in sums:
        wide = [jnp.broadcast_to(tile, (8, LANES)) for tile in tiles]
        own = wide[0]
        for t in range(1, 8):
            own = jnp.where(line == t, wide[t], own)
        stack += [own, wide[8]]
    mean = exact_dot(jnp.concatenate(stack, axis=0), reducer())
    rows = []
    for i in range(len(sums)):
        tiles, last = mean[16 * i : 16 * i + 8], mean[16 * i + 8 : 16 * i + 16]
        own = jnp.zeros((8, LANES), jnp.float32)
        for t in range(8):
            own = jnp.where((line == t) & (lane >> 4 == t), roll(tiles, 16 * t, 1), own)
        own = jnp.sum(own, axis=0, keepdims=True)
        halo = jnp.where(lane < 4, last, jnp.where(lane >= 124, roll(last, 112, 1), 0.0))
        rows.append(jnp.concatenate([own, halo[0:1]], axis=1))
    return rows


class Sender:
    def __init__(self, even, first_ref, second_ref):
        self.even, self.first, self.second = even, first_ref, second_ref

    def put(self, at, right, left):
        end = at + right.shape[0]
        self.first[at:end, :] = jnp.where(self.even, right, left)
        self.second[at:end, :] = jnp.where(self.even, left, right)

    def put_solid(self, at, slabs, right, left):
        lane = iota((8, LANES), 1)
        tails = [jnp.zeros((8, LANES), jnp.float32) for _ in range(2)]
        for k in range(slabs):
            here = (lane >= 8 * k) & (lane < 8 * k + 8)
            values = (right(k), left(k))
            for i, value in enumerate(values):
                tails[i] = jnp.where(here, roll(value[:, LANES:], 4 + 8 * k, 1), tails[i])
            self.put(at + 8 * k, values[0][:, :LANES], values[1][:, :LANES])
        self.put(at + 8 * slabs, *tails)


class Receiver:
    def __init__(self, even, first_ref, second_ref):
        self.even, self.first, self.second = even, first_ref, second_ref

    def right(self, at):
        return jnp.where(self.even, self.first[at : at + 8, :], self.second[at : at + 8, :])

    def left(self, at):
        return jnp.where(self.even, self.second[at : at + 8, :], self.first[at : at + 8, :])

    def solid(self, side, at, k, slabs):
        take = self.right if side > 0 else self.left
        tail = roll(take(at + 8 * slabs), -(4 + 8 * k), 1)
        return jnp.concatenate([take(at + 8 * k), tail], axis=1)


def offsets(slabs):
    part = 8 * slabs + 8
    ocean = 3 * part
    extra = ocean + OCEAN
    more = extra + 16
    return part, ocean, extra, more, more + part


def payload_rows(slabs, kind):
    part, _, _, more, static = offsets(slabs)
    return {"first": static + 4 * TILES * 8, "usual": more, "last": more + OCEAN}[kind]


def finish(out, slabs, motion, stress, buoyancy, ocean, wet, mean_row, kind, static=None):
    part, ocean_at, extra_at, more_at, static_at = offsets(slabs)

    def get(ref, field, row):
        return lambda k: ref[field, row, 8 * k : 8 * k + 8, :]

    def rate(row, k):
        return SOLID_STEP * buoyancy[0, row, 8 * k : 8 * k + 8, :]

    def sum_x(k):
        xx, xy, xz = (get(stress, f, 1) for f in (0, 3, 4))
        mid = xy(k)
        force = (mid - prev_lane(mid)) + (xz(k) - below(xz, k)) - xx(k)
        return get(motion, 0, 1)(k) + rate(1, k) * force

    def sum_y(k):
        xy, yy, yz = (get(stress, f, 0) for f in (3, 1, 5))
        mid = yy(k)
        force = xy(k) + (next_lane(mid) - mid) + (yz(k) - below(yz, k))
        return get(motion, 1, 0)(k) + rate(0, k) * force

    def sum_z(k):
        xz, yz, zz = (get(stress, f, 0) for f in (4, 5, 2))
        mid = yz(k)
        force = xz(k) + (mid - prev_lane(mid)) + (above(zz, k, slabs) - zz(k))
        return get(motion, 2, 0)(k) + rate(0, k) * force

    out.put_solid(0, slabs, sum_x, sum_y)
    out.put_solid(part, slabs, get(stress, 3, 1), sum_z)
    out.put_solid(2 * part, slabs, get(stress, 4, 1), get(stress, 0, 0))
    (spread,) = upsampled([motion[2, 0, 0:1, :]])
    for t in range(TILES):
        ocean[0, t, 8:16, :] = (
            ocean[0, t, 8:16, :] + UPLIFT_GAIN * wet[t, 8:16, :] * spread[t : t + 1]
        )
        for f in range(3):
            at = (f * TILES + t) * 8
            lower, upper = ocean[f, t, 0:8, :], ocean[f, t, 8:16, :]
            out.put(ocean_at + at, upper, lower)
            if kind == "last":
                out.put(more_at + at, upper, upper)
    top = motion[2, 1, 0:8, :]
    mean_row = jnp.zeros((8, 256), jnp.float32) if mean_row is None else mean_row
    mean_row = jnp.broadcast_to(mean_row, (8, 256))
    for i in range(2):
        lanes = slice(LANES * i, LANES * i + LANES)
        out.put(extra_at + 8 * i, top[:, lanes], mean_row[:, lanes])
    if kind == "first":
        out.put_solid(more_at, slabs, get(buoyancy, 0, 1), get(buoyancy, 0, 0))
        for f, array in enumerate(static):
            for t in range(TILES):
                at = static_at + (f * 2 * TILES + t) * 8
                lower, upper = array[t, 0:8, :], array[t, 8:16, :]
                out.put(at, upper, lower)
                out.put(at + TILES * 8, upper, upper)


def pack_y_kernel(
    parity, motion, stress, buoyancy, first, shear, surface, momentum, depth, wet, one, two
):
    even = parity[1] == 0
    out = Sender(even, one, two)
    slabs = motion.shape[2] // 8
    lane = iota((8, LANES), 1)
    fields = [(motion, f) for f in range(3)] + [(stress, f) for f in range(6)]
    fields += [(buoyancy, None), (first, None), (shear, None)]
    count, at = 0, 0
    right = left = jnp.zeros((8, LANES), jnp.float32)
    for ref, f in fields:
        for row in range(2):
            for k in range(slabs):
                z = slice(8 * k, 8 * k + 8)
                value = ref[row, z, :] if f is None else ref[f, row, z, :]
                here = lane >> 2 == count
                right = jnp.where(here, roll(value, 4 * count + 4, 1), right)
                left = jnp.where(here, roll(value, 4 * count, 1), left)
                count += 1
                if count == 32:
                    out.put(at, right, left)
                    count, at = 0, at + 8
    if count:
        out.put(at, right, left)
        count, at = 0, at + 8
    width = surface.shape[1]
    for ref, f in ((surface, None), (momentum, 0), (momentum, 1), (depth, None), (wet, None)):
        for group in range(2):
            rows = slice(8 * group, 8 * group + 8)
            ends = []
            for lanes in (slice(0, LANES), slice(width - LANES, width)):
                value = ref[rows, lanes] if f is None else ref[f, rows, lanes]
                ends.append(value.astype(jnp.float32))
            here = lane >> 5 == count
            right = jnp.where(here, roll(ends[1], 32 * count + 32, 1), right)
            left = jnp.where(here, roll(ends[0], 32 * count, 1), left)
            count += 1
            if count == 4:
                out.put(at, right, left)
                count, at = 0, at + 8
    if count:
        out.put(at, right, left)


def pack_y_rows(slabs):
    return 8 * (-(-24 * slabs // 32) + 3)


def start_kernel(
    parity, motion, stress, buoyancy, first, shear, surface, momentum, depth, wet, one, two,
    motion_out, stress_out, solid_out, ocean_out, floor_out, send_one, send_two,
):
    inbox = Receiver(parity[1] == 0, one, two)
    slabs = motion.shape[2] // 8
    lane = iota((8, LANES), 1)
    fields = [(motion, f, motion_out, f) for f in range(3)]
    fields += [(stress, f, stress_out, f) for f in range(6)]
    fields += [(ref, None, solid_out, f) for f, ref in enumerate((buoyancy, first, shear))]
    count, at = 0, 0
    for ref, f, target, g in fields:
        for row in range(2):
            for k in range(slabs):
                z = slice(8 * k, 8 * k + 8)
                value = ref[row, z, :] if f is None else ref[f, row, z, :]
                if count == 0:
                    packed = inbox.right(at), inbox.left(at)
                after = roll(packed[0], -4 * count, 1)
                before = roll(packed[1], 124 - 4 * count, 1)
                halo = jnp.where(lane < 4, after, jnp.where(lane >= 124, before, 0.0))
                target[g, row, z, 0:LANES] = value
                target[g, row, z, LANES : 2 * LANES] = halo
                count += 1
                if count == 32:
                    count, at = 0, at + 8
    if count:
        count, at = 0, at + 8
    targets = ((surface, None), (momentum, 0), (momentum, 1), (depth, None), (wet, None))
    for i, (ref, f) in enumerate(targets):
        for group in range(2):
            rows = slice(8 * group, 8 * group + 8)
            if count == 0:
                packed = inbox.right(at), inbox.left(at)
            after = roll(packed[0], -32 * count, 1)
            before = roll(packed[1], 96 - 32 * count, 1)
            halo = jnp.where(lane < 32, after, jnp.where(lane >= 96, before, 0.0))
            for t in range(TILES):
                if t == TILES - 1:
                    value = halo
                else:
                    lanes = slice(LANES * t, LANES * t + LANES)
                    value = ref[rows, lanes] if f is None else ref[f, rows, lanes]
                    value = value.astype(jnp.float32)
                if i < 3:
                    ocean_out[i, t, rows, :] = value
                else:
                    floor_out[i - 3, t, rows, :] = value
            count += 1
            if count == 4:
                count, at = 0, at + 8
    out = Sender(parity[0] == 0, send_one, send_two)
    static = (floor_out.at[0], floor_out.at[1])
    finish(
        out, slabs, motion_out, stress_out, solid_out, ocean_out, floor_out.at[1], None, "first",
        static,
    )


def ocean_part(
    inbox, base, slabs, motion, ocean, floor, kind, coef, height, flow, row_left
):
    _, ocean_at, _, more_at, static_at = offsets(slabs)
    wide = kind == "last"
    low = iota((8, LANES), 0) < 4

    def joined(upper, lower):
        return jnp.where(low, upper, lower)

    def floor_tile(f, t, wide_rows):
        at = static_at + (f * 2 * TILES + t) * 8
        near, far, top = base.right(at), base.right(at + TILES * 8), base.left(at)
        own = floor[f, t, :, :]
        if wide_rows:
            return jnp.concatenate([own, near, joined(far, top)], axis=0)
        return jnp.concatenate([own, joined(near, top)], axis=0)

    def narrowed(value):
        if wide:
            return value
        return jnp.concatenate([value[0:16], joined(value[16:24], value[24:32])], axis=0)

    lane0 = lambda rows: iota((rows, LANES), 1) == 0
    lane127 = lambda rows: iota((rows, LANES), 1) == LANES - 1

    def west(tile, t):
        mine, other = roll(tile(t), 1, 1), roll(tile((t - 1) % TILES), 1, 1)
        return jnp.where(lane0(mine.shape[0]), other, mine)

    def east(tile, t):
        mine, other = roll(tile(t), -1, 1), roll(tile((t + 1) % TILES), -1, 1)
        return jnp.where(lane127(mine.shape[0]), other, mine)

    own_last = motion[2, 1, 0:1, :]
    spread_left, spread_last = upsampled([row_left, own_last])
    for t in range(TILES):
        wet = floor_tile(1, t, True)
        coef[0, t] = narrowed(wet)
        coef[1, t] = narrowed(wet * roll(wet, -1, 0))
        coef[7, t] = floor_tile(0, t, wide)
    for t in range(TILES):
        wet = coef[0, t]
        coef[8, t] = wet * east(lambda i: coef[0, i], t)
    for t in range(TILES):
        for at, depth_side in ((1, 0), (8, 1)):
            face = coef[at, t]
            near = [roll(face, -1, 0), roll(face, 1, 0)]
            tile = functools.partial(lambda at, i: coef[at, i], at)
            near += [east(tile, t), west(tile, t)]
            total = near[0] + near[1] + near[2] + near[3]
            for j in range(4):
                coef[at + 1 + j, t] = VISCOSITY * face * near[j]
            coef[at + 5, t] = face - VISCOSITY * face * total
        depth = coef[7, t]
        coef[14, t] = depth + east(lambda i: coef[7, i], t)
    for t in range(TILES):
        depth = coef[7, t]
        coef[7, t] = depth + roll(depth, -1, 0)
        coef[1, t] = WAVE_STEP * 0.5 * coef[1, t]
        coef[8, t] = WAVE_STEP * 0.5 * coef[8, t]
        for f in range(3):
            at = (f * TILES + t) * 8
            near, top = inbox.right(ocean_at + at), inbox.left(ocean_at + at)
            first, second = ocean[f, t, 0:8, :], ocean[f, t, 8:16, :]
            wet = coef[0, t]
            if f == 0:
                first = first + UPLIFT_GAIN * wet[0:8] * spread_left[t : t + 1]
                near = near + UPLIFT_GAIN * wet[16:24] * spread_last[t : t + 1]
            if wide:
                far = inbox.right(more_at + at)
                value = jnp.concatenate([first, second, near, joined(far, top)], axis=0)
            else:
                value = jnp.concatenate([first, second, joined(near, top)], axis=0)
            if f == 0:
                height[t] = value
            else:
                flow[0, f - 1, t] = value
        coef[0, t] = WAVE_STEP * coef[0, t]
    for step in range(NSUB):
        old, new = step % 2, (step + 1) % 2
        for t in range(TILES):
            m, n = flow[old, 0, t], flow[old, 1, t]
            spill = (m - roll(m, 1, 0)) + (n - west(lambda i: flow[old, 1, i], t))
            height[t] = height[t] - coef[0, t] * spill
        for t in range(TILES):
            h = height[t]
            ahead = [roll(h, -1, 0), east(lambda i: height[i], t)]
            for d in range(2):
                at = 1 + 7 * d
                tile = functools.partial(lambda d, i: flow[old, d, i], d)
                q = flow[old, d, t]
                slope = (coef[at + 6, t] + h + ahead[d]) * (ahead[d] - h)
                value = coef[at + 5, t] * q - coef[at, t] * slope
                value = value + coef[at + 1, t] * roll(q, -1, 0)
                value = value + coef[at + 2, t] * roll(q, 1, 0)
                value = value + coef[at + 3, t] * east(tile, t)
                value = value + coef[at + 4, t] * west(tile, t)
                flow[new, d, t] = value


def step_kernel(kind, last, is_first, *refs):
    parity, base_one, base_two = refs[0:3]
    refs = refs[3:]
    if is_first:
        one, two = base_one, base_two
    else:
        one, two = refs[0:2]
        refs = refs[2:]
    motion, stress, solid, ocean, floor = refs[0:5]
    if last:
        motion_out, stress_out, surface_out, momentum_out = refs[5:9]
        refs = refs[9:]
    else:
        motion_out, stress_out, ocean_out, send_one, send_two = refs[5:10]
        refs = refs[10:]
    coef, height, flow, edge, speed = refs
    slabs = motion.shape[2] // 8
    part, ocean_at, extra_at, more_at, static_at = offsets(slabs)
    even = parity[0] == 0
    base = Receiver(even, base_one, base_two)
    inbox = Receiver(even, one, two)

    def extra_row(take):
        return jnp.concatenate([take(extra_at)[0:1], take(extra_at + 8)[0:1]], axis=1)

    row_left = extra_row(inbox.left)
    loaded = None if is_first else -LOAD_GAIN * extra_row(inbox.right)
    ocean_part(inbox, base, slabs, motion, ocean, floor, kind, coef, height, flow, row_left)
    blocks = 3 if last else 2
    sums = [[] for _ in range(blocks)]
    for t in range(TILES):
        h = height[t]
        wet = (1.0 / WAVE_STEP) * coef[0, t]
        for b in range(blocks):
            rows = slice(8 * b, 8 * b + 8)
            sums[b].append(jnp.sum(wet[rows] * h[rows], axis=0, keepdims=True))
        if last:
            if t < TILES - 1:
                lanes = slice(LANES * t, LANES * t + LANES)
                surface_out[:, lanes] = h[0:16]
                for d in range(2):
                    momentum_out[d, :, lanes] = flow[NSUB % 2, d, t, 0:16, :]
        else:
            ocean_out[0, t] = h[0:16]
            for d in range(2):
                ocean_out[1 + d, t] = flow[NSUB % 2, d, t, 0:16, :]
    means = block_means(sums)

    def old(f, row):
        def get(k):
            value = stress[f, row, 8 * k : 8 * k + 8, :]
            if (f, row, k) == (2, 1, 0) and loaded is not None:
                value = jnp.where(iota(value.shape, 0) == 0, loaded, value)
            return value

        return get

    def new(f, row):
        return lambda k: speed[f, row, 8 * k : 8 * k + 8, :]

    for k in range(slabs):
        z = slice(8 * k, 8 * k + 8)
        xx = [stress[0, 0, z, :], stress[0, 1, z, :], inbox.solid(1, 2 * part, k, slabs)]
        xy = [inbox.solid(-1, part, k, slabs), stress[3, 0, z, :], stress[3, 1, z, :]]
        xz = [inbox.solid(-1, 2 * part, k, slabs), stress[4, 0, z, :], stress[4, 1, z, :]]
        rate_left = SOLID_STEP * base.solid(-1, more_at, k, slabs)
        rate_right = SOLID_STEP * base.solid(1, more_at, k, slabs)
        speed[0, 2, z, :] = inbox.solid(-1, 0, k, slabs) + rate_left * xx[0]
        speed[1, 2, z, :] = inbox.solid(1, 0, k, slabs) - rate_right * xy[2]
        speed[2, 2, z, :] = inbox.solid(1, part, k, slabs) - rate_right * xz[2]
        for row in range(2):
            rate = SOLID_STEP * solid[0, row, z, :]
            yy, zz, yz = stress[1, row, z, :], old(2, row)(k), stress[5, row, z, :]
            mid_xy, mid_xz = xy[row + 1], xz[row + 1]
            force_x = (xx[row + 1] - xx[row]) + (mid_xy - prev_lane(mid_xy))
            force_x = force_x + (mid_xz - below(old(4, row), k))
            force_y = (mid_xy - xy[row]) + (next_lane(yy) - yy) + (yz - below(old(5, row), k))
            force_z = (mid_xz - xz[row]) + (yz - prev_lane(yz))
            force_z = force_z + (above(old(2, row), k, slabs) - zz)
            for f, force in enumerate((force_x, force_y, force_z)):
                value = motion[f, row, z, :] + rate * force
                speed[f, row, z, :] = value
                if last:
                    motion_out[f, row, z, :] = value[:, :LANES]
                else:
                    motion_out[f, row, z, :] = value
    width = LANES if last else 2 * LANES
    for k in range(slabs):
        z = slice(8 * k, 8 * k + 8)
        x_of = [speed[0, 2, z, :], speed[0, 0, z, :], speed[0, 1, z, :]]
        y_of = [speed[1, 0, z, :], speed[1, 1, z, :], speed[1, 2, z, :]]
        z_of = [speed[2, 0, z, :], speed[2, 1, z, :], speed[2, 2, z, :]]
        for row in range(2):
            vx, vy, vz = x_of[row + 1], y_of[row], z_of[row]
            strain_x = vx - x_of[row]
            strain_y = vy - prev_lane(vy)
            strain_z = vz - below(new(2, row), k)
            shear = SOLID_STEP * solid[2, row, z, :]
            lame = SOLID_STEP * solid[1, row, z, :]
            common = lame * (strain_x + strain_y + strain_z)
            twice = shear + shear
            rates = [common + twice * strain for strain in (strain_x, strain_y, strain_z)]
            rates.append(shear * ((next_lane(vx) - vx) + (y_of[row + 1] - vy)))
            rates.append(shear * ((above(new(0, row), k, slabs) - vx) + (z_of[row + 1] - vz)))
            rates.append(shear * ((above(new(1, row), k, slabs) - vy) + (next_lane(vz) - vz)))
            for f in range(6):
                value = stress[f, row, z, :] + rates[f]
                stress_out[f, row, z, :] = value[:, :width]
    stress_out[2, 0, 0:1, :] = -LOAD_GAIN * means[1][:, :width]
    if last:
        stress_out[2, 1, 0:1, :] = -LOAD_GAIN * means[2][:, :width]
        return
    out = Sender(even, send_one, send_two)
    next_kind = "last" if edge else "usual"
    finish(
        out, slabs, motion_out, stress_out, solid, ocean_out, floor.at[1], means[0], next_kind
    )


def swap(size, start):
    pairs = []
    for i in range(start, size - 1, 2):
        pairs += [(i, i + 1), (i + 1, i)]
    return pairs


def exchanged(first, second, axis):
    size = lax.axis_size(axis)
    return (
        lax.ppermute(first, axis, swap(size, 0)),
        lax.ppermute(second, axis, swap(size, 1)),
    )


def body(motion, stress, buoyancy, lame_first, lame_shear, surface, momentum, bathymetry, wet_mask):
    depth_cells = motion.shape[2]
    slabs = depth_cells // 8
    f32 = jnp.float32

    def array(*shape):
        return jax.ShapeDtypeStruct(shape, f32)

    def call(kernel, outs, args, scratch=()):
        specs = [pl.BlockSpec(memory_space=pltpu.SMEM)]
        specs += [pl.BlockSpec(memory_space=pltpu.VMEM)] * (len(args) - 1)
        return pl.pallas_call(
            kernel,
            out_shape=outs,
            in_specs=specs,
            out_specs=tuple(pl.BlockSpec(memory_space=pltpu.VMEM) for _ in outs),
            scratch_shapes=list(scratch),
            interpret=INTERPRET,
        )(*args)

    parity = jnp.stack([lax.axis_index("gx") % 2, lax.axis_index("gy") % 2]).astype(jnp.int32)
    own = (
        motion, stress, buoyancy, lame_first, lame_shear, surface, momentum, bathymetry, wet_mask,
    )
    rows = pack_y_rows(slabs)
    send = call(pack_y_kernel, (array(rows, LANES),) * 2, (parity, *own))
    received = exchanged(*send, "gy")
    state = (
        array(3, 2, depth_cells, 256),
        array(6, 2, depth_cells, 256),
    )
    rows = payload_rows(slabs, "first")
    outs = (
        *state,
        array(3, 2, depth_cells, 256),
        array(3, TILES, 16, LANES),
        array(2, TILES, 16, LANES),
        array(rows, LANES),
        array(rows, LANES),
    )
    motion, stress, solid, ocean, floor, *send = call(start_kernel, outs, (parity, *own, *received))
    base = None
    for step in range(STEPS):
        received = exchanged(*send, "gx")
        last = step == STEPS - 1
        if step == 0:
            base = received
            inputs = (parity, *base)
        else:
            inputs = (parity, *base, *received)
        inputs = (*inputs, motion, stress, solid, ocean, floor)
        height = 32 if last else 24
        scratch = (
            pltpu.VMEM((15, TILES, height, LANES), f32),
            pltpu.VMEM((TILES, height, LANES), f32),
            pltpu.VMEM((2, 2, TILES, height, LANES), f32),
            pltpu.VMEM((3, 3, depth_cells, 256), f32),
        )
        if last:
            outs = (
                array(3, 2, depth_cells, LANES),
                array(6, 2, depth_cells, LANES),
                array(16, 8 * LANES),
                array(2, 16, 8 * LANES),
            )
        else:
            rows = payload_rows(slabs, "last" if step == STEPS - 2 else "usual")
            outs = (*state, array(3, TILES, 16, LANES), array(rows, LANES), array(rows, LANES))
        kernel = functools.partial(
            run_step, "last" if last else "usual", last, step == 0, step == STEPS - 2
        )
        results = call(kernel, outs, inputs, scratch)
        if not last:
            motion, stress, ocean, *send = results
    return results


def run_step(kind, last, is_first, edge, *refs):
    coef, height, flow, speed = refs[-4:]
    step_kernel(kind, last, is_first, *refs[:-4], coef, height, flow, edge, speed)


def solution(mesh):
    return jax.shard_map(
        body,
        mesh=mesh,
        in_specs=(
            P(None, "gx", None, "gy"),
            P(None, "gx", None, "gy"),
            P("gx", None, "gy"),
            P("gx", None, "gy"),
            P("gx", None, "gy"),
            P("gx", "gy"),
            P(None, "gx", "gy"),
            P("gx", "gy"),
            P("gx", "gy"),
        ),
        out_specs=(
            P(None, "gx", None, "gy"),
            P(None, "gx", None, "gy"),
            P("gx", "gy"),
            P(None, "gx", "gy"),
        ),
        check_vma=False,
    )
```

time: 780 us -> 135 us (0.17); the launches traced: 768 us -> 134 us
  starting transfers between devices: 354 us -> 24.4 us
  waiting for transfers between devices: 296 us -> 70.7 us
  local copies, waits for them, and re-layouts: 65.1 us -> 3.6 us
  other arithmetic: 48.3 us -> 0.6 us
  Pallas kernels: 0 us -> 34.5 us
    ppermute x108 -> x10, starting transfers between devices: 354 us -> 24.4 us  [the longest x5 22.8 us: exchanged(): lax.ppermute(second, axis, swap(size, 1))]
    ppermute x108 -> x10, waiting for transfers between devices: 296 us -> 70.7 us  [the longest x5 52.2 us: exchanged(): lax.ppermute(second, axis, swap(size, 1))]
    pallas_call x0 -> x6, Pallas kernels: none -> 34.5 us  [call(): pl.pallas_call(kernel, out_shape=outs, in_specs=specs, out_specs=tuple((p...]
    slice x60 -> x0, local copies, waits for them, and re-layouts: 19.1 us -> none  [the longest x13 8.39 us: padded(): last = lax.slice_in_dim(shard, length - width, length, axis=dim)]
    concatenate x30 -> x0, other arithmetic: 13.7 us -> none  [the longest x25 12.7 us: padded(): shard = jnp.concatenate([before, shard, after], axis=dim)]
    another operation x47 -> x1, other arithmetic: 14.2 us -> 0.6 us  [body(): jnp.stack([lax.axis_index('gx') % 2, lax.axis_index('gy') % 2])]
    reshape x8 -> x0, local copies, waits for them, and re-layouts: 11.3 us -> none  [the longest x4 6.17 us: block_average(): fine_grid.reshape(count_x // RATIO, RATIO, count_y // RATIO, RATIO)]
    squeeze x26 -> x0, local copies, waits for them, and re-layouts: 9.53 us -> none  [the longest x16 6.68 us: wave_substep(): height, flow_x, flow_y = (ocean_state[0], ocean_state[1], ocean_state[2])]
  transfers between devices with their start and end apart: 108 -> 10, of which waited for: 49 -> 9; matrix products, arithmetic and copies ran while one was open for 6% -> 0% of each run, Pallas kernels for 0% -> 0%
where the time goes in v1:
time: 135 us; the launch traced here: 134 us
  waiting for transfers between devices  70.7 us (52%)
  Pallas kernels  34.5 us (26%)
  starting transfers between devices  24.4 us (18%)
  local copies, waits for them, and re-layouts  3.6 us (3%)
    ppermute x5, waiting for transfers between devices, exchanged(): lax.ppermute(second, axis, swap(size, 1))  52.2 us
    pallas_call x6, Pallas kernels, call(): pl.pallas_call(kernel, out_shape=outs, in_specs=specs, out_specs=tuple((p...  34.5 us
    ppermute x5, starting transfers between devices, exchanged(): lax.ppermute(second, axis, swap(size, 1))  22.8 us
    ppermute x5, waiting for transfers between devices, exchanged(): lax.ppermute(first, axis, swap(size, 0))  18.4 us
    unnamed x20, local copies, waits for them, and re-layouts  3.6 us
  transfers between devices with their start and end apart: 10, of which 9 were waited for; matrix products, arithmetic and copies ran while one was open for 0% of the time, Pallas kernels for 0%

profile of v1, /device:TPU:192, one launch (start us, length us, event | category | flops | bytes accessed | tf_op | source)
XLA Modules:
  0.0 134.5 jit_solution(3663258329942923080)
XLA Ops:
  0.6 0.6 pad_add_fusion.parity.refs_0_
  1.2 2.6 %shard_map.120 = (f32[96,128]{1,0:T(8,128)}, f32[96,128]{1,0:T(8,128)}) custom-call(s32[2]{0:T(128)} %pad_add_fusion.parity.refs_0_, f32[3,2,96,128]{3,2,1,0:T(8,128)} %motion.3, f32[6,2,96,128]{3,2,1,0:T(8,128)} %stress.3, f32[2,96,128]{2,1,0:T(8,128)} %buoyancy.3, f32[2,96,128]{2,1,0:T(8,128)} %first.3, f32[2,96,128]{2,1,0:T(8,128)} %shear.3, ...), custom_call_target="tpu_custom_call" | custom-call | tf_op jit(solution)/shard_map/pallas_call | solution.py:566
  3.9 0.0 collective-permute-start
  3.9 3.0 %collective-permute-start.1 = (f32[96,128]{1,0:T(8,128)}, f32[96,128]{1,0:T(8,128)S(1)}, u32[]{:S(2)}, u32[]{:S(2)}) collective-permute-start(f32[96,128]{1,0:T(8,128)} %get-tuple-element.29), channel_id=1, source_target_pairs={{1,2},{2,1},{3,4},{4,3},{5,6},{6,5},{9,10},{10,9},{11,12},{12,11},... | collective-permute-start | bytes 147464 | tf_op jit(solution)/shard_map/ppermute | solution.py:551
  6.9 0.0 collective-permute-done.one
  6.9 0.0 copy-start.8
  6.9 2.6 %collective-permute-done.1.two = f32[96,128]{1,0:T(8,128)S(1)} collective-permute-done((f32[96,128]{1,0:T(8,128)}, f32[96,128]{1,0:T(8,128)S(1)}, u32[]{:S(2)}, u32[]{:S(2)}) %collective-permute-start.1) | collective-permute-done | bytes 49184 | tf_op jit(solution)/shard_map/ppermute | solution.py:551
  9.5 0.0 copy-done.8
  9.5 0.0 copy-start.9
  9.5 0.6 copy-done.9
  10.1 5.3 %shard_map.121 = (f32[3,2,96,256]{3,2,1,0:T(8,128)}, f32[6,2,96,256]{3,2,1,0:T(8,128)}, f32[3,2,96,256]{3,2,1,0:T(8,128)}, f32[3,9,16,128]{3,2,1,0:T(8,128)}, f3...) custom-call(s32[2]{0:T(128)} %pad_add_fusion.parity.refs_0_, f32[3,2,96,128]{3,2,1,0:T(8,128)} %motion.3, ...), custom_call_target="tpu_custom_call" | custom-call | tf_op jit(solution)/shard_map/pallas_call | solution.py:566
  15.4 1.6 %collective-permute-start.2 = (f32[936,128]{1,0:T(8,128)}, f32[936,128]{1,0:T(8,128)S(1)}, u32[]{:S(2)}, u32[]{:S(2)}) collective-permute-start(f32[936,128]{1,0:T(8,128)} %get-tuple-element.30), channel_id=1, source_target_pairs={{0,8},{8,0},{16,24},{24,16},{32,40},{40,32},{48,56},{56,48},{64,72... | collective-permute-start | bytes 1437704 | tf_op jit(solution)/shard_map/ppermute | solution.py:550
  17.0 6.2 %collective-permute-start.3 = (f32[936,128]{1,0:T(8,128)}, f32[936,128]{1,0:T(8,128)S(1)}, u32[]{:S(2)}, u32[]{:S(2)}) collective-permute-start(f32[936,128]{1,0:T(8,128)} %get-tuple-element.31), channel_id=1, source_target_pairs={{8,16},{16,8},{24,32},{32,24},{40,48},{48,40},{56,64},{64,56},{72,... | collective-permute-start | bytes 1437704 | tf_op jit(solution)/shard_map/ppermute | solution.py:551
  23.2 5.7 %collective-permute-done.2.refs_1_ = f32[936,128]{1,0:T(8,128)S(1)} collective-permute-done((f32[936,128]{1,0:T(8,128)}, f32[936,128]{1,0:T(8,128)S(1)}, u32[]{:S(2)}, u32[]{:S(2)}) %collective-permute-start.2) | collective-permute-done | bytes 479264 | tf_op jit(solution)/shard_map/ppermute | solution.py:550
  29.0 0.0 copy-start
  29.0 19.7 %collective-permute-done.3.refs_2_ = f32[936,128]{1,0:T(8,128)S(1)} collective-permute-done((f32[936,128]{1,0:T(8,128)}, f32[936,128]{1,0:T(8,128)S(1)}, u32[]{:S(2)}, u32[]{:S(2)}) %collective-permute-start.3) | collective-permute-done | bytes 479264 | tf_op jit(solution)/shard_map/ppermute | solution.py:551
  48.6 0.0 copy-start.1
  48.6 0.0 copy-done
  48.6 0.8 copy-done.1
  49.4 6.6 %shard_map.122 = (f32[3,2,96,256]{3,2,1,0:T(8,128)}, f32[6,2,96,256]{3,2,1,0:T(8,128)}, f32[3,9,16,128]{3,2,1,0:T(8,128)}, f32[544,128]{1,0:T(8,128)}, f32[544,128]{1,0:T(8,128)}) custom-call(s32[2]{0:T(128)} %pad_add_fusion.parity.refs_0_, f32[936,128]{1,0:T(8,128)} %copy-done, f32[936,128]{1,0:T(8,128)} %copy-done.1, ...), custom_call_target="tpu_custom_call" | custom-call | tf_op jit(solution)/shard_map/pallas_call | solution.py:566
  56.0 0.0 collective-permute-start.4
  56.0 4.5 %collective-permute-start.5 = (f32[544,128]{1,0:T(8,128)}, f32[544,128]{1,0:T(8,128)S(1)}, u32[]{:S(2)}, u32[]{:S(2)}) collective-permute-start(f32[544,128]{1,0:T(8,128)} %get-tuple-element.38), channel_id=1, source_target_pairs={{8,16},{16,8},{24,32},{32,24},{40,48},{48,40},{56,64},{64,56},{72,... | collective-permute-start | bytes 835592 | tf_op jit(solution)/shard_map/ppermute | solution.py:551
  60.5 4.4 %collective-permute-done.4.refs_3_ = f32[544,128]{1,0:T(8,128)S(1)} collective-permute-done((f32[544,128]{1,0:T(8,128)}, f32[544,128]{1,0:T(8,128)S(1)}, u32[]{:S(2)}, u32[]{:S(2)}) %collective-permute-start.4) | collective-permute-done | bytes 278560 | tf_op jit(solution)/shard_map/ppermute | solution.py:550
  64.8 0.0 copy-start.4
  64.8 10.0 %collective-permute-done.5.refs_4_ = f32[544,128]{1,0:T(8,128)S(1)} collective-permute-done((f32[544,128]{1,0:T(8,128)}, f32[544,128]{1,0:T(8,128)S(1)}, u32[]{:S(2)}, u32[]{:S(2)}) %collective-permute-start.5) | collective-permute-done | bytes 278560 | tf_op jit(solution)/shard_map/ppermute | solution.py:551
  74.8 0.0 copy-start.6
  74.8 0.0 copy-done.4
  74.8 0.7 copy-done.6
  75.6 6.8 %shard_map.123 = (f32[3,2,96,256]{3,2,1,0:T(8,128)}, f32[6,2,96,256]{3,2,1,0:T(8,128)}, f32[3,9,16,128]{3,2,1,0:T(8,128)}, f32[544,128]{1,0:T(8,128)}, f32[544,128]{1,0:T(8,128)}) custom-call(s32[2]{0:T(128)} %pad_add_fusion.parity.refs_0_, f32[936,128]{1,0:T(8,128)} %copy-done, f32[936,128]{1,0:T(8,128)} %copy-done.1, f32[544,128]{1,0:T(8,128)} %copy-done.4, ...), custom_call_target="tpu_custom_call" | custom-call | tf_op jit(solution)/shard_map/pallas_call | solution.py:566
  82.4 0.0 collective-permute-start.6
  82.4 4.6 %collective-permute-start.7 = (f32[544,128]{1,0:T(8,128)}, f32[544,128]{1,0:T(8,128)S(1)}, u32[]{:S(2)}, u32[]{:S(2)}) collective-permute-start(f32[544,128]{1,0:T(8,128)} %get-tuple-element.43), channel_id=1, source_target_pairs={{8,16},{16,8},{24,32},{32,24},{40,48},{48,40},{56,64},{64,56},{72,... | collective-permute-start | bytes 835592 | tf_op jit(solution)/shard_map/ppermute | solution.py:551
  87.0 3.3 %collective-permute-done.6.refs_3_ = f32[544,128]{1,0:T(8,128)S(1)} collective-permute-done((f32[544,128]{1,0:T(8,128)}, f32[544,128]{1,0:T(8,128)S(1)}, u32[]{:S(2)}, u32[]{:S(2)}) %collective-permute-start.6) | collective-permute-done | bytes 278560 | tf_op jit(solution)/shard_map/ppermute | solution.py:550
  90.3 0.0 copy-start.5
  90.3 10.0 %collective-permute-done.7.refs_4_ = f32[544,128]{1,0:T(8,128)S(1)} collective-permute-done((f32[544,128]{1,0:T(8,128)}, f32[544,128]{1,0:T(8,128)S(1)}, u32[]{:S(2)}, u32[]{:S(2)}) %collective-permute-start.7) | collective-permute-done | bytes 278560 | tf_op jit(solution)/shard_map/ppermute | solution.py:551
  100.3 0.0 copy-start.7
  100.3 0.0 copy-done.5
  100.3 0.7 copy-done.7
  101.1 7.0 %shard_map.124 = (f32[3,2,96,256]{3,2,1,0:T(8,128)}, f32[6,2,96,256]{3,2,1,0:T(8,128)}, f32[3,9,16,128]{3,2,1,0:T(8,128)}, f32[760,128]{1,0:T(8,128)}, f32[760,128]{1,0:T(8,128)}) custom-call(s32[2]{0:T(128)} %pad_add_fusion.parity.refs_0_, f32[936,128]{1,0:T(8,128)} %copy-done, f32[936,128]{1,0:T(8,128)} %copy-done.1, f32[544,128]{1,0:T(8,128)} %copy-done.5, ...), custom_call_target="tpu_custom_call" | custom-call | tf_op jit(solution)/shard_map/pallas_call | solution.py:566
  108.0 0.0 collective-permute-start.8
  108.0 4.5 %collective-permute-start.9 = (f32[760,128]{1,0:T(8,128)}, f32[760,128]{1,0:T(8,128)S(1)}, u32[]{:S(2)}, u32[]{:S(2)}) collective-permute-start(f32[760,128]{1,0:T(8,128)} %get-tuple-element.48), channel_id=1, source_target_pairs={{8,16},{16,8},{24,32},{32,24},{40,48},{48,40},{56,64},{64,56},{72,... | collective-permute-start | bytes 1167368 | tf_op jit(solution)/shard_map/ppermute | solution.py:551
  112.5 5.0 %collective-permute-done.8.refs_3_ = f32[760,128]{1,0:T(8,128)S(1)} collective-permute-done((f32[760,128]{1,0:T(8,128)}, f32[760,128]{1,0:T(8,128)S(1)}, u32[]{:S(2)}, u32[]{:S(2)}) %collective-permute-start.8) | collective-permute-done | bytes 389152 | tf_op jit(solution)/shard_map/ppermute | solution.py:550
  117.5 0.0 copy-start.2
  117.5 10.0 %collective-permute-done.9.refs_4_ = f32[760,128]{1,0:T(8,128)S(1)} collective-permute-done((f32[760,128]{1,0:T(8,128)}, f32[760,128]{1,0:T(8,128)S(1)}, u32[]{:S(2)}, u32[]{:S(2)}) %collective-permute-start.9) | collective-permute-done | bytes 389152 | tf_op jit(solution)/shard_map/ppermute | solution.py:551
  127.5 0.0 copy-start.3
  127.5 0.0 copy-done.2
  127.5 0.7 copy-done.3
  128.3 6.2 %shard_map.125 = (f32[3,2,96,128]{3,2,1,0:T(8,128)}, f32[6,2,96,128]{3,2,1,0:T(8,128)}, f32[16,1024]{1,0:T(8,128)}, f32[2,16,1024]{2,1,0:T(8,128)}) custom-call(s32[2]{0:T(128)} %pad_add_fusion.parity.refs_0_, f32[936,128]{1,0:T(8,128)} %copy-done, f32[936,128]{1,0:T(8,128)} %copy-done.1, f32[760,128]{1,0:T(8,128)} %copy-done.2, f32[760,128]{1,0:T(8,128)} %copy-done.3, ...), custom_call_target="tpu_custom_call" | custom-call | tf_op jit(solution)/shard_map/pallas_call | solution.py:566
Async XLA Ops:
  3.9 3.0 %collective-permute-start = (f32[96,128]{1,0:T(8,128)}, f32[96,128]{1,0:T(8,128)S(1)}, u32[]{:S(2)}, u32[]{:S(2)}) collective-permute-start(f32[96,128]{1,0:T(8,128)} %get-tuple-element.28), channel_id=1, source_target_pairs={{0,1},{1,0},{2,3},{3,2},{4,5},{5,4},{6,7},{7,6},{8,9},{9,8},{10,11... | collective-permute-start | bytes 147464 | tf_op jit(solution)/shard_map/ppermute | solution.py:550
  3.9 5.6 %collective-permute-start.1 = (f32[96,128]{1,0:T(8,128)}, f32[96,128]{1,0:T(8,128)S(1)}, u32[]{:S(2)}, u32[]{:S(2)}) collective-permute-start(f32[96,128]{1,0:T(8,128)} %get-tuple-element.29), channel_id=1, source_target_pairs={{1,2},{2,1},{3,4},{4,3},{5,6},{6,5},{9,10},{10,9},{11,12},{12,11},... | collective-permute-start | bytes 147464 | tf_op jit(solution)/shard_map/ppermute | solution.py:551
  6.9 2.6 %copy-start.8 = (f32[96,128]{1,0:T(8,128)}, f32[96,128]{1,0:T(8,128)S(1)}, u32[]{:S(2)}) copy-start(f32[96,128]{1,0:T(8,128)S(1)} %collective-permute-done.one) | copy-start | bytes 147460
  9.5 0.6 copy-start.9
  15.4 13.6 %collective-permute-start.2 = (f32[936,128]{1,0:T(8,128)}, f32[936,128]{1,0:T(8,128)S(1)}, u32[]{:S(2)}, u32[]{:S(2)}) collective-permute-start(f32[936,128]{1,0:T(8,128)} %get-tuple-element.30), channel_id=1, source_target_pairs={{0,8},{8,0},{16,24},{24,16},{32,40},{40,32},{48,56},{56,48},{64,72... | collective-permute-start | bytes 1437704 | tf_op jit(solution)/shard_map/ppermute | solution.py:550
  17.0 31.7 %collective-permute-start.3 = (f32[936,128]{1,0:T(8,128)}, f32[936,128]{1,0:T(8,128)S(1)}, u32[]{:S(2)}, u32[]{:S(2)}) collective-permute-start(f32[936,128]{1,0:T(8,128)} %get-tuple-element.31), channel_id=1, source_target_pairs={{8,16},{16,8},{24,32},{32,24},{40,48},{48,40},{56,64},{64,56},{72,... | collective-permute-start | bytes 1437704 | tf_op jit(solution)/shard_map/ppermute | solution.py:551
  29.0 19.7 %copy-start = (f32[936,128]{1,0:T(8,128)}, f32[936,128]{1,0:T(8,128)S(1)}, u32[]{:S(2)}) copy-start(f32[936,128]{1,0:T(8,128)S(1)} %collective-permute-done.2.refs_1_) | copy-start | bytes 1437700
  48.6 0.8 copy-start.1
  56.0 8.8 %collective-permute-start.4 = (f32[544,128]{1,0:T(8,128)}, f32[544,128]{1,0:T(8,128)S(1)}, u32[]{:S(2)}, u32[]{:S(2)}) collective-permute-start(f32[544,128]{1,0:T(8,128)} %get-tuple-element.37), channel_id=1, source_target_pairs={{0,8},{8,0},{16,24},{24,16},{32,40},{40,32},{48,56},{56,48},{64,72... | collective-permute-start | bytes 835592 | tf_op jit(solution)/shard_map/ppermute | solution.py:550
  56.0 18.8 %collective-permute-start.5 = (f32[544,128]{1,0:T(8,128)}, f32[544,128]{1,0:T(8,128)S(1)}, u32[]{:S(2)}, u32[]{:S(2)}) collective-permute-start(f32[544,128]{1,0:T(8,128)} %get-tuple-element.38), channel_id=1, source_target_pairs={{8,16},{16,8},{24,32},{32,24},{40,48},{48,40},{56,64},{64,56},{72,... | collective-permute-start | bytes 835592 | tf_op jit(solution)/shard_map/ppermute | solution.py:551
  64.8 10.0 %copy-start.4 = (f32[544,128]{1,0:T(8,128)}, f32[544,128]{1,0:T(8,128)S(1)}, u32[]{:S(2)}) copy-start(f32[544,128]{1,0:T(8,128)S(1)} %collective-permute-done.4.refs_3_) | copy-start | bytes 835588
  74.8 0.7 copy-start.6
  82.4 8.0 %collective-permute-start.6 = (f32[544,128]{1,0:T(8,128)}, f32[544,128]{1,0:T(8,128)S(1)}, u32[]{:S(2)}, u32[]{:S(2)}) collective-permute-start(f32[544,128]{1,0:T(8,128)} %get-tuple-element.42), channel_id=1, source_target_pairs={{0,8},{8,0},{16,24},{24,16},{32,40},{40,32},{48,56},{56,48},{64,72... | collective-permute-start | bytes 835592 | tf_op jit(solution)/shard_map/ppermute | solution.py:550
  82.4 18.0 %collective-permute-start.7 = (f32[544,128]{1,0:T(8,128)}, f32[544,128]{1,0:T(8,128)S(1)}, u32[]{:S(2)}, u32[]{:S(2)}) collective-permute-start(f32[544,128]{1,0:T(8,128)} %get-tuple-element.43), channel_id=1, source_target_pairs={{8,16},{16,8},{24,32},{32,24},{40,48},{48,40},{56,64},{64,56},{72,... | collective-permute-start | bytes 835592 | tf_op jit(solution)/shard_map/ppermute | solution.py:551
  90.3 10.0 %copy-start.5 = (f32[544,128]{1,0:T(8,128)}, f32[544,128]{1,0:T(8,128)S(1)}, u32[]{:S(2)}) copy-start(f32[544,128]{1,0:T(8,128)S(1)} %collective-permute-done.6.refs_3_) | copy-start | bytes 835588
  100.3 0.7 copy-start.7
  108.0 9.5 %collective-permute-start.8 = (f32[760,128]{1,0:T(8,128)}, f32[760,128]{1,0:T(8,128)S(1)}, u32[]{:S(2)}, u32[]{:S(2)}) collective-permute-start(f32[760,128]{1,0:T(8,128)} %get-tuple-element.47), channel_id=1, source_target_pairs={{0,8},{8,0},{16,24},{24,16},{32,40},{40,32},{48,56},{56,48},{64,72... | collective-permute-start | bytes 1167368 | tf_op jit(solution)/shard_map/ppermute | solution.py:550
  108.0 19.5 %collective-permute-start.9 = (f32[760,128]{1,0:T(8,128)}, f32[760,128]{1,0:T(8,128)S(1)}, u32[]{:S(2)}, u32[]{:S(2)}) collective-permute-start(f32[760,128]{1,0:T(8,128)} %get-tuple-element.48), channel_id=1, source_target_pairs={{8,16},{16,8},{24,32},{32,24},{40,48},{48,40},{56,64},{64,56},{72,... | collective-permute-start | bytes 1167368 | tf_op jit(solution)/shard_map/ppermute | solution.py:551
  117.5 10.0 %copy-start.2 = (f32[760,128]{1,0:T(8,128)}, f32[760,128]{1,0:T(8,128)S(1)}, u32[]{:S(2)}) copy-start(f32[760,128]{1,0:T(8,128)S(1)} %collective-permute-done.8.refs_3_) | copy-start | bytes 1167364
  127.5 0.7 copy-start.3

commit v2 on v1

--- a/solution.py
+++ b/solution.py
@@ -16,9 +16,11 @@
 LOAD_GAIN = 8.0
 
 INTERPRET = False
+VMEM_LIMIT = 20 << 20
 LANES = 128
 TILES = 9
-OCEAN = 3 * TILES * 8
+UNITS = 3 * TILES
+FLOOR_UNITS = 2 * TILES
 
 
 def iota(shape, dim):
@@ -123,6 +125,15 @@
         self.put(at + 8 * slabs, *tails)
 
 
+    def put_halves(self, at, units):
+        low = iota((8, LANES), 0) < 4
+        for i in range(0, len(units), 2):
+            (lower, upper), (lower2, upper2) = units[i], units[min(i + 1, len(units) - 1)]
+            right = jnp.where(low, roll(upper, 4, 0), upper2)
+            left = jnp.where(low, lower, roll(lower2, 4, 0))
+            self.put(at + 4 * i, right, left)
+
+
 class Receiver:
     def __init__(self, even, first_ref, second_ref):
         self.even, self.first, self.second = even, first_ref, second_ref
@@ -132,6 +143,13 @@
 
     def left(self, at):
         return jnp.where(self.even, self.second[at : at + 8, :], self.first[at : at + 8, :])
+
+    def halves(self, at, unit):
+        at = at + 8 * (unit // 2)
+        near, top = self.right(at), self.left(at)
+        near = roll(near, 4, 0) if unit % 2 else near
+        top = top if unit % 2 else roll(top, 4, 0)
+        return near, top
 
     def solid(self, side, at, k, slabs):
         take = self.right if side > 0 else self.left
@@ -142,18 +160,23 @@
 def offsets(slabs):
     part = 8 * slabs + 8
     ocean = 3 * part
-    extra = ocean + OCEAN
+    extra = ocean + 8 * ((UNITS + 1) // 2)
     more = extra + 16
-    return part, ocean, extra, more, more + part
+    return part, ocean, extra, more
 
 
 def payload_rows(slabs, kind):
-    part, _, _, more, static = offsets(slabs)
-    return {"first": static + 4 * TILES * 8, "usual": more, "last": more + OCEAN}[kind]
-
-
-def finish(out, slabs, motion, stress, buoyancy, ocean, wet, mean_row, kind, static=None):
-    part, ocean_at, extra_at, more_at, static_at = offsets(slabs)
+    part, _, _, more = offsets(slabs)
+    return {
+        "first": more + part + 8 * ((FLOOR_UNITS + TILES + 1) // 2),
+        "usual": more,
+        "last": more + 8 * (UNITS + FLOOR_UNITS),
+    }[kind]
+
+
+def finish(out, slabs, motion, stress, buoyancy, ocean, floor, mean_row, kind):
+    part, ocean_at, extra_at, more_at = offsets(slabs)
+    low = iota((8, LANES), 0) < 4
 
     def get(ref, field, row):
         return lambda k: ref[field, row, 8 * k : 8 * k + 8, :]
@@ -185,14 +208,14 @@
     (spread,) = upsampled([motion[2, 0, 0:1, :]])
     for t in range(TILES):
         ocean[0, t, 8:16, :] = (
-            ocean[0, t, 8:16, :] + UPLIFT_GAIN * wet[t, 8:16, :] * spread[t : t + 1]
+            ocean[0, t, 8:16, :] + UPLIFT_GAIN * floor[1, t, 8:16, :] * spread[t : t + 1]
         )
-        for f in range(3):
-            at = (f * TILES + t) * 8
-            lower, upper = ocean[f, t, 0:8, :], ocean[f, t, 8:16, :]
-            out.put(ocean_at + at, upper, lower)
-            if kind == "last":
-                out.put(more_at + at, upper, upper)
+
+    def units(ref, fields):
+        pairs = [(f, t) for f in range(fields) for t in range(TILES)]
+        return [(ref[f, t, 0:8, :], ref[f, t, 8:16, :]) for f, t in pairs]
+
+    out.put_halves(ocean_at, units(ocean, 3))
     top = motion[2, 1, 0:8, :]
     mean_row = jnp.zeros((8, 256), jnp.float32) if mean_row is None else mean_row
     mean_row = jnp.broadcast_to(mean_row, (8, 256))
@@ -201,12 +224,15 @@
         out.put(extra_at + 8 * i, top[:, lanes], mean_row[:, lanes])
     if kind == "first":
         out.put_solid(more_at, slabs, get(buoyancy, 0, 1), get(buoyancy, 0, 0))
-        for f, array in enumerate(static):
-            for t in range(TILES):
-                at = static_at + (f * 2 * TILES + t) * 8
-                lower, upper = array[t, 0:8, :], array[t, 8:16, :]
-                out.put(at, upper, lower)
-                out.put(at + TILES * 8, upper, upper)
+        faces = []
+        for t in range(TILES):
+            wet = floor[1, t, :, :]
+            faces.append(((wet * roll(wet, -1, 0))[0:8], wet[8:16]))
+        out.put_halves(more_at + part, units(floor, 2) + faces)
+    if kind == "last":
+        for i, (lower, upper) in enumerate(units(ocean, 3) + units(floor, 2)):
+            value = jnp.where(low, upper, lower)
+            out.put(more_at + 8 * i, value, value)
 
 
 def pack_y_kernel(
@@ -310,59 +336,23 @@
             if count == 4:
                 count, at = 0, at + 8
     out = Sender(parity[0] == 0, send_one, send_two)
-    static = (floor_out.at[0], floor_out.at[1])
-    finish(
-        out, slabs, motion_out, stress_out, solid_out, ocean_out, floor_out.at[1], None, "first",
-        static,
-    )
-
-
-def ocean_part(
-    inbox, base, slabs, motion, ocean, floor, kind, coef, height, flow, row_left
-):
-    _, ocean_at, _, more_at, static_at = offsets(slabs)
-    wide = kind == "last"
-    low = iota((8, LANES), 0) < 4
-
-    def joined(upper, lower):
-        return jnp.where(low, upper, lower)
-
-    def floor_tile(f, t, wide_rows):
-        at = static_at + (f * 2 * TILES + t) * 8
-        near, far, top = base.right(at), base.right(at + TILES * 8), base.left(at)
-        own = floor[f, t, :, :]
-        if wide_rows:
-            return jnp.concatenate([own, near, joined(far, top)], axis=0)
-        return jnp.concatenate([own, joined(near, top)], axis=0)
-
-    def narrowed(value):
-        if wide:
-            return value
-        return jnp.concatenate([value[0:16], joined(value[16:24], value[24:32])], axis=0)
-
-    lane0 = lambda rows: iota((rows, LANES), 1) == 0
-    lane127 = lambda rows: iota((rows, LANES), 1) == LANES - 1
-
-    def west(tile, t):
-        mine, other = roll(tile(t), 1, 1), roll(tile((t - 1) % TILES), 1, 1)
-        return jnp.where(lane0(mine.shape[0]), other, mine)
-
-    def east(tile, t):
-        mine, other = roll(tile(t), -1, 1), roll(tile((t + 1) % TILES), -1, 1)
-        return jnp.where(lane127(mine.shape[0]), other, mine)
-
-    own_last = motion[2, 1, 0:1, :]
-    spread_left, spread_last = upsampled([row_left, own_last])
+    finish(out, slabs, motion_out, stress_out, solid_out, ocean_out, floor_out, None, "first")
+
+
+def coefficients(floor_tile, after, coef, east, west):
     for t in range(TILES):
-        wet = floor_tile(1, t, True)
-        coef[0, t] = narrowed(wet)
-        coef[1, t] = narrowed(wet * roll(wet, -1, 0))
-        coef[7, t] = floor_tile(0, t, wide)
+        wet = floor_tile(1, t)
+        coef[0, t] = wet
+        face = wet * roll(wet, -1, 0)
+        if after is not None:
+            low = iota((8, LANES), 0) < 4
+            face = jnp.concatenate([face[0:16], jnp.where(low, after(t), face[16:24])], axis=0)
+        coef[1, t] = face
+        coef[7, t] = floor_tile(0, t)
     for t in range(TILES):
-        wet = coef[0, t]
-        coef[8, t] = wet * east(lambda i: coef[0, i], t)
+        coef[8, t] = coef[0, t] * east(lambda i: coef[0, i], t)
     for t in range(TILES):
-        for at, depth_side in ((1, 0), (8, 1)):
+        for at in (1, 8):
             face = coef[at, t]
             near = [roll(face, -1, 0), roll(face, 1, 0)]
             tile = functools.partial(lambda at, i: coef[at, i], at)
@@ -371,23 +361,59 @@
             for j in range(4):
                 coef[at + 1 + j, t] = VISCOSITY * face * near[j]
             coef[at + 5, t] = face - VISCOSITY * face * total
-        depth = coef[7, t]
-        coef[14, t] = depth + east(lambda i: coef[7, i], t)
+        coef[14, t] = coef[7, t] + east(lambda i: coef[7, i], t)
     for t in range(TILES):
         depth = coef[7, t]
         coef[7, t] = depth + roll(depth, -1, 0)
         coef[1, t] = WAVE_STEP * 0.5 * coef[1, t]
         coef[8, t] = WAVE_STEP * 0.5 * coef[8, t]
+
+
+def ocean_part(
+    inbox, base, slabs, motion, ocean, floor, wide, ready, coef, height, flow, row_left
+):
+    part, ocean_at, _, more_at = offsets(slabs)
+    low = iota((8, LANES), 0) < 4
+
+    def joined(upper, lower):
+        return jnp.where(low, upper, lower)
+
+    def floor_tile(f, t):
+        near, top = base.halves(more_at + part, f * TILES + t)
+        own = floor[f, t, :, :]
+        if wide:
+            far = inbox.right(more_at + 8 * (UNITS + f * TILES + t))
+            return jnp.concatenate([own, joined(near, far), joined(far, top)], axis=0)
+        return jnp.concatenate([own, joined(near, top)], axis=0)
+
+    lane0 = lambda rows: iota((rows, LANES), 1) == 0
+    lane127 = lambda rows: iota((rows, LANES), 1) == LANES - 1
+
+    def west(tile, t):
+        mine, other = roll(tile(t), 1, 1), roll(tile((t - 1) % TILES), 1, 1)
+        return jnp.where(lane0(mine.shape[0]), other, mine)
+
+    def east(tile, t):
+        mine, other = roll(tile(t), -1, 1), roll(tile((t + 1) % TILES), -1, 1)
+        return jnp.where(lane127(mine.shape[0]), other, mine)
+
+    if not ready:
+        after = lambda t: base.halves(more_at + part, 2 * TILES + t)[0]
+        coefficients(floor_tile, None if wide else after, coef, east, west)
+    own_last = motion[2, 1, 0:1, :]
+    spread_left, spread_last = upsampled([row_left, own_last])
+    for t in range(TILES):
+        wet = coef[0, t]
         for f in range(3):
-            at = (f * TILES + t) * 8
-            near, top = inbox.right(ocean_at + at), inbox.left(ocean_at + at)
+            near, top = inbox.halves(ocean_at, f * TILES + t)
             first, second = ocean[f, t, 0:8, :], ocean[f, t, 8:16, :]
-            wet = coef[0, t]
+            if wide:
+                far = inbox.right(more_at + 8 * (f * TILES + t))
+                near = joined(near, far)
             if f == 0:
                 first = first + UPLIFT_GAIN * wet[0:8] * spread_left[t : t + 1]
                 near = near + UPLIFT_GAIN * wet[16:24] * spread_last[t : t + 1]
             if wide:
-                far = inbox.right(more_at + at)
                 value = jnp.concatenate([first, second, near, joined(far, top)], axis=0)
             else:
                 value = jnp.concatenate([first, second, joined(near, top)], axis=0)
@@ -395,13 +421,12 @@
                 height[t] = value
             else:
                 flow[0, f - 1, t] = value
-        coef[0, t] = WAVE_STEP * coef[0, t]
     for step in range(NSUB):
         old, new = step % 2, (step + 1) % 2
         for t in range(TILES):
             m, n = flow[old, 0, t], flow[old, 1, t]
             spill = (m - roll(m, 1, 0)) + (n - west(lambda i: flow[old, 1, i], t))
-            height[t] = height[t] - coef[0, t] * spill
+            height[t] = height[t] - coef[0, t] * (WAVE_STEP * spill)
         for t in range(TILES):
             h = height[t]
             ahead = [roll(h, -1, 0), east(lambda i: height[i], t)]
@@ -418,24 +443,29 @@
                 flow[new, d, t] = value
 
 
-def step_kernel(kind, last, is_first, *refs):
-    parity, base_one, base_two = refs[0:3]
-    refs = refs[3:]
-    if is_first:
-        one, two = base_one, base_two
+def step_kernel(last, is_first, edge, *refs):
+    parity, refs = refs[0], list(refs[1:])
+
+    def take(count):
+        taken = refs[:count]
+        del refs[:count]
+        return taken
+
+    base_one, base_two = take(2)
+    one, two = (base_one, base_two) if is_first else take(2)
+    motion, stress, solid, ocean, floor = take(5)
+    ready = not (is_first or last)
+    if ready:
+        (coef,) = take(1)
+    if last:
+        motion_out, stress_out, surface_out, momentum_out = take(4)
     else:
-        one, two = refs[0:2]
-        refs = refs[2:]
-    motion, stress, solid, ocean, floor = refs[0:5]
-    if last:
-        motion_out, stress_out, surface_out, momentum_out = refs[5:9]
-        refs = refs[9:]
-    else:
-        motion_out, stress_out, ocean_out, send_one, send_two = refs[5:10]
-        refs = refs[10:]
-    coef, height, flow, edge, speed = refs
+        motion_out, stress_out, ocean_out, send_one, send_two = take(5)
+    if not ready:
+        (coef,) = take(1)
+    height, flow, speed = take(3)
     slabs = motion.shape[2] // 8
-    part, ocean_at, extra_at, more_at, static_at = offsets(slabs)
+    part, _, extra_at, more_at = offsets(slabs)
     even = parity[0] == 0
     base = Receiver(even, base_one, base_two)
     inbox = Receiver(even, one, two)
@@ -445,12 +475,14 @@
 
     row_left = extra_row(inbox.left)
     loaded = None if is_first else -LOAD_GAIN * extra_row(inbox.right)
-    ocean_part(inbox, base, slabs, motion, ocean, floor, kind, coef, height, flow, row_left)
+    ocean_part(
+        inbox, base, slabs, motion, ocean, floor, last, ready, coef, height, flow, row_left
+    )
     blocks = 3 if last else 2
     sums = [[] for _ in range(blocks)]
     for t in range(TILES):
         h = height[t]
-        wet = (1.0 / WAVE_STEP) * coef[0, t]
+        wet = coef[0, t]
         for b in range(blocks):
             rows = slice(8 * b, 8 * b + 8)
             sums[b].append(jnp.sum(wet[rows] * h[rows], axis=0, keepdims=True))
@@ -532,9 +564,7 @@
         return
     out = Sender(even, send_one, send_two)
     next_kind = "last" if edge else "usual"
-    finish(
-        out, slabs, motion_out, stress_out, solid, ocean_out, floor.at[1], means[0], next_kind
-    )
+    finish(out, slabs, motion_out, stress_out, solid, ocean_out, floor, means[0], next_kind)
 
 
 def swap(size, start):
@@ -569,6 +599,7 @@
             in_specs=specs,
             out_specs=tuple(pl.BlockSpec(memory_space=pltpu.VMEM) for _ in outs),
             scratch_shapes=list(scratch),
+            compiler_params=pltpu.CompilerParams(vmem_limit_bytes=VMEM_LIMIT),
             interpret=INTERPRET,
         )(*args)
 
@@ -593,24 +624,27 @@
         array(rows, LANES),
     )
     motion, stress, solid, ocean, floor, *send = call(start_kernel, outs, (parity, *own, *received))
-    base = None
+    base = coef = None
     for step in range(STEPS):
         received = exchanged(*send, "gx")
-        last = step == STEPS - 1
-        if step == 0:
-            base = received
-            inputs = (parity, *base)
-        else:
-            inputs = (parity, *base, *received)
-        inputs = (*inputs, motion, stress, solid, ocean, floor)
+        first, last, edge = step == 0, step == STEPS - 1, step == STEPS - 2
         height = 32 if last else 24
-        scratch = (
-            pltpu.VMEM((15, TILES, height, LANES), f32),
+        table = (15, TILES, height, LANES)
+        scratch = [
             pltpu.VMEM((TILES, height, LANES), f32),
             pltpu.VMEM((2, 2, TILES, height, LANES), f32),
             pltpu.VMEM((3, 3, depth_cells, 256), f32),
-        )
-        if last:
+        ]
+        rows = payload_rows(slabs, "last" if edge else "usual")
+        outs = (*state, array(3, TILES, 16, LANES), array(rows, LANES), array(rows, LANES))
+        fixed = (motion, stress, solid, ocean, floor)
+        if first:
+            base = received
+            inputs = (parity, *base, *fixed)
+            outs = (*outs, array(*table))
+        elif last:
+            inputs = (parity, *base, *received, *fixed)
+            scratch = [pltpu.VMEM(table, f32), *scratch]
             outs = (
                 array(3, 2, depth_cells, LANES),
                 array(6, 2, depth_cells, LANES),
@@ -618,20 +652,14 @@
                 array(2, 16, 8 * LANES),
             )
         else:
-            rows = payload_rows(slabs, "last" if step == STEPS - 2 else "usual")
-            outs = (*state, array(3, TILES, 16, LANES), array(rows, LANES), array(rows, LANES))
-        kernel = functools.partial(
-            run_step, "last" if last else "usual", last, step == 0, step == STEPS - 2
-        )
+            inputs = (parity, *base, *received, *fixed, coef)
+        kernel = functools.partial(step_kernel, last, first, edge)
         results = call(kernel, outs, inputs, scratch)
+        if first:
+            coef = results[-1]
         if not last:
-            motion, stress, ocean, *send = results
+            motion, stress, ocean, *send = results[:5]
     return results
-
-
-def run_step(kind, last, is_first, edge, *refs):
-    coef, height, flow, speed = refs[-4:]
-    step_kernel(kind, last, is_first, *refs[:-4], coef, height, flow, edge, speed)
 
 
 def solution(mesh):

time: 135 us -> 117 us (0.87)
  Pallas kernels: 34.5 us -> 21.8 us
  waiting for transfers between devices: 70.7 us -> 61.2 us
  local copies, waits for them, and re-layouts: 3.6 us -> 8.12 us
    pallas_call x6, Pallas kernels: 34.5 us -> 21.8 us  [call(): pl.pallas_call(kernel, out_shape=outs, in_specs=specs, out_specs=tuple((p...]
    ppermute x5, waiting for transfers between devices: 18.4 us -> 12.6 us  [exchanged(): lax.ppermute(first, axis, swap(size, 0))]
    unnamed x20 -> x18, local copies, waits for them, and re-layouts: 3.6 us -> 8.12 us
    ppermute x5, waiting for transfers between devices: 52.2 us -> 48.6 us  [exchanged(): lax.ppermute(second, axis, swap(size, 1))]
where the time goes in v2:
time: 117 us
  waiting for transfers between devices  61.2 us (52%)
  starting transfers between devices  24.9 us (21%)
  Pallas kernels  21.8 us (19%)
  local copies, waits for them, and re-layouts  8.12 us (7%)
    ppermute x5, waiting for transfers between devices, exchanged(): lax.ppermute(second, axis, swap(size, 1))  48.6 us
    ppermute x5, starting transfers between devices, exchanged(): lax.ppermute(second, axis, swap(size, 1))  22.8 us
    pallas_call x6, Pallas kernels, call(): pl.pallas_call(kernel, out_shape=outs, in_specs=specs, out_specs=tuple((p...  21.8 us
    ppermute x5, waiting for transfers between devices, exchanged(): lax.ppermute(first, axis, swap(size, 0))  12.6 us
    unnamed x18, local copies, waits for them, and re-layouts  8.12 us
  transfers between devices with their start and end apart: 10, of which 9 were waited for; matrix products, arithmetic and copies ran while one was open for 0% of the time, Pallas kernels for 0%

profile of v2, /device:TPU:192, one launch (start us, length us, event | category | flops | bytes accessed | tf_op | source)
XLA Modules:
  0.0 116.8 jit_solution(670323159209626350)
XLA Ops:
  0.6 0.1 pad_add_fusion.parity.refs_0_
  0.7 0.0 copy-start
  0.7 1.1 copy-done
  1.8 0.0 copy-start.1
  1.8 1.0 copy-done.1
  2.8 0.0 copy-start.2
  2.8 0.9 copy-done.2
  3.7 0.0 copy-start.3
  3.7 0.9 copy-done.3
  4.5 0.0 copy-start.4
  4.5 0.9 copy-done.4
  5.4 0.0 copy-start.5
  5.4 0.9 copy-done.5
  6.3 0.0 copy-start.6
  6.3 0.8 copy-done.6
  7.2 0.0 copy-start.7
  7.2 0.8 copy-done.7
  8.0 0.0 copy-start.8
  8.0 0.8 copy-done.8
  8.9 1.2 %shard_map.120 = (f32[96,128]{1,0:T(8,128)S(1)}, f32[96,128]{1,0:T(8,128)S(1)}) custom-call(s32[2]{0:T(128)S(1)} %pad_add_fusion.parity.refs_0_, f32[3,2,96,128]{3,2,1,0:T(8,128)S(1)} %copy-done.1, f32[6,2,96,128]{3,2,1,0:T(8,128)S(1)} %copy-done, f32[2,96,128]{2,1,0:T(8,128)S(1)} %copy-done.3, f32[2,96,128]{2,1,0:T(8,128)S(1)} %copy-done.4, ...), custom_call_target="tpu_custom_call" | custom-call | tf_op jit(solution)/shard_map/pallas_call | solution.py:596
  10.1 0.1 collective-permute-start
  10.2 3.0 %collective-permute-start.1 = (f32[96,128]{1,0:T(8,128)S(1)}, f32[96,128]{1,0:T(8,128)S(1)}, u32[]{:S(2)}, u32[]{:S(2)}) collective-permute-start(f32[96,128]{1,0:T(8,128)S(1)} %get-tuple-element.30), channel_id=1, source_target_pairs={{1,2},{2,1},{3,4},{4,3},{5,6},{6,5},{9,10},{10,9},{11,12},{12,11},... | collective-permute-start | bytes 147464 | tf_op jit(solution)/shard_map/ppermute | solution.py:581
  13.2 0.0 collective-permute-done.one
  13.2 2.4 %collective-permute-done.1.two = f32[96,128]{1,0:T(8,128)S(1)} collective-permute-done((f32[96,128]{1,0:T(8,128)S(1)}, f32[96,128]{1,0:T(8,128)S(1)}, u32[]{:S(2)}, u32[]{:S(2)}) %collective-permute-start.1) | collective-permute-done | bytes 49184 | tf_op jit(solution)/shard_map/ppermute | solution.py:581
  15.6 2.7 %shard_map.121 = (f32[3,2,96,256]{3,2,1,0:T(8,128)S(1)}, f32[6,2,96,256]{3,2,1,0:T(8,128)S(1)}, f32[3,2,96,256]{3,2,1,0:T(8,128)S(1)}, f32[3,9,16,128]{3,2,1,0:T...) custom-call(s32[2]{0:T(128)S(1)} %pad_add_fusion.parity.refs_0_, ...), custom_call_target="tpu_custom_call" | custom-call | tf_op jit(solution)/shard_map/pallas_call | solution.py:596
  18.3 1.7 %collective-permute-start.2 = (f32[656,128]{1,0:T(8,128)S(1)}, f32[656,128]{1,0:T(8,128)S(1)}, u32[]{:S(2)}, u32[]{:S(2)}) collective-permute-start(f32[656,128]{1,0:T(8,128)S(1)} %get-tuple-element.31), channel_id=1, source_target_pairs={{0,8},{8,0},{16,24},{24,16},{32,40},{40,32},{48,56},{56,48},{64,72... | collective-permute-start | bytes 1007624 | tf_op jit(solution)/shard_map/ppermute | solution.py:580
  19.9 6.3 %collective-permute-start.3 = (f32[656,128]{1,0:T(8,128)S(1)}, f32[656,128]{1,0:T(8,128)S(1)}, u32[]{:S(2)}, u32[]{:S(2)}) collective-permute-start(f32[656,128]{1,0:T(8,128)S(1)} %get-tuple-element.32), channel_id=1, source_target_pairs={{8,16},{16,8},{24,32},{32,24},{40,48},{48,40},{56,64},{64,56},{72,... | collective-permute-start | bytes 1007624 | tf_op jit(solution)/shard_map/ppermute | solution.py:581
  26.2 2.4 %collective-permute-done.2.refs_1_ = f32[656,128]{1,0:T(8,128)S(1)} collective-permute-done((f32[656,128]{1,0:T(8,128)S(1)}, f32[656,128]{1,0:T(8,128)S(1)}, u32[]{:S(2)}, u32[]{:S(2)}) %collective-permute-start.2) | collective-permute-done | bytes 335904 | tf_op jit(solution)/shard_map/ppermute | solution.py:580
  28.6 16.0 %collective-permute-done.3.refs_2_ = f32[656,128]{1,0:T(8,128)S(1)} collective-permute-done((f32[656,128]{1,0:T(8,128)S(1)}, f32[656,128]{1,0:T(8,128)S(1)}, u32[]{:S(2)}, u32[]{:S(2)}) %collective-permute-start.3) | collective-permute-done | bytes 335904 | tf_op jit(solution)/shard_map/ppermute | solution.py:581
  44.6 4.7 %shard_map.122 = (f32[3,2,96,256]{3,2,1,0:T(8,128)S(1)}, f32[6,2,96,256]{3,2,1,0:T(8,128)S(1)}, f32[3,9,16,128]{3,2,1,0:T(8,128)S(1)}, f32[440,128]{1,0:T(8,128)...) custom-call(s32[2]{0:T(128)S(1)} %pad_add_fusion.parity.refs_0_, ...), custom_call_target="tpu_custom_call" | custom-call | tf_op jit(solution)/shard_map/pallas_call | solution.py:596
  49.3 0.1 collective-permute-start.4
  49.4 4.5 %collective-permute-start.5 = (f32[440,128]{1,0:T(8,128)S(1)}, f32[440,128]{1,0:T(8,128)S(1)}, u32[]{:S(2)}, u32[]{:S(2)}) collective-permute-start(f32[440,128]{1,0:T(8,128)S(1)} %get-tuple-element.39), channel_id=1, source_target_pairs={{8,16},{16,8},{24,32},{32,24},{40,48},{48,40},{56,64},{64,56},{72,... | collective-permute-start | bytes 675848 | tf_op jit(solution)/shard_map/ppermute | solution.py:581
  53.9 3.0 %collective-permute-done.4.refs_3_ = f32[440,128]{1,0:T(8,128)S(1)} collective-permute-done((f32[440,128]{1,0:T(8,128)S(1)}, f32[440,128]{1,0:T(8,128)S(1)}, u32[]{:S(2)}, u32[]{:S(2)}) %collective-permute-start.4) | collective-permute-done | bytes 225312 | tf_op jit(solution)/shard_map/ppermute | solution.py:580
  56.8 10.0 %collective-permute-done.5.refs_4_ = f32[440,128]{1,0:T(8,128)S(1)} collective-permute-done((f32[440,128]{1,0:T(8,128)S(1)}, f32[440,128]{1,0:T(8,128)S(1)}, u32[]{:S(2)}, u32[]{:S(2)}) %collective-permute-start.5) | collective-permute-done | bytes 225312 | tf_op jit(solution)/shard_map/ppermute | solution.py:581
  66.9 4.2 %shard_map.123 = (f32[3,2,96,256]{3,2,1,0:T(8,128)S(1)}, f32[6,2,96,256]{3,2,1,0:T(8,128)S(1)}, f32[3,9,16,128]{3,2,1,0:T(8,128)S(1)}, f32[440,128]{1,0:T(8,128)S(1)}, f32[440,128]{1,0:T(8,128)S(1)}) custom-call(s32[2]{0:T(128)S(1)} %pad_add_fusion.parity.refs_0_, f32[656,128]{1,0:T(8,128)S(1)} %collective-permute-done.2.refs_1_, ...), custom_call_target="tpu_custom_call" | custom-call | tf_op jit(solution)/shard_map/pallas_call | solution.py:596
  71.0 0.1 collective-permute-start.6
  71.1 4.6 %collective-permute-start.7 = (f32[440,128]{1,0:T(8,128)S(1)}, f32[440,128]{1,0:T(8,128)S(1)}, u32[]{:S(2)}, u32[]{:S(2)}) collective-permute-start(f32[440,128]{1,0:T(8,128)S(1)} %get-tuple-element.45), channel_id=1, source_target_pairs={{8,16},{16,8},{24,32},{32,24},{40,48},{48,40},{56,64},{64,56},{72,... | collective-permute-start | bytes 675848 | tf_op jit(solution)/shard_map/ppermute | solution.py:581
  75.8 1.9 %collective-permute-done.6.refs_3_ = f32[440,128]{1,0:T(8,128)S(1)} collective-permute-done((f32[440,128]{1,0:T(8,128)S(1)}, f32[440,128]{1,0:T(8,128)S(1)}, u32[]{:S(2)}, u32[]{:S(2)}) %collective-permute-start.6) | collective-permute-done | bytes 225312 | tf_op jit(solution)/shard_map/ppermute | solution.py:580
  77.7 10.0 %collective-permute-done.7.refs_4_ = f32[440,128]{1,0:T(8,128)S(1)} collective-permute-done((f32[440,128]{1,0:T(8,128)S(1)}, f32[440,128]{1,0:T(8,128)S(1)}, u32[]{:S(2)}, u32[]{:S(2)}) %collective-permute-start.7) | collective-permute-done | bytes 225312 | tf_op jit(solution)/shard_map/ppermute | solution.py:581
  87.8 4.1 %shard_map.124 = (f32[3,2,96,256]{3,2,1,0:T(8,128)S(1)}, f32[6,2,96,256]{3,2,1,0:T(8,128)S(1)}, f32[3,9,16,128]{3,2,1,0:T(8,128)S(1)}, f32[800,128]{1,0:T(8,128)S(1)}, f32[800,128]{1,0:T(8,128)S(1)}) custom-call(s32[2]{0:T(128)S(1)} %pad_add_fusion.parity.refs_0_, f32[656,128]{1,0:T(8,128)S(1)} %collective-permute-done.2.refs_1_, ...), custom_call_target="tpu_custom_call" | custom-call | tf_op jit(solution)/shard_map/pallas_call | solution.py:596
  91.9 0.1 collective-permute-start.8
  92.0 4.5 %collective-permute-start.9 = (f32[800,128]{1,0:T(8,128)S(1)}, f32[800,128]{1,0:T(8,128)S(1)}, u32[]{:S(2)}, u32[]{:S(2)}) collective-permute-start(f32[800,128]{1,0:T(8,128)S(1)} %get-tuple-element.50), channel_id=1, source_target_pairs={{8,16},{16,8},{24,32},{32,24},{40,48},{48,40},{56,64},{64,56},{72,... | collective-permute-start | bytes 1228808 | tf_op jit(solution)/shard_map/ppermute | solution.py:581
  96.5 5.2 %collective-permute-done.8.refs_3_ = f32[800,128]{1,0:T(8,128)S(1)} collective-permute-done((f32[800,128]{1,0:T(8,128)S(1)}, f32[800,128]{1,0:T(8,128)S(1)}, u32[]{:S(2)}, u32[]{:S(2)}) %collective-permute-start.8) | collective-permute-done | bytes 409632 | tf_op jit(solution)/shard_map/ppermute | solution.py:580
  101.7 10.2 %collective-permute-done.9.refs_4_ = f32[800,128]{1,0:T(8,128)S(1)} collective-permute-done((f32[800,128]{1,0:T(8,128)S(1)}, f32[800,128]{1,0:T(8,128)S(1)}, u32[]{:S(2)}, u32[]{:S(2)}) %collective-permute-start.9) | collective-permute-done | bytes 409632 | tf_op jit(solution)/shard_map/ppermute | solution.py:581
  111.9 4.9 %shard_map.125 = (f32[3,2,96,128]{3,2,1,0:T(8,128)}, f32[6,2,96,128]{3,2,1,0:T(8,128)}, f32[16,1024]{1,0:T(8,128)}, f32[2,16,1024]{2,1,0:T(8,128)}) custom-call(s32[2]{0:T(128)S(1)} %pad_add_fusion.parity.refs_0_, f32[656,128]{1,0:T(8,128)S(1)} %collective-permute-done.2.refs_1_, f32[656,128]{1,0:T(8,128)S(1)} %collective-permute-done.3.refs_2_, ...), custom_call_target="tpu_custom_call" | custom-call | tf_op jit(solution)/shard_map/pallas_call | solution.py:596
Async XLA Ops:
  0.7 1.1 copy-start
  1.8 1.0 copy-start.1
  2.8 0.9 copy-start.2
  3.7 0.9 copy-start.3
  4.5 0.9 copy-start.4
  5.4 0.9 copy-start.5
  6.3 0.8 copy-start.6
  7.2 0.8 copy-start.7
  8.0 0.8 copy-start.8
  10.1 3.1 %collective-permute-start = (f32[96,128]{1,0:T(8,128)S(1)}, f32[96,128]{1,0:T(8,128)S(1)}, u32[]{:S(2)}, u32[]{:S(2)}) collective-permute-start(f32[96,128]{1,0:T(8,128)S(1)} %get-tuple-element.29), channel_id=1, source_target_pairs={{0,1},{1,0},{2,3},{3,2},{4,5},{5,4},{6,7},{7,6},{8,9},{9,8},{10,11... | collective-permute-start | bytes 147464 | tf_op jit(solution)/shard_map/ppermute | solution.py:580
  10.2 5.4 %collective-permute-start.1 = (f32[96,128]{1,0:T(8,128)S(1)}, f32[96,128]{1,0:T(8,128)S(1)}, u32[]{:S(2)}, u32[]{:S(2)}) collective-permute-start(f32[96,128]{1,0:T(8,128)S(1)} %get-tuple-element.30), channel_id=1, source_target_pairs={{1,2},{2,1},{3,4},{4,3},{5,6},{6,5},{9,10},{10,9},{11,12},{12,11},... | collective-permute-start | bytes 147464 | tf_op jit(solution)/shard_map/ppermute | solution.py:581
  18.3 10.4 %collective-permute-start.2 = (f32[656,128]{1,0:T(8,128)S(1)}, f32[656,128]{1,0:T(8,128)S(1)}, u32[]{:S(2)}, u32[]{:S(2)}) collective-permute-start(f32[656,128]{1,0:T(8,128)S(1)} %get-tuple-element.31), channel_id=1, source_target_pairs={{0,8},{8,0},{16,24},{24,16},{32,40},{40,32},{48,56},{56,48},{64,72... | collective-permute-start | bytes 1007624 | tf_op jit(solution)/shard_map/ppermute | solution.py:580
  19.9 24.7 %collective-permute-start.3 = (f32[656,128]{1,0:T(8,128)S(1)}, f32[656,128]{1,0:T(8,128)S(1)}, u32[]{:S(2)}, u32[]{:S(2)}) collective-permute-start(f32[656,128]{1,0:T(8,128)S(1)} %get-tuple-element.32), channel_id=1, source_target_pairs={{8,16},{16,8},{24,32},{32,24},{40,48},{48,40},{56,64},{64,56},{72,... | collective-permute-start | bytes 1007624 | tf_op jit(solution)/shard_map/ppermute | solution.py:581
  49.3 7.6 %collective-permute-start.4 = (f32[440,128]{1,0:T(8,128)S(1)}, f32[440,128]{1,0:T(8,128)S(1)}, u32[]{:S(2)}, u32[]{:S(2)}) collective-permute-start(f32[440,128]{1,0:T(8,128)S(1)} %get-tuple-element.38), channel_id=1, source_target_pairs={{0,8},{8,0},{16,24},{24,16},{32,40},{40,32},{48,56},{56,48},{64,72... | collective-permute-start | bytes 675848 | tf_op jit(solution)/shard_map/ppermute | solution.py:580
  49.4 17.5 %collective-permute-start.5 = (f32[440,128]{1,0:T(8,128)S(1)}, f32[440,128]{1,0:T(8,128)S(1)}, u32[]{:S(2)}, u32[]{:S(2)}) collective-permute-start(f32[440,128]{1,0:T(8,128)S(1)} %get-tuple-element.39), channel_id=1, source_target_pairs={{8,16},{16,8},{24,32},{32,24},{40,48},{48,40},{56,64},{64,56},{72,... | collective-permute-start | bytes 675848 | tf_op jit(solution)/shard_map/ppermute | solution.py:581
  71.0 6.7 %collective-permute-start.6 = (f32[440,128]{1,0:T(8,128)S(1)}, f32[440,128]{1,0:T(8,128)S(1)}, u32[]{:S(2)}, u32[]{:S(2)}) collective-permute-start(f32[440,128]{1,0:T(8,128)S(1)} %get-tuple-element.44), channel_id=1, source_target_pairs={{0,8},{8,0},{16,24},{24,16},{32,40},{40,32},{48,56},{56,48},{64,72... | collective-permute-start | bytes 675848 | tf_op jit(solution)/shard_map/ppermute | solution.py:580
  71.1 16.6 %collective-permute-start.7 = (f32[440,128]{1,0:T(8,128)S(1)}, f32[440,128]{1,0:T(8,128)S(1)}, u32[]{:S(2)}, u32[]{:S(2)}) collective-permute-start(f32[440,128]{1,0:T(8,128)S(1)} %get-tuple-element.45), channel_id=1, source_target_pairs={{8,16},{16,8},{24,32},{32,24},{40,48},{48,40},{56,64},{64,56},{72,... | collective-permute-start | bytes 675848 | tf_op jit(solution)/shard_map/ppermute | solution.py:581
  91.9 9.8 %collective-permute-start.8 = (f32[800,128]{1,0:T(8,128)S(1)}, f32[800,128]{1,0:T(8,128)S(1)}, u32[]{:S(2)}, u32[]{:S(2)}) collective-permute-start(f32[800,128]{1,0:T(8,128)S(1)} %get-tuple-element.49), channel_id=1, source_target_pairs={{0,8},{8,0},{16,24},{24,16},{32,40},{40,32},{48,56},{56,48},{64,72... | collective-permute-start | bytes 1228808 | tf_op jit(solution)/shard_map/ppermute | solution.py:580
  92.0 19.9 %collective-permute-start.9 = (f32[800,128]{1,0:T(8,128)S(1)}, f32[800,128]{1,0:T(8,128)S(1)}, u32[]{:S(2)}, u32[]{:S(2)}) collective-permute-start(f32[800,128]{1,0:T(8,128)S(1)} %get-tuple-element.50), channel_id=1, source_target_pairs={{8,16},{16,8},{24,32},{32,24},{40,48},{48,40},{56,64},{64,56},{72,... | collective-permute-start | bytes 1228808 | tf_op jit(solution)/shard_map/ppermute | solution.py:581

commit v3 on v2

--- a/solution.py
+++ b/solution.py
@@ -202,10 +202,18 @@
         force = xz(k) + (mid - prev_lane(mid)) + (above(zz, k, slabs) - zz(k))
         return get(motion, 2, 0)(k) + rate(0, k) * force
 
-    out.put_solid(0, slabs, sum_x, sum_y)
-    out.put_solid(part, slabs, get(stress, 3, 1), sum_z)
+    def kept(compute, field, row):
+        def get_and_keep(k):
+            value = compute(k)
+            motion[field, row, 8 * k : 8 * k + 8, :] = value
+            return value
+
+        return get_and_keep
+
+    (spread,) = upsampled([motion[2, 0, 0:1, :]])
+    out.put_solid(0, slabs, kept(sum_x, 0, 1), kept(sum_y, 1, 0))
+    out.put_solid(part, slabs, get(stress, 3, 1), kept(sum_z, 2, 0))
     out.put_solid(2 * part, slabs, get(stress, 4, 1), get(stress, 0, 0))
-    (spread,) = upsampled([motion[2, 0, 0:1, :]])
     for t in range(TILES):
         ocean[0, t, 8:16, :] = (
             ocean[0, t, 8:16, :] + UPLIFT_GAIN * floor[1, t, 8:16, :] * spread[t : t + 1]
@@ -236,21 +244,35 @@
 
 
 def pack_y_kernel(
-    parity, motion, stress, buoyancy, first, shear, surface, momentum, depth, wet, one, two
+    parity, motion, stress, buoyancy, first, shear, surface, momentum, depth, wet,
+    motion_out, stress_out, solid_out, ocean_out, floor_out, one, two,
+    surface_in, momentum_in, depth_in, wet_in, semaphores,
 ):
-    even = parity[1] == 0
-    out = Sender(even, one, two)
+    own = slice(0, LANES)
+    pairs = [(motion, motion_out.at[:, :, :, own]), (stress, stress_out.at[:, :, :, own])]
+    for f, ref in enumerate((buoyancy, first, shear)):
+        pairs.append((ref, solid_out.at[f, :, :, own]))
+    pairs += [(surface, surface_in), (momentum, momentum_in), (depth, depth_in), (wet, wet_in)]
+    copies = [
+        pltpu.make_async_copy(source, target, semaphores.at[i])
+        for i, (source, target) in enumerate(pairs)
+    ]
+    for copy in copies:
+        copy.start()
+    out = Sender(parity[1] == 0, one, two)
     slabs = motion.shape[2] // 8
     lane = iota((8, LANES), 1)
-    fields = [(motion, f) for f in range(3)] + [(stress, f) for f in range(6)]
-    fields += [(buoyancy, None), (first, None), (shear, None)]
-    count, at = 0, 0
+    fields = [(motion_out, f, 0) for f in range(3)] + [(stress_out, f, 1) for f in range(6)]
+    fields += [(solid_out, f, 2 + f) for f in range(3)]
+    count, at, waited = 0, 0, set()
     right = left = jnp.zeros((8, LANES), jnp.float32)
-    for ref, f in fields:
+    for ref, f, copy in fields:
+        if copy not in waited:
+            copies[copy].wait()
+            waited.add(copy)
         for row in range(2):
             for k in range(slabs):
-                z = slice(8 * k, 8 * k + 8)
-                value = ref[row, z, :] if f is None else ref[f, row, z, :]
+                value = ref[f, row, 8 * k : 8 * k + 8, own]
                 here = lane >> 2 == count
                 right = jnp.where(here, roll(value, 4 * count + 4, 1), right)
                 left = jnp.where(here, roll(value, 4 * count, 1), left)
@@ -261,17 +283,22 @@
     if count:
         out.put(at, right, left)
         count, at = 0, at + 8
-    width = surface.shape[1]
-    for ref, f in ((surface, None), (momentum, 0), (momentum, 1), (depth, None), (wet, None)):
+    for copy in copies[5:]:
+        copy.wait()
+    targets = [ocean_out.at[f] for f in range(3)] + [floor_out.at[f] for f in range(2)]
+    sources = [surface_in, momentum_in.at[0], momentum_in.at[1], depth_in, wet_in]
+    for target, source in zip(targets, sources):
         for group in range(2):
             rows = slice(8 * group, 8 * group + 8)
-            ends = []
-            for lanes in (slice(0, LANES), slice(width - LANES, width)):
-                value = ref[rows, lanes] if f is None else ref[f, rows, lanes]
-                ends.append(value.astype(jnp.float32))
-            here = lane >> 5 == count
-            right = jnp.where(here, roll(ends[1], 32 * count + 32, 1), right)
-            left = jnp.where(here, roll(ends[0], 32 * count, 1), left)
+            for t in range(TILES - 1):
+                lanes = slice(LANES * t, LANES * t + LANES)
+                value = source[rows, lanes].astype(jnp.float32)
+                target[t, rows, :] = value
+                here = lane >> 5 == count
+                if t == 0:
+                    left = jnp.where(here, roll(value, 32 * count, 1), left)
+                if t == TILES - 2:
+                    right = jnp.where(here, roll(value, 32 * count + 32, 1), right)
             count += 1
             if count == 4:
                 out.put(at, right, left)
@@ -285,162 +312,179 @@
 
 
 def start_kernel(
-    parity, motion, stress, buoyancy, first, shear, surface, momentum, depth, wet, one, two,
-    motion_out, stress_out, solid_out, ocean_out, floor_out, send_one, send_two,
+    parity, motion_in, stress_in, solid_in, ocean_in, floor_in, one, two,
+    motion, stress, solid, ocean, floor, send_one, send_two,
 ):
     inbox = Receiver(parity[1] == 0, one, two)
     slabs = motion.shape[2] // 8
     lane = iota((8, LANES), 1)
-    fields = [(motion, f, motion_out, f) for f in range(3)]
-    fields += [(stress, f, stress_out, f) for f in range(6)]
-    fields += [(ref, None, solid_out, f) for f, ref in enumerate((buoyancy, first, shear))]
+    fields = [(motion, f) for f in range(3)] + [(stress, f) for f in range(6)]
+    fields += [(solid, f) for f in range(3)]
     count, at = 0, 0
-    for ref, f, target, g in fields:
+    for ref, f in fields:
         for row in range(2):
             for k in range(slabs):
-                z = slice(8 * k, 8 * k + 8)
-                value = ref[row, z, :] if f is None else ref[f, row, z, :]
                 if count == 0:
                     packed = inbox.right(at), inbox.left(at)
                 after = roll(packed[0], -4 * count, 1)
                 before = roll(packed[1], 124 - 4 * count, 1)
                 halo = jnp.where(lane < 4, after, jnp.where(lane >= 124, before, 0.0))
-                target[g, row, z, 0:LANES] = value
-                target[g, row, z, LANES : 2 * LANES] = halo
+                ref[f, row, 8 * k : 8 * k + 8, LANES : 2 * LANES] = halo
                 count += 1
                 if count == 32:
                     count, at = 0, at + 8
     if count:
         count, at = 0, at + 8
-    targets = ((surface, None), (momentum, 0), (momentum, 1), (depth, None), (wet, None))
-    for i, (ref, f) in enumerate(targets):
+    for ref, f in [(ocean, 0), (ocean, 1), (ocean, 2), (floor, 0), (floor, 1)]:
         for group in range(2):
-            rows = slice(8 * group, 8 * group + 8)
             if count == 0:
                 packed = inbox.right(at), inbox.left(at)
             after = roll(packed[0], -32 * count, 1)
             before = roll(packed[1], 96 - 32 * count, 1)
             halo = jnp.where(lane < 32, after, jnp.where(lane >= 96, before, 0.0))
-            for t in range(TILES):
-                if t == TILES - 1:
-                    value = halo
-                else:
-                    lanes = slice(LANES * t, LANES * t + LANES)
-                    value = ref[rows, lanes] if f is None else ref[f, rows, lanes]
-                    value = value.astype(jnp.float32)
-                if i < 3:
-                    ocean_out[i, t, rows, :] = value
-                else:
-                    floor_out[i - 3, t, rows, :] = value
+            ref[f, TILES - 1, 8 * group : 8 * group + 8, :] = halo
             count += 1
             if count == 4:
                 count, at = 0, at + 8
     out = Sender(parity[0] == 0, send_one, send_two)
-    finish(out, slabs, motion_out, stress_out, solid_out, ocean_out, floor_out, None, "first")
-
-
-def coefficients(floor_tile, after, coef, east, west):
+    finish(out, slabs, motion, stress, solid, ocean, floor, None, "first")
+
+
+PAD = 8
+
+
+class Shifts:
+    def __init__(self, tile, by):
+        self.tile, self.by, self.rolled = tile, by, {}
+
+    def rotated(self, t):
+        if t not in self.rolled:
+            self.rolled[t] = roll(self.tile(t), self.by, 1)
+        return self.rolled[t]
+
+    def at(self, t):
+        lane = iota((8, LANES), 1)
+        other, mine = self.rotated((t - self.by) % TILES), self.rotated(t)
+        return jnp.where(lane == (0 if self.by > 0 else LANES - 1), other, mine)
+
+
+def coefficients(coef, face, depth, after):
+    groups = coef.shape[2] // 8
     for t in range(TILES):
-        wet = floor_tile(1, t)
-        coef[0, t] = wet
-        face = wet * roll(wet, -1, 0)
-        if after is not None:
-            low = iota((8, LANES), 0) < 4
-            face = jnp.concatenate([face[0:16], jnp.where(low, after(t), face[16:24])], axis=0)
-        coef[1, t] = face
-        coef[7, t] = floor_tile(0, t)
-    for t in range(TILES):
-        coef[8, t] = coef[0, t] * east(lambda i: coef[0, i], t)
-    for t in range(TILES):
-        for at in (1, 8):
-            face = coef[at, t]
-            near = [roll(face, -1, 0), roll(face, 1, 0)]
-            tile = functools.partial(lambda at, i: coef[at, i], at)
-            near += [east(tile, t), west(tile, t)]
-            total = near[0] + near[1] + near[2] + near[3]
-            for j in range(4):
-                coef[at + 1 + j, t] = VISCOSITY * face * near[j]
-            coef[at + 5, t] = face - VISCOSITY * face * total
-        coef[14, t] = coef[7, t] + east(lambda i: coef[7, i], t)
-    for t in range(TILES):
-        depth = coef[7, t]
-        coef[7, t] = depth + roll(depth, -1, 0)
-        coef[1, t] = WAVE_STEP * 0.5 * coef[1, t]
-        coef[8, t] = WAVE_STEP * 0.5 * coef[8, t]
+        for g in range(groups):
+            at = PAD + 8 * g
+            wet = face[0, t, at : at + 8, :]
+            coef[7, t, 8 * g : 8 * g + 8, :] = wet
+            coef[0, t, 8 * g : 8 * g + 8, :] = WAVE_STEP * wet
+    for direction in range(2):
+        for g in range(groups):
+            at = PAD + 8 * g
+            wets = Shifts(lambda t: coef[7, t, 8 * g : 8 * g + 8, :], -1)
+            depths = Shifts(lambda t: depth[t, at : at + 8, :], -1)
+            for t in range(TILES):
+                wet = wets.tile(t)
+                here = depths.tile(t)
+                if direction == 0:
+                    beside = face[0, t, at + 1 : at + 9, :]
+                    deep = depth[t, at + 1 : at + 9, :]
+                else:
+                    beside, deep = wets.at(t), depths.at(t)
+                face[1, t, at : at + 8, :] = wet * beside
+                coef[3 + 3 * direction, t, 8 * g : 8 * g + 8, :] = here + deep
+        if direction == 0 and after is not None:
+            for t in range(TILES):
+                face[1, t, PAD + 20 : PAD + 28, :] = after(t)
+        for g in range(groups):
+            at = PAD + 8 * g
+            ahead = Shifts(lambda t: face[1, t, at : at + 8, :], -1)
+            behind = Shifts(ahead.tile, 1)
+            for t in range(TILES):
+                own = ahead.tile(t)
+                total = face[1, t, at - 1 : at + 7, :] + face[1, t, at + 1 : at + 9, :]
+                total = total + ahead.at(t) + behind.at(t)
+                rows = slice(8 * g, 8 * g + 8)
+                coef[1 + 3 * direction, t, rows, :] = VISCOSITY * own
+                coef[2 + 3 * direction, t, rows, :] = own - VISCOSITY * own * total
 
 
 def ocean_part(
-    inbox, base, slabs, motion, ocean, floor, wide, ready, coef, height, flow, row_left
+    inbox, base, slabs, motion, ocean, floor, wide, first, coef, height, flow, side, row_left
 ):
     part, ocean_at, _, more_at = offsets(slabs)
     low = iota((8, LANES), 0) < 4
-
-    def joined(upper, lower):
-        return jnp.where(low, upper, lower)
-
-    def floor_tile(f, t):
-        near, top = base.halves(more_at + part, f * TILES + t)
-        own = floor[f, t, :, :]
+    groups = 4 if wide else 3
+
+    def place(target, t, own, near, top, far):
+        target[t, PAD - 4 : PAD + 4, :] = top
+        target[t, PAD + 4 : PAD + 20, :] = own
         if wide:
-            far = inbox.right(more_at + 8 * (UNITS + f * TILES + t))
-            return jnp.concatenate([own, joined(near, far), joined(far, top)], axis=0)
-        return jnp.concatenate([own, joined(near, top)], axis=0)
-
-    lane0 = lambda rows: iota((rows, LANES), 1) == 0
-    lane127 = lambda rows: iota((rows, LANES), 1) == LANES - 1
-
-    def west(tile, t):
-        mine, other = roll(tile(t), 1, 1), roll(tile((t - 1) % TILES), 1, 1)
-        return jnp.where(lane0(mine.shape[0]), other, mine)
-
-    def east(tile, t):
-        mine, other = roll(tile(t), -1, 1), roll(tile((t + 1) % TILES), -1, 1)
-        return jnp.where(lane127(mine.shape[0]), other, mine)
-
-    if not ready:
+            near = jnp.where(low, near, far)
+            target[t, PAD + 28 : PAD + 36, :] = far
+        target[t, PAD + 20 : PAD + 28, :] = near
+
+    if first or wide:
+        for t in range(TILES):
+            for f, target in ((1, flow.at[0, 0]), (0, height)):
+                near, top = base.halves(more_at + part, f * TILES + t)
+                far = inbox.right(more_at + 8 * (UNITS + f * TILES + t)) if wide else None
+                place(target, t, floor[f, t, :, :], near, top, far)
         after = lambda t: base.halves(more_at + part, 2 * TILES + t)[0]
-        coefficients(floor_tile, None if wide else after, coef, east, west)
-    own_last = motion[2, 1, 0:1, :]
-    spread_left, spread_last = upsampled([row_left, own_last])
+        coefficients(coef, flow.at[0], height, None if wide else after)
+    spread_left, spread_last = upsampled([row_left, motion[2, 1, 0:1, :]])
     for t in range(TILES):
-        wet = coef[0, t]
         for f in range(3):
             near, top = inbox.halves(ocean_at, f * TILES + t)
-            first, second = ocean[f, t, 0:8, :], ocean[f, t, 8:16, :]
-            if wide:
-                far = inbox.right(more_at + 8 * (f * TILES + t))
-                near = joined(near, far)
-            if f == 0:
-                first = first + UPLIFT_GAIN * wet[0:8] * spread_left[t : t + 1]
-                near = near + UPLIFT_GAIN * wet[16:24] * spread_last[t : t + 1]
-            if wide:
-                value = jnp.concatenate([first, second, near, joined(far, top)], axis=0)
-            else:
-                value = jnp.concatenate([first, second, joined(near, top)], axis=0)
-            if f == 0:
-                height[t] = value
-            else:
-                flow[0, f - 1, t] = value
+            far = inbox.right(more_at + 8 * (f * TILES + t)) if wide else None
+            target = height if f == 0 else flow.at[0, f - 1]
+            place(target, t, ocean[f, t, :, :], near, top, far)
+        for g in range(groups):
+            spread = spread_left if g < 2 else spread_last
+            lift = UPLIFT_GAIN * coef[7, t, 8 * g : 8 * g + 8, :] * spread[t : t + 1]
+            lift = jnp.where(low == (g % 2 == 1), lift, 0.0)
+            at = PAD + 8 * g
+            height[t, at : at + 8, :] = height[t, at : at + 8, :] + lift
     for step in range(NSUB):
         old, new = step % 2, (step + 1) % 2
-        for t in range(TILES):
-            m, n = flow[old, 0, t], flow[old, 1, t]
-            spill = (m - roll(m, 1, 0)) + (n - west(lambda i: flow[old, 1, i], t))
-            height[t] = height[t] - coef[0, t] * (WAVE_STEP * spill)
-        for t in range(TILES):
-            h = height[t]
-            ahead = [roll(h, -1, 0), east(lambda i: height[i], t)]
-            for d in range(2):
-                at = 1 + 7 * d
-                tile = functools.partial(lambda d, i: flow[old, d, i], d)
-                q = flow[old, d, t]
-                slope = (coef[at + 6, t] + h + ahead[d]) * (ahead[d] - h)
-                value = coef[at + 5, t] * q - coef[at, t] * slope
-                value = value + coef[at + 1, t] * roll(q, -1, 0)
-                value = value + coef[at + 2, t] * roll(q, 1, 0)
-                value = value + coef[at + 3, t] * east(tile, t)
-                value = value + coef[at + 4, t] * west(tile, t)
-                flow[new, d, t] = value
+        for g in range(groups):
+            at, rows = PAD + 8 * g, slice(8 * g, 8 * g + 8)
+            n_behind = Shifts(lambda t: flow[old, 1, t, at : at + 8, :], 1)
+            for t in range(TILES):
+                m, n = flow[old, 0, t, at : at + 8, :], n_behind.tile(t)
+                west = n_behind.at(t)
+                if not (first and step == 0):
+                    side[t, rows, :] = west
+                spill = (m - flow[old, 0, t, at - 1 : at + 7, :]) + (n - west)
+                height[t, at : at + 8, :] = height[t, at : at + 8, :] - coef[0, t, rows, :] * spill
+        if first and step == 0:
+            for t in range(TILES):
+                for g in range(groups):
+                    at, rows = PAD + 8 * g, slice(8 * g, 8 * g + 8)
+                    for d in range(2):
+                        wet = jnp.where(coef[1 + 3 * d, t, rows, :] > 0.0, 1.0, 0.0)
+                        flow[old, d, t, at : at + 8, :] = wet * flow[old, d, t, at : at + 8, :]
+        for g in range(groups):
+            at, rows = PAD + 8 * g, slice(8 * g, 8 * g + 8)
+            h_ahead = Shifts(lambda t: height[t, at : at + 8, :], -1)
+            ahead = [Shifts(lambda t, d=d: flow[old, d, t, at : at + 8, :], -1) for d in range(2)]
+            m_behind = Shifts(ahead[0].tile, 1)
+            n_behind = Shifts(ahead[1].tile, 1)
+            for t in range(TILES):
+                h = height[t, at : at + 8, :]
+                sides = [height[t, at + 1 : at + 9, :], h_ahead.at(t)]
+                for d in range(2):
+                    q = flow[old, d, t, at : at + 8, :]
+                    around = flow[old, d, t, at - 1 : at + 7, :] + flow[old, d, t, at + 1 : at + 9, :]
+                    around = around + ahead[d].at(t)
+                    if d == 0:
+                        around = around + m_behind.at(t)
+                    elif first and step == 0:
+                        around = around + n_behind.at(t)
+                    else:
+                        around = around + side[t, rows, :]
+                    c = 1 + 3 * d
+                    slope = (coef[c + 2, t, rows, :] + h + sides[d]) * (sides[d] - h)
+                    value = coef[c + 1, t, rows, :] * q + coef[c, t, rows, :] * (around - slope)
+                    flow[new, d, t, at : at + 8, :] = value
 
 
 def step_kernel(last, is_first, edge, *refs):
@@ -463,7 +507,7 @@
         motion_out, stress_out, ocean_out, send_one, send_two = take(5)
     if not ready:
         (coef,) = take(1)
-    height, flow, speed = take(3)
+    height, flow, side, speed = take(4)
     slabs = motion.shape[2] // 8
     part, _, extra_at, more_at = offsets(slabs)
     even = parity[0] == 0
@@ -476,26 +520,27 @@
     row_left = extra_row(inbox.left)
     loaded = None if is_first else -LOAD_GAIN * extra_row(inbox.right)
     ocean_part(
-        inbox, base, slabs, motion, ocean, floor, last, ready, coef, height, flow, row_left
+        inbox, base, slabs, motion, ocean, floor, last, is_first, coef, height, flow, side, row_left
     )
     blocks = 3 if last else 2
     sums = [[] for _ in range(blocks)]
+    rows = slice(PAD + 4, PAD + 20)
     for t in range(TILES):
-        h = height[t]
-        wet = coef[0, t]
         for b in range(blocks):
-            rows = slice(8 * b, 8 * b + 8)
-            sums[b].append(jnp.sum(wet[rows] * h[rows], axis=0, keepdims=True))
+            at = 8 * b + 4
+            wet = coef[7, t, at : at + 8, :]
+            h = height[t, PAD + at : PAD + at + 8, :]
+            sums[b].append(jnp.sum(wet * h, axis=0, keepdims=True))
         if last:
             if t < TILES - 1:
                 lanes = slice(LANES * t, LANES * t + LANES)
-                surface_out[:, lanes] = h[0:16]
+                surface_out[:, lanes] = height[t, rows, :]
                 for d in range(2):
-                    momentum_out[d, :, lanes] = flow[NSUB % 2, d, t, 0:16, :]
+                    momentum_out[d, :, lanes] = flow[NSUB % 2, d, t, rows, :]
         else:
-            ocean_out[0, t] = h[0:16]
+            ocean_out[0, t] = height[t, rows, :]
             for d in range(2):
-                ocean_out[1 + d, t] = flow[NSUB % 2, d, t, 0:16, :]
+                ocean_out[1 + d, t] = flow[NSUB % 2, d, t, rows, :]
     means = block_means(sums)
 
     def old(f, row):
@@ -520,22 +565,20 @@
         speed[0, 2, z, :] = inbox.solid(-1, 0, k, slabs) + rate_left * xx[0]
         speed[1, 2, z, :] = inbox.solid(1, 0, k, slabs) - rate_right * xy[2]
         speed[2, 2, z, :] = inbox.solid(1, part, k, slabs) - rate_right * xz[2]
-        for row in range(2):
-            rate = SOLID_STEP * solid[0, row, z, :]
-            yy, zz, yz = stress[1, row, z, :], old(2, row)(k), stress[5, row, z, :]
-            mid_xy, mid_xz = xy[row + 1], xz[row + 1]
-            force_x = (xx[row + 1] - xx[row]) + (mid_xy - prev_lane(mid_xy))
-            force_x = force_x + (mid_xz - below(old(4, row), k))
-            force_y = (mid_xy - xy[row]) + (next_lane(yy) - yy) + (yz - below(old(5, row), k))
-            force_z = (mid_xz - xz[row]) + (yz - prev_lane(yz))
-            force_z = force_z + (above(old(2, row), k, slabs) - zz)
-            for f, force in enumerate((force_x, force_y, force_z)):
-                value = motion[f, row, z, :] + rate * force
-                speed[f, row, z, :] = value
-                if last:
-                    motion_out[f, row, z, :] = value[:, :LANES]
-                else:
-                    motion_out[f, row, z, :] = value
+        rates = [SOLID_STEP * solid[0, row, z, :] for row in range(2)]
+        whole_x = (xx[1] - xx[0]) + (xy[1] - prev_lane(xy[1])) + (xz[1] - below(old(4, 0), k))
+        yy, zz, yz = stress[1, 1, z, :], old(2, 1), stress[5, 1, z, :]
+        whole_y = (xy[2] - xy[1]) + (next_lane(yy) - yy) + (yz - below(old(5, 1), k))
+        whole_z = (xz[2] - xz[1]) + (yz - prev_lane(yz)) + (above(zz, k, slabs) - zz(k))
+        forces = {
+            (0, 0): whole_x, (0, 1): xx[2],
+            (1, 0): -xy[0], (1, 1): whole_y,
+            (2, 0): -xz[0], (2, 1): whole_z,
+        }
+        for (f, row), force in forces.items():
+            value = motion[f, row, z, :] + rates[row] * force
+            speed[f, row, z, :] = value
+            motion_out[f, row, z, :] = value[:, :LANES] if last else value
     width = LANES if last else 2 * LANES
     for k in range(slabs):
         z = slice(8 * k, 8 * k + 8)
@@ -590,15 +633,16 @@
     def array(*shape):
         return jax.ShapeDtypeStruct(shape, f32)
 
-    def call(kernel, outs, args, scratch=()):
+    def call(kernel, outs, args, scratch=(), space=pltpu.VMEM, aliases=None):
         specs = [pl.BlockSpec(memory_space=pltpu.SMEM)]
-        specs += [pl.BlockSpec(memory_space=pltpu.VMEM)] * (len(args) - 1)
+        specs += [pl.BlockSpec(memory_space=space)] * (len(args) - 1)
         return pl.pallas_call(
             kernel,
             out_shape=outs,
             in_specs=specs,
             out_specs=tuple(pl.BlockSpec(memory_space=pltpu.VMEM) for _ in outs),
             scratch_shapes=list(scratch),
+            input_output_aliases=aliases or {},
             compiler_params=pltpu.CompilerParams(vmem_limit_bytes=VMEM_LIMIT),
             interpret=INTERPRET,
         )(*args)
@@ -607,32 +651,33 @@
     own = (
         motion, stress, buoyancy, lame_first, lame_shear, surface, momentum, bathymetry, wet_mask,
     )
-    rows = pack_y_rows(slabs)
-    send = call(pack_y_kernel, (array(rows, LANES),) * 2, (parity, *own))
-    received = exchanged(*send, "gy")
-    state = (
-        array(3, 2, depth_cells, 256),
-        array(6, 2, depth_cells, 256),
-    )
-    rows = payload_rows(slabs, "first")
-    outs = (
+    state = (array(3, 2, depth_cells, 256), array(6, 2, depth_cells, 256))
+    wide = (
         *state,
         array(3, 2, depth_cells, 256),
         array(3, TILES, 16, LANES),
         array(2, TILES, 16, LANES),
-        array(rows, LANES),
-        array(rows, LANES),
     )
-    motion, stress, solid, ocean, floor, *send = call(start_kernel, outs, (parity, *own, *received))
+    scratch = [pltpu.VMEM(x.shape, x.dtype) for x in (surface, momentum, bathymetry, wet_mask)]
+    scratch.append(pltpu.SemaphoreType.DMA((len(own),)))
+    packed = (array(pack_y_rows(slabs), LANES),) * 2
+    *held, one, two = call(pack_y_kernel, (*wide, *packed), (parity, *own), scratch, pltpu.HBM)
+    received = exchanged(one, two, "gy")
+    packed = (array(payload_rows(slabs, "first"), LANES),) * 2
+    motion, stress, solid, ocean, floor, *send = call(
+        start_kernel, (*wide, *packed), (parity, *held, *received), aliases={i + 1: i for i in range(5)}
+    )
     base = coef = None
     for step in range(STEPS):
         received = exchanged(*send, "gx")
         first, last, edge = step == 0, step == STEPS - 1, step == STEPS - 2
         height = 32 if last else 24
-        table = (15, TILES, height, LANES)
+        table = (8, TILES, height, LANES)
+        padded = height + 2 * PAD
         scratch = [
+            pltpu.VMEM((TILES, padded, LANES), f32),
+            pltpu.VMEM((2, 2, TILES, padded, LANES), f32),
             pltpu.VMEM((TILES, height, LANES), f32),
-            pltpu.VMEM((2, 2, TILES, height, LANES), f32),
             pltpu.VMEM((3, 3, depth_cells, 256), f32),
         ]
         rows = payload_rows(slabs, "last" if edge else "usual")

time: 117 us -> 115 us (0.983)
  Pallas kernels: 21.8 us -> 19.2 us
    pallas_call x6, Pallas kernels: 21.8 us -> 19.2 us  [call(): pl.pallas_call(kernel, out_shape=outs, in_specs=specs, out_specs=tuple((p...]
where the time goes in v3:
time: 115 us; the launch traced here: 114 us
  waiting for transfers between devices  61.4 us (53%)
  starting transfers between devices  24.7 us (21%)
  Pallas kernels  19.2 us (17%)
  local copies, waits for them, and re-layouts  8.12 us (7%)
    ppermute x5, waiting for transfers between devices, exchanged(): lax.ppermute(second, axis, swap(size, 1))  48.6 us
    ppermute x5, starting transfers between devices, exchanged(): lax.ppermute(second, axis, swap(size, 1))  22.6 us
    pallas_call x6, Pallas kernels, call(): pl.pallas_call(kernel, out_shape=outs, in_specs=specs, out_specs=tuple((p...  19.2 us
    ppermute x5, waiting for transfers between devices, exchanged(): lax.ppermute(first, axis, swap(size, 0))  12.8 us
    unnamed x18, local copies, waits for them, and re-layouts  8.12 us
  transfers between devices with their start and end apart: 10, of which 9 were waited for; matrix products, arithmetic and copies ran while one was open for 0% of the time, Pallas kernels for 0%

profile of v3, /device:TPU:192, one launch (start us, length us, event | category | flops | bytes accessed | tf_op | source)
XLA Modules:
  0.0 114.2 jit_solution(5770752356892755143)
XLA Ops:
  0.6 0.1 pad_add_fusion.parity.refs_0_
  0.7 0.0 copy-start
  0.7 1.1 copy-done
  1.8 0.0 copy-start.1
  1.8 1.0 copy-done.1
  2.8 0.0 copy-start.2
  2.8 0.9 copy-done.2
  3.7 0.0 copy-start.3
  3.7 0.9 copy-done.3
  4.5 0.0 copy-start.4
  4.5 0.9 copy-done.4
  5.4 0.0 copy-start.5
  5.4 0.9 copy-done.5
  6.3 0.0 copy-start.6
  6.3 0.8 copy-done.6
  7.2 0.0 copy-start.7
  7.2 0.8 copy-done.7
  8.0 0.0 copy-start.8
  8.0 0.8 copy-done.8
  8.9 2.2 %shard_map.120 = (f32[3,2,96,256]{3,2,1,0:T(8,128)S(1)}, f32[6,2,96,256]{3,2,1,0:T(8,128)S(1)}, f32[3,2,96,256]{3,2,1,0:T(8,128)S(1)}, f32[3,9,16,128]{3,2,1,0:T...) custom-call(s32[2]{0:T(128)S(1)} %pad_add_fusion.parity.refs_0_, ...), custom_call_target="tpu_custom_call" | custom-call | tf_op jit(solution)/shard_map/pallas_call | solution.py:639
  11.0 0.1 collective-permute-start
  11.1 3.0 %collective-permute-start.1 = (f32[96,128]{1,0:T(8,128)S(1)}, f32[96,128]{1,0:T(8,128)S(1)}, u32[]{:S(2)}, u32[]{:S(2)}) collective-permute-start(f32[96,128]{1,0:T(8,128)S(1)} %get-tuple-element.40), channel_id=1, source_target_pairs={{1,2},{2,1},{3,4},{4,3},{5,6},{6,5},{9,10},{10,9},{11,12},{12,11},... | collective-permute-start | bytes 147464 | tf_op jit(solution)/shard_map/ppermute | solution.py:624
  14.1 0.0 collective-permute-done.one
  14.2 2.4 %collective-permute-done.1.two = f32[96,128]{1,0:T(8,128)S(1)} collective-permute-done((f32[96,128]{1,0:T(8,128)S(1)}, f32[96,128]{1,0:T(8,128)S(1)}, u32[]{:S(2)}, u32[]{:S(2)}) %collective-permute-start.1) | collective-permute-done | bytes 49184 | tf_op jit(solution)/shard_map/ppermute | solution.py:624
  16.5 2.7 %shard_map.121 = (f32[3,2,96,256]{3,2,1,0:T(8,128)S(1)}, f32[6,2,96,256]{3,2,1,0:T(8,128)S(1)}, f32[3,2,96,256]{3,2,1,0:T(8,128)S(1)}, f32[3,9,16,128]{3,2,1,0:T...) custom-call(s32[2]{0:T(128)S(1)} %pad_add_fusion.parity.refs_0_, ...), custom_call_target="tpu_custom_call", output_to_operand_aliasing={{0}: (1, {}), {1}: (2, {}), {2}: (3, {}), {3}: (4, {}), {4}... | custom-call | tf_op jit(solution)/shard_map/pallas_call | solution.py:639
  19.2 1.7 %collective-permute-start.2 = (f32[656,128]{1,0:T(8,128)S(1)}, f32[656,128]{1,0:T(8,128)S(1)}, u32[]{:S(2)}, u32[]{:S(2)}) collective-permute-start(f32[656,128]{1,0:T(8,128)S(1)} %get-tuple-element.41), channel_id=1, source_target_pairs={{0,8},{8,0},{16,24},{24,16},{32,40},{40,32},{48,56},{56,48},{64,72... | collective-permute-start | bytes 1007624 | tf_op jit(solution)/shard_map/ppermute | solution.py:623
  20.9 6.3 %collective-permute-start.3 = (f32[656,128]{1,0:T(8,128)S(1)}, f32[656,128]{1,0:T(8,128)S(1)}, u32[]{:S(2)}, u32[]{:S(2)}) collective-permute-start(f32[656,128]{1,0:T(8,128)S(1)} %get-tuple-element.42), channel_id=1, source_target_pairs={{8,16},{16,8},{24,32},{32,24},{40,48},{48,40},{56,64},{64,56},{72,... | collective-permute-start | bytes 1007624 | tf_op jit(solution)/shard_map/ppermute | solution.py:624
  27.1 2.4 %collective-permute-done.2.refs_1_ = f32[656,128]{1,0:T(8,128)S(1)} collective-permute-done((f32[656,128]{1,0:T(8,128)S(1)}, f32[656,128]{1,0:T(8,128)S(1)}, u32[]{:S(2)}, u32[]{:S(2)}) %collective-permute-start.2) | collective-permute-done | bytes 335904 | tf_op jit(solution)/shard_map/ppermute | solution.py:623
  29.6 16.0 %collective-permute-done.3.refs_2_ = f32[656,128]{1,0:T(8,128)S(1)} collective-permute-done((f32[656,128]{1,0:T(8,128)S(1)}, f32[656,128]{1,0:T(8,128)S(1)}, u32[]{:S(2)}, u32[]{:S(2)}) %collective-permute-start.3) | collective-permute-done | bytes 335904 | tf_op jit(solution)/shard_map/ppermute | solution.py:624
  45.6 3.8 %shard_map.122 = (f32[3,2,96,256]{3,2,1,0:T(8,128)S(1)}, f32[6,2,96,256]{3,2,1,0:T(8,128)S(1)}, f32[3,9,16,128]{3,2,1,0:T(8,128)S(1)}, f32[440,128]{1,0:T(8,128)...) custom-call(s32[2]{0:T(128)S(1)} %pad_add_fusion.parity.refs_0_, ...), custom_call_target="tpu_custom_call" | custom-call | tf_op jit(solution)/shard_map/pallas_call | solution.py:639
  49.4 0.1 collective-permute-start.4
  49.5 4.5 %collective-permute-start.5 = (f32[440,128]{1,0:T(8,128)S(1)}, f32[440,128]{1,0:T(8,128)S(1)}, u32[]{:S(2)}, u32[]{:S(2)}) collective-permute-start(f32[440,128]{1,0:T(8,128)S(1)} %get-tuple-element.49), channel_id=1, source_target_pairs={{8,16},{16,8},{24,32},{32,24},{40,48},{48,40},{56,64},{64,56},{72,... | collective-permute-start | bytes 675848 | tf_op jit(solution)/shard_map/ppermute | solution.py:624
  53.9 3.0 %collective-permute-done.4.refs_3_ = f32[440,128]{1,0:T(8,128)S(1)} collective-permute-done((f32[440,128]{1,0:T(8,128)S(1)}, f32[440,128]{1,0:T(8,128)S(1)}, u32[]{:S(2)}, u32[]{:S(2)}) %collective-permute-start.4) | collective-permute-done | bytes 225312 | tf_op jit(solution)/shard_map/ppermute | solution.py:623
  56.9 10.0 %collective-permute-done.5.refs_4_ = f32[440,128]{1,0:T(8,128)S(1)} collective-permute-done((f32[440,128]{1,0:T(8,128)S(1)}, f32[440,128]{1,0:T(8,128)S(1)}, u32[]{:S(2)}, u32[]{:S(2)}) %collective-permute-start.5) | collective-permute-done | bytes 225312 | tf_op jit(solution)/shard_map/ppermute | solution.py:624
  66.9 3.5 %shard_map.123 = (f32[3,2,96,256]{3,2,1,0:T(8,128)S(1)}, f32[6,2,96,256]{3,2,1,0:T(8,128)S(1)}, f32[3,9,16,128]{3,2,1,0:T(8,128)S(1)}, f32[440,128]{1,0:T(8,128)S(1)}, f32[440,128]{1,0:T(8,128)S(1)}) custom-call(s32[2]{0:T(128)S(1)} %pad_add_fusion.parity.refs_0_, f32[656,128]{1,0:T(8,128)S(1)} %collective-permute-done.2.refs_1_, ...), custom_call_target="tpu_custom_call" | custom-call | tf_op jit(solution)/shard_map/pallas_call | solution.py:639
  70.4 0.1 collective-permute-start.6
  70.5 4.5 %collective-permute-start.7 = (f32[440,128]{1,0:T(8,128)S(1)}, f32[440,128]{1,0:T(8,128)S(1)}, u32[]{:S(2)}, u32[]{:S(2)}) collective-permute-start(f32[440,128]{1,0:T(8,128)S(1)} %get-tuple-element.55), channel_id=1, source_target_pairs={{8,16},{16,8},{24,32},{32,24},{40,48},{48,40},{56,64},{64,56},{72,... | collective-permute-start | bytes 675848 | tf_op jit(solution)/shard_map/ppermute | solution.py:624
  75.0 2.1 %collective-permute-done.6.refs_3_ = f32[440,128]{1,0:T(8,128)S(1)} collective-permute-done((f32[440,128]{1,0:T(8,128)S(1)}, f32[440,128]{1,0:T(8,128)S(1)}, u32[]{:S(2)}, u32[]{:S(2)}) %collective-permute-start.6) | collective-permute-done | bytes 225312 | tf_op jit(solution)/shard_map/ppermute | solution.py:623
  77.1 10.0 %collective-permute-done.7.refs_4_ = f32[440,128]{1,0:T(8,128)S(1)} collective-permute-done((f32[440,128]{1,0:T(8,128)S(1)}, f32[440,128]{1,0:T(8,128)S(1)}, u32[]{:S(2)}, u32[]{:S(2)}) %collective-permute-start.7) | collective-permute-done | bytes 225312 | tf_op jit(solution)/shard_map/ppermute | solution.py:624
  87.1 3.5 %shard_map.124 = (f32[3,2,96,256]{3,2,1,0:T(8,128)S(1)}, f32[6,2,96,256]{3,2,1,0:T(8,128)S(1)}, f32[3,9,16,128]{3,2,1,0:T(8,128)S(1)}, f32[800,128]{1,0:T(8,128)S(1)}, f32[800,128]{1,0:T(8,128)S(1)}) custom-call(s32[2]{0:T(128)S(1)} %pad_add_fusion.parity.refs_0_, f32[656,128]{1,0:T(8,128)S(1)} %collective-permute-done.2.refs_1_, ...), custom_call_target="tpu_custom_call" | custom-call | tf_op jit(solution)/shard_map/pallas_call | solution.py:639
  90.6 0.1 collective-permute-start.8
  90.7 4.5 %collective-permute-start.9 = (f32[800,128]{1,0:T(8,128)S(1)}, f32[800,128]{1,0:T(8,128)S(1)}, u32[]{:S(2)}, u32[]{:S(2)}) collective-permute-start(f32[800,128]{1,0:T(8,128)S(1)} %get-tuple-element.60), channel_id=1, source_target_pairs={{8,16},{16,8},{24,32},{32,24},{40,48},{48,40},{56,64},{64,56},{72,... | collective-permute-start | bytes 1228808 | tf_op jit(solution)/shard_map/ppermute | solution.py:624
  95.2 5.2 %collective-permute-done.8.refs_3_ = f32[800,128]{1,0:T(8,128)S(1)} collective-permute-done((f32[800,128]{1,0:T(8,128)S(1)}, f32[800,128]{1,0:T(8,128)S(1)}, u32[]{:S(2)}, u32[]{:S(2)}) %collective-permute-start.8) | collective-permute-done | bytes 409632 | tf_op jit(solution)/shard_map/ppermute | solution.py:623
  100.4 10.2 %collective-permute-done.9.refs_4_ = f32[800,128]{1,0:T(8,128)S(1)} collective-permute-done((f32[800,128]{1,0:T(8,128)S(1)}, f32[800,128]{1,0:T(8,128)S(1)}, u32[]{:S(2)}, u32[]{:S(2)}) %collective-permute-start.9) | collective-permute-done | bytes 409632 | tf_op jit(solution)/shard_map/ppermute | solution.py:624
  110.6 3.6 %shard_map.125 = (f32[3,2,96,128]{3,2,1,0:T(8,128)}, f32[6,2,96,128]{3,2,1,0:T(8,128)}, f32[16,1024]{1,0:T(8,128)}, f32[2,16,1024]{2,1,0:T(8,128)}) custom-call(s32[2]{0:T(128)S(1)} %pad_add_fusion.parity.refs_0_, f32[656,128]{1,0:T(8,128)S(1)} %collective-permute-done.2.refs_1_, f32[656,128]{1,0:T(8,128)S(1)} %collective-permute-done.3.refs_2_, ...), custom_call_target="tpu_custom_call" | custom-call | tf_op jit(solution)/shard_map/pallas_call | solution.py:639
Async XLA Ops:
  0.7 1.1 copy-start
  1.8 1.0 copy-start.1
  2.8 0.9 copy-start.2
  3.7 0.9 copy-start.3
  4.5 0.9 copy-start.4
  5.4 0.9 copy-start.5
  6.3 0.8 copy-start.6
  7.2 0.8 copy-start.7
  8.0 0.8 copy-start.8
  11.0 3.1 %collective-permute-start = (f32[96,128]{1,0:T(8,128)S(1)}, f32[96,128]{1,0:T(8,128)S(1)}, u32[]{:S(2)}, u32[]{:S(2)}) collective-permute-start(f32[96,128]{1,0:T(8,128)S(1)} %get-tuple-element.39), channel_id=1, source_target_pairs={{0,1},{1,0},{2,3},{3,2},{4,5},{5,4},{6,7},{7,6},{8,9},{9,8},{10,11... | collective-permute-start | bytes 147464 | tf_op jit(solution)/shard_map/ppermute | solution.py:623
  11.1 5.4 %collective-permute-start.1 = (f32[96,128]{1,0:T(8,128)S(1)}, f32[96,128]{1,0:T(8,128)S(1)}, u32[]{:S(2)}, u32[]{:S(2)}) collective-permute-start(f32[96,128]{1,0:T(8,128)S(1)} %get-tuple-element.40), channel_id=1, source_target_pairs={{1,2},{2,1},{3,4},{4,3},{5,6},{6,5},{9,10},{10,9},{11,12},{12,11},... | collective-permute-start | bytes 147464 | tf_op jit(solution)/shard_map/ppermute | solution.py:624
  19.2 10.4 %collective-permute-start.2 = (f32[656,128]{1,0:T(8,128)S(1)}, f32[656,128]{1,0:T(8,128)S(1)}, u32[]{:S(2)}, u32[]{:S(2)}) collective-permute-start(f32[656,128]{1,0:T(8,128)S(1)} %get-tuple-element.41), channel_id=1, source_target_pairs={{0,8},{8,0},{16,24},{24,16},{32,40},{40,32},{48,56},{56,48},{64,72... | collective-permute-start | bytes 1007624 | tf_op jit(solution)/shard_map/ppermute | solution.py:623
  20.9 24.7 %collective-permute-start.3 = (f32[656,128]{1,0:T(8,128)S(1)}, f32[656,128]{1,0:T(8,128)S(1)}, u32[]{:S(2)}, u32[]{:S(2)}) collective-permute-start(f32[656,128]{1,0:T(8,128)S(1)} %get-tuple-element.42), channel_id=1, source_target_pairs={{8,16},{16,8},{24,32},{32,24},{40,48},{48,40},{56,64},{64,56},{72,... | collective-permute-start | bytes 1007624 | tf_op jit(solution)/shard_map/ppermute | solution.py:624
  49.4 7.6 %collective-permute-start.4 = (f32[440,128]{1,0:T(8,128)S(1)}, f32[440,128]{1,0:T(8,128)S(1)}, u32[]{:S(2)}, u32[]{:S(2)}) collective-permute-start(f32[440,128]{1,0:T(8,128)S(1)} %get-tuple-element.48), channel_id=1, source_target_pairs={{0,8},{8,0},{16,24},{24,16},{32,40},{40,32},{48,56},{56,48},{64,72... | collective-permute-start | bytes 675848 | tf_op jit(solution)/shard_map/ppermute | solution.py:623
  49.5 17.5 %collective-permute-start.5 = (f32[440,128]{1,0:T(8,128)S(1)}, f32[440,128]{1,0:T(8,128)S(1)}, u32[]{:S(2)}, u32[]{:S(2)}) collective-permute-start(f32[440,128]{1,0:T(8,128)S(1)} %get-tuple-element.49), channel_id=1, source_target_pairs={{8,16},{16,8},{24,32},{32,24},{40,48},{48,40},{56,64},{64,56},{72,... | collective-permute-start | bytes 675848 | tf_op jit(solution)/shard_map/ppermute | solution.py:624
  70.4 6.7 %collective-permute-start.6 = (f32[440,128]{1,0:T(8,128)S(1)}, f32[440,128]{1,0:T(8,128)S(1)}, u32[]{:S(2)}, u32[]{:S(2)}) collective-permute-start(f32[440,128]{1,0:T(8,128)S(1)} %get-tuple-element.54), channel_id=1, source_target_pairs={{0,8},{8,0},{16,24},{24,16},{32,40},{40,32},{48,56},{56,48},{64,72... | collective-permute-start | bytes 675848 | tf_op jit(solution)/shard_map/ppermute | solution.py:623
  70.5 16.6 %collective-permute-start.7 = (f32[440,128]{1,0:T(8,128)S(1)}, f32[440,128]{1,0:T(8,128)S(1)}, u32[]{:S(2)}, u32[]{:S(2)}) collective-permute-start(f32[440,128]{1,0:T(8,128)S(1)} %get-tuple-element.55), channel_id=1, source_target_pairs={{8,16},{16,8},{24,32},{32,24},{40,48},{48,40},{56,64},{64,56},{72,... | collective-permute-start | bytes 675848 | tf_op jit(solution)/shard_map/ppermute | solution.py:624
  90.6 9.8 %collective-permute-start.8 = (f32[800,128]{1,0:T(8,128)S(1)}, f32[800,128]{1,0:T(8,128)S(1)}, u32[]{:S(2)}, u32[]{:S(2)}) collective-permute-start(f32[800,128]{1,0:T(8,128)S(1)} %get-tuple-element.59), channel_id=1, source_target_pairs={{0,8},{8,0},{16,24},{24,16},{32,40},{40,32},{48,56},{56,48},{64,72... | collective-permute-start | bytes 1228808 | tf_op jit(solution)/shard_map/ppermute | solution.py:623
  90.7 19.9 %collective-permute-start.9 = (f32[800,128]{1,0:T(8,128)S(1)}, f32[800,128]{1,0:T(8,128)S(1)}, u32[]{:S(2)}, u32[]{:S(2)}) collective-permute-start(f32[800,128]{1,0:T(8,128)S(1)} %get-tuple-element.60), channel_id=1, source_target_pairs={{8,16},{16,8},{24,32},{32,24},{40,48},{48,40},{56,64},{64,56},{72,... | collective-permute-start | bytes 1228808 | tf_op jit(solution)/shard_map/ppermute | solution.py:624

commit v4 on v3

--- a/solution.py
+++ b/solution.py
@@ -17,6 +17,7 @@
 
 INTERPRET = False
 VMEM_LIMIT = 20 << 20
+LOADER_LIMIT = 62_000_000
 LANES = 128
 TILES = 9
 UNITS = 3 * TILES
@@ -244,35 +245,21 @@
 
 
 def pack_y_kernel(
-    parity, motion, stress, buoyancy, first, shear, surface, momentum, depth, wet,
-    motion_out, stress_out, solid_out, ocean_out, floor_out, one, two,
-    surface_in, momentum_in, depth_in, wet_in, semaphores,
+    parity, motion, stress, buoyancy, first, shear, surface, momentum, depth, wet, one, two
 ):
-    own = slice(0, LANES)
-    pairs = [(motion, motion_out.at[:, :, :, own]), (stress, stress_out.at[:, :, :, own])]
-    for f, ref in enumerate((buoyancy, first, shear)):
-        pairs.append((ref, solid_out.at[f, :, :, own]))
-    pairs += [(surface, surface_in), (momentum, momentum_in), (depth, depth_in), (wet, wet_in)]
-    copies = [
-        pltpu.make_async_copy(source, target, semaphores.at[i])
-        for i, (source, target) in enumerate(pairs)
-    ]
-    for copy in copies:
-        copy.start()
-    out = Sender(parity[1] == 0, one, two)
+    even = parity[1] == 0
+    out = Sender(even, one, two)
     slabs = motion.shape[2] // 8
     lane = iota((8, LANES), 1)
-    fields = [(motion_out, f, 0) for f in range(3)] + [(stress_out, f, 1) for f in range(6)]
-    fields += [(solid_out, f, 2 + f) for f in range(3)]
-    count, at, waited = 0, 0, set()
+    fields = [(motion, f) for f in range(3)] + [(stress, f) for f in range(6)]
+    fields += [(buoyancy, None), (first, None), (shear, None)]
+    count, at = 0, 0
     right = left = jnp.zeros((8, LANES), jnp.float32)
-    for ref, f, copy in fields:
-        if copy not in waited:
-            copies[copy].wait()
-            waited.add(copy)
+    for ref, f in fields:
         for row in range(2):
             for k in range(slabs):
-                value = ref[f, row, 8 * k : 8 * k + 8, own]
+                z = slice(8 * k, 8 * k + 8)
+                value = ref[row, z, :] if f is None else ref[f, row, z, :]
                 here = lane >> 2 == count
                 right = jnp.where(here, roll(value, 4 * count + 4, 1), right)
                 left = jnp.where(here, roll(value, 4 * count, 1), left)
@@ -283,22 +270,17 @@
     if count:
         out.put(at, right, left)
         count, at = 0, at + 8
-    for copy in copies[5:]:
-        copy.wait()
-    targets = [ocean_out.at[f] for f in range(3)] + [floor_out.at[f] for f in range(2)]
-    sources = [surface_in, momentum_in.at[0], momentum_in.at[1], depth_in, wet_in]
-    for target, source in zip(targets, sources):
+    width = surface.shape[1]
+    for ref, f in ((surface, None), (momentum, 0), (momentum, 1), (depth, None), (wet, None)):
         for group in range(2):
             rows = slice(8 * group, 8 * group + 8)
-            for t in range(TILES - 1):
-                lanes = slice(LANES * t, LANES * t + LANES)
-                value = source[rows, lanes].astype(jnp.float32)
-                target[t, rows, :] = value
-                here = lane >> 5 == count
-                if t == 0:
-                    left = jnp.where(here, roll(value, 32 * count, 1), left)
-                if t == TILES - 2:
-                    right = jnp.where(here, roll(value, 32 * count + 32, 1), right)
+            ends = []
+            for lanes in (slice(0, LANES), slice(width - LANES, width)):
+                value = ref[rows, lanes] if f is None else ref[f, rows, lanes]
+                ends.append(value.astype(jnp.float32))
+            here = lane >> 5 == count
+            right = jnp.where(here, roll(ends[1], 32 * count + 32, 1), right)
+            left = jnp.where(here, roll(ends[0], 32 * count, 1), left)
             count += 1
             if count == 4:
                 out.put(at, right, left)
@@ -312,42 +294,58 @@
 
 
 def start_kernel(
-    parity, motion_in, stress_in, solid_in, ocean_in, floor_in, one, two,
-    motion, stress, solid, ocean, floor, send_one, send_two,
+    parity, motion, stress, buoyancy, first, shear, surface, momentum, depth, wet, one, two,
+    motion_out, stress_out, solid_out, ocean_out, floor_out, send_one, send_two,
 ):
     inbox = Receiver(parity[1] == 0, one, two)
     slabs = motion.shape[2] // 8
     lane = iota((8, LANES), 1)
-    fields = [(motion, f) for f in range(3)] + [(stress, f) for f in range(6)]
-    fields += [(solid, f) for f in range(3)]
+    fields = [(motion, f, motion_out, f) for f in range(3)]
+    fields += [(stress, f, stress_out, f) for f in range(6)]
+    fields += [(ref, None, solid_out, f) for f, ref in enumerate((buoyancy, first, shear))]
     count, at = 0, 0
-    for ref, f in fields:
+    for ref, f, target, g in fields:
         for row in range(2):
             for k in range(slabs):
+                z = slice(8 * k, 8 * k + 8)
+                value = ref[row, z, :] if f is None else ref[f, row, z, :]
                 if count == 0:
                     packed = inbox.right(at), inbox.left(at)
                 after = roll(packed[0], -4 * count, 1)
                 before = roll(packed[1], 124 - 4 * count, 1)
                 halo = jnp.where(lane < 4, after, jnp.where(lane >= 124, before, 0.0))
-                ref[f, row, 8 * k : 8 * k + 8, LANES : 2 * LANES] = halo
+                target[g, row, z, 0:LANES] = value
+                target[g, row, z, LANES : 2 * LANES] = halo
                 count += 1
                 if count == 32:
                     count, at = 0, at + 8
     if count:
         count, at = 0, at + 8
-    for ref, f in [(ocean, 0), (ocean, 1), (ocean, 2), (floor, 0), (floor, 1)]:
+    targets = ((surface, None), (momentum, 0), (momentum, 1), (depth, None), (wet, None))
+    for i, (ref, f) in enumerate(targets):
         for group in range(2):
+            rows = slice(8 * group, 8 * group + 8)
             if count == 0:
                 packed = inbox.right(at), inbox.left(at)
             after = roll(packed[0], -32 * count, 1)
             before = roll(packed[1], 96 - 32 * count, 1)
             halo = jnp.where(lane < 32, after, jnp.where(lane >= 96, before, 0.0))
-            ref[f, TILES - 1, 8 * group : 8 * group + 8, :] = halo
+            for t in range(TILES):
+                if t == TILES - 1:
+                    value = halo
+                else:
+                    lanes = slice(LANES * t, LANES * t + LANES)
+                    value = ref[rows, lanes] if f is None else ref[f, rows, lanes]
+                    value = value.astype(jnp.float32)
+                if i < 3:
+                    ocean_out[i, t, rows, :] = value
+                else:
+                    floor_out[i - 3, t, rows, :] = value
             count += 1
             if count == 4:
                 count, at = 0, at + 8
     out = Sender(parity[0] == 0, send_one, send_two)
-    finish(out, slabs, motion, stress, solid, ocean, floor, None, "first")
+    finish(out, slabs, motion_out, stress_out, solid_out, ocean_out, floor_out, None, "first")
 
 
 PAD = 8
@@ -633,17 +631,16 @@
     def array(*shape):
         return jax.ShapeDtypeStruct(shape, f32)
 
-    def call(kernel, outs, args, scratch=(), space=pltpu.VMEM, aliases=None):
+    def call(kernel, outs, args, scratch=(), grant=VMEM_LIMIT):
         specs = [pl.BlockSpec(memory_space=pltpu.SMEM)]
-        specs += [pl.BlockSpec(memory_space=space)] * (len(args) - 1)
+        specs += [pl.BlockSpec(memory_space=pltpu.VMEM)] * (len(args) - 1)
         return pl.pallas_call(
             kernel,
             out_shape=outs,
             in_specs=specs,
             out_specs=tuple(pl.BlockSpec(memory_space=pltpu.VMEM) for _ in outs),
             scratch_shapes=list(scratch),
-            input_output_aliases=aliases or {},
-            compiler_params=pltpu.CompilerParams(vmem_limit_bytes=VMEM_LIMIT),
+            compiler_params=pltpu.CompilerParams(vmem_limit_bytes=grant),
             interpret=INTERPRET,
         )(*args)
 
@@ -658,14 +655,11 @@
         array(3, TILES, 16, LANES),
         array(2, TILES, 16, LANES),
     )
-    scratch = [pltpu.VMEM(x.shape, x.dtype) for x in (surface, momentum, bathymetry, wet_mask)]
-    scratch.append(pltpu.SemaphoreType.DMA((len(own),)))
     packed = (array(pack_y_rows(slabs), LANES),) * 2
-    *held, one, two = call(pack_y_kernel, (*wide, *packed), (parity, *own), scratch, pltpu.HBM)
-    received = exchanged(one, two, "gy")
+    received = exchanged(*call(pack_y_kernel, packed, (parity, *own), grant=LOADER_LIMIT), "gy")
     packed = (array(payload_rows(slabs, "first"), LANES),) * 2
     motion, stress, solid, ocean, floor, *send = call(
-        start_kernel, (*wide, *packed), (parity, *held, *received), aliases={i + 1: i for i in range(5)}
+        start_kernel, (*wide, *packed), (parity, *own, *received)
     )
     base = coef = None
     for step in range(STEPS):

time: 115 us -> 108 us (0.939)
  local copies, waits for them, and re-layouts: 8.12 us -> 0.06 us
    unnamed x18 -> x20, local copies, waits for them, and re-layouts: 8.12 us -> 0.06 us
where the time goes in v4:
time: 108 us; the launch traced here: 107 us
  waiting for transfers between devices  61.6 us (57%)
  starting transfers between devices  24.6 us (23%)
  Pallas kernels  19.6 us (18%)
    ppermute x5, waiting for transfers between devices, exchanged(): lax.ppermute(second, axis, swap(size, 1))  48.8 us
    ppermute x5, starting transfers between devices, exchanged(): lax.ppermute(second, axis, swap(size, 1))  22.7 us
    pallas_call x6, Pallas kernels, call(): pl.pallas_call(kernel, out_shape=outs, in_specs=specs, out_specs=tuple((p...  19.6 us
    ppermute x5, waiting for transfers between devices, exchanged(): lax.ppermute(first, axis, swap(size, 0))  12.8 us
  transfers between devices with their start and end apart: 10, of which 9 were waited for; matrix products, arithmetic and copies ran while one was open for 0% of the time, Pallas kernels for 0%

profile of v4, /device:TPU:192, one launch (start us, length us, event | category | flops | bytes accessed | tf_op | source)
XLA Modules:
  0.0 107.4 jit_solution(10948262073832369143)
XLA Ops:
  0.6 0.0 copy-start.8
  0.6 0.0 copy-start.7
  0.7 0.0 copy-start.2
  0.7 0.0 copy-start.6
  0.7 0.0 copy-start.5
  0.7 0.0 copy-start.4
  0.7 0.0 copy-start.3
  0.7 0.0 copy-start
  0.7 0.0 copy-start.1
  0.8 0.6 pad_add_fusion.parity.refs_0_
  1.3 0.0 copy-start.9
  1.3 2.6 %shard_map.120 = (f32[96,128]{1,0:T(8,128)}, f32[96,128]{1,0:T(8,128)}) custom-call(s32[2]{0:T(128)} %pad_add_fusion.parity.refs_0_, f32[3,2,96,128]{3,2,1,0:T(8,128)} %motion.3, f32[6,2,96,128]{3,2,1,0:T(8,128)} %stress.3, f32[2,96,128]{2,1,0:T(8,128)} %buoyancy.3, f32[2,96,128]{2,1,0:T(8,128)} %first.3, f32[2,96,128]{2,1,0:T(8,128)} %shear.3, ...), custom_call_target="tpu_custom_call" | custom-call | tf_op jit(solution)/shard_map/pallas_call | solution.py:637
  4.0 0.0 collective-permute-start
  4.0 3.0 %collective-permute-start.1 = (f32[96,128]{1,0:T(8,128)}, f32[96,128]{1,0:T(8,128)S(1)}, u32[]{:S(2)}, u32[]{:S(2)}) collective-permute-start(f32[96,128]{1,0:T(8,128)} %get-tuple-element.30), channel_id=1, source_target_pairs={{1,2},{2,1},{3,4},{4,3},{5,6},{6,5},{9,10},{10,9},{11,12},{12,11},... | collective-permute-start | bytes 147464 | tf_op jit(solution)/shard_map/ppermute | solution.py:622
  7.0 0.0 collective-permute-done.one
  7.0 2.6 %collective-permute-done.1.two = f32[96,128]{1,0:T(8,128)S(1)} collective-permute-done((f32[96,128]{1,0:T(8,128)}, f32[96,128]{1,0:T(8,128)S(1)}, u32[]{:S(2)}, u32[]{:S(2)}) %collective-permute-start.1) | collective-permute-done | bytes 49184 | tf_op jit(solution)/shard_map/ppermute | solution.py:622
  9.6 0.0 copy-done.8
  9.6 0.0 copy-done.7
  9.6 0.0 copy-done.2
  9.6 0.0 copy-done.6
  9.6 0.0 copy-done.5
  9.6 0.0 copy-done.4
  9.6 0.0 copy-done.3
  9.6 0.0 copy-done
  9.6 0.0 copy-done.1
  9.7 0.0 copy-done.9
  9.7 2.7 %shard_map.121 = (f32[3,2,96,256]{3,2,1,0:T(8,128)S(1)}, f32[6,2,96,256]{3,2,1,0:T(8,128)S(1)}, f32[3,2,96,256]{3,2,1,0:T(8,128)S(1)}, f32[3,9,16,128]{3,2,1,0:T...) custom-call(s32[2]{0:T(128)S(1)} %copy-done.9, ...), custom_call_target="tpu_custom_call" | custom-call | tf_op jit(solution)/shard_map/pallas_call | solution.py:637
  12.4 1.7 %collective-permute-start.2 = (f32[656,128]{1,0:T(8,128)S(1)}, f32[656,128]{1,0:T(8,128)S(1)}, u32[]{:S(2)}, u32[]{:S(2)}) collective-permute-start(f32[656,128]{1,0:T(8,128)S(1)} %get-tuple-element.31), channel_id=1, source_target_pairs={{0,8},{8,0},{16,24},{24,16},{32,40},{40,32},{48,56},{56,48},{64,72... | collective-permute-start | bytes 1007624 | tf_op jit(solution)/shard_map/ppermute | solution.py:621
  14.1 6.3 %collective-permute-start.3 = (f32[656,128]{1,0:T(8,128)S(1)}, f32[656,128]{1,0:T(8,128)S(1)}, u32[]{:S(2)}, u32[]{:S(2)}) collective-permute-start(f32[656,128]{1,0:T(8,128)S(1)} %get-tuple-element.32), channel_id=1, source_target_pairs={{8,16},{16,8},{24,32},{32,24},{40,48},{48,40},{56,64},{64,56},{72,... | collective-permute-start | bytes 1007624 | tf_op jit(solution)/shard_map/ppermute | solution.py:622
  20.3 2.5 %collective-permute-done.2.refs_1_ = f32[656,128]{1,0:T(8,128)S(1)} collective-permute-done((f32[656,128]{1,0:T(8,128)S(1)}, f32[656,128]{1,0:T(8,128)S(1)}, u32[]{:S(2)}, u32[]{:S(2)}) %collective-permute-start.2) | collective-permute-done | bytes 335904 | tf_op jit(solution)/shard_map/ppermute | solution.py:621
  22.8 16.0 %collective-permute-done.3.refs_2_ = f32[656,128]{1,0:T(8,128)S(1)} collective-permute-done((f32[656,128]{1,0:T(8,128)S(1)}, f32[656,128]{1,0:T(8,128)S(1)}, u32[]{:S(2)}, u32[]{:S(2)}) %collective-permute-start.3) | collective-permute-done | bytes 335904 | tf_op jit(solution)/shard_map/ppermute | solution.py:622
  38.8 3.8 %shard_map.122 = (f32[3,2,96,256]{3,2,1,0:T(8,128)S(1)}, f32[6,2,96,256]{3,2,1,0:T(8,128)S(1)}, f32[3,9,16,128]{3,2,1,0:T(8,128)S(1)}, f32[440,128]{1,0:T(8,128)...) custom-call(s32[2]{0:T(128)S(1)} %copy-done.9, f32[656,128]{1,0:T(8,128)S(1)} %collective-permute-done.2.refs_1_, ...), custom_call_target="tpu_custom_call" | custom-call | tf_op jit(solution)/shard_map/pallas_call | solution.py:637
  42.5 0.1 collective-permute-start.4
  42.6 4.5 %collective-permute-start.5 = (f32[440,128]{1,0:T(8,128)S(1)}, f32[440,128]{1,0:T(8,128)S(1)}, u32[]{:S(2)}, u32[]{:S(2)}) collective-permute-start(f32[440,128]{1,0:T(8,128)S(1)} %get-tuple-element.39), channel_id=1, source_target_pairs={{8,16},{16,8},{24,32},{32,24},{40,48},{48,40},{56,64},{64,56},{72,... | collective-permute-start | bytes 675848 | tf_op jit(solution)/shard_map/ppermute | solution.py:622
  47.1 3.0 %collective-permute-done.4.refs_3_ = f32[440,128]{1,0:T(8,128)S(1)} collective-permute-done((f32[440,128]{1,0:T(8,128)S(1)}, f32[440,128]{1,0:T(8,128)S(1)}, u32[]{:S(2)}, u32[]{:S(2)}) %collective-permute-start.4) | collective-permute-done | bytes 225312 | tf_op jit(solution)/shard_map/ppermute | solution.py:621
  50.1 10.0 %collective-permute-done.5.refs_4_ = f32[440,128]{1,0:T(8,128)S(1)} collective-permute-done((f32[440,128]{1,0:T(8,128)S(1)}, f32[440,128]{1,0:T(8,128)S(1)}, u32[]{:S(2)}, u32[]{:S(2)}) %collective-permute-start.5) | collective-permute-done | bytes 225312 | tf_op jit(solution)/shard_map/ppermute | solution.py:622
  60.1 3.4 %shard_map.123 = (f32[3,2,96,256]{3,2,1,0:T(8,128)S(1)}, f32[6,2,96,256]{3,2,1,0:T(8,128)S(1)}, f32[3,9,16,128]{3,2,1,0:T(8,128)S(1)}, f32[440,128]{1,0:T(8,128)S(1)}, f32[440,128]{1,0:T(8,128)S(1)}) custom-call(s32[2]{0:T(128)S(1)} %copy-done.9, f32[656,128]{1,0:T(8,128)S(1)} %collective-permute-done.2.refs_1_, ...), custom_call_target="tpu_custom_call" | custom-call | tf_op jit(solution)/shard_map/pallas_call | solution.py:637
  63.6 0.1 collective-permute-start.6
  63.7 4.5 %collective-permute-start.7 = (f32[440,128]{1,0:T(8,128)S(1)}, f32[440,128]{1,0:T(8,128)S(1)}, u32[]{:S(2)}, u32[]{:S(2)}) collective-permute-start(f32[440,128]{1,0:T(8,128)S(1)} %get-tuple-element.45), channel_id=1, source_target_pairs={{8,16},{16,8},{24,32},{32,24},{40,48},{48,40},{56,64},{64,56},{72,... | collective-permute-start | bytes 675848 | tf_op jit(solution)/shard_map/ppermute | solution.py:622
  68.1 2.1 %collective-permute-done.6.refs_3_ = f32[440,128]{1,0:T(8,128)S(1)} collective-permute-done((f32[440,128]{1,0:T(8,128)S(1)}, f32[440,128]{1,0:T(8,128)S(1)}, u32[]{:S(2)}, u32[]{:S(2)}) %collective-permute-start.6) | collective-permute-done | bytes 225312 | tf_op jit(solution)/shard_map/ppermute | solution.py:621
  70.3 10.0 %collective-permute-done.7.refs_4_ = f32[440,128]{1,0:T(8,128)S(1)} collective-permute-done((f32[440,128]{1,0:T(8,128)S(1)}, f32[440,128]{1,0:T(8,128)S(1)}, u32[]{:S(2)}, u32[]{:S(2)}) %collective-permute-start.7) | collective-permute-done | bytes 225312 | tf_op jit(solution)/shard_map/ppermute | solution.py:622
  80.3 3.5 %shard_map.124 = (f32[3,2,96,256]{3,2,1,0:T(8,128)S(1)}, f32[6,2,96,256]{3,2,1,0:T(8,128)S(1)}, f32[3,9,16,128]{3,2,1,0:T(8,128)S(1)}, f32[800,128]{1,0:T(8,128)S(1)}, f32[800,128]{1,0:T(8,128)S(1)}) custom-call(s32[2]{0:T(128)S(1)} %copy-done.9, f32[656,128]{1,0:T(8,128)S(1)} %collective-permute-done.2.refs_1_, ...), custom_call_target="tpu_custom_call" | custom-call | tf_op jit(solution)/shard_map/pallas_call | solution.py:637
  83.8 0.1 collective-permute-start.8
  83.9 4.5 %collective-permute-start.9 = (f32[800,128]{1,0:T(8,128)S(1)}, f32[800,128]{1,0:T(8,128)S(1)}, u32[]{:S(2)}, u32[]{:S(2)}) collective-permute-start(f32[800,128]{1,0:T(8,128)S(1)} %get-tuple-element.50), channel_id=1, source_target_pairs={{8,16},{16,8},{24,32},{32,24},{40,48},{48,40},{56,64},{64,56},{72,... | collective-permute-start | bytes 1228808 | tf_op jit(solution)/shard_map/ppermute | solution.py:622
  88.3 5.2 %collective-permute-done.8.refs_3_ = f32[800,128]{1,0:T(8,128)S(1)} collective-permute-done((f32[800,128]{1,0:T(8,128)S(1)}, f32[800,128]{1,0:T(8,128)S(1)}, u32[]{:S(2)}, u32[]{:S(2)}) %collective-permute-start.8) | collective-permute-done | bytes 409632 | tf_op jit(solution)/shard_map/ppermute | solution.py:621
  93.6 10.2 %collective-permute-done.9.refs_4_ = f32[800,128]{1,0:T(8,128)S(1)} collective-permute-done((f32[800,128]{1,0:T(8,128)S(1)}, f32[800,128]{1,0:T(8,128)S(1)}, u32[]{:S(2)}, u32[]{:S(2)}) %collective-permute-start.9) | collective-permute-done | bytes 409632 | tf_op jit(solution)/shard_map/ppermute | solution.py:622
  103.8 3.6 %shard_map.125 = (f32[3,2,96,128]{3,2,1,0:T(8,128)}, f32[6,2,96,128]{3,2,1,0:T(8,128)}, f32[16,1024]{1,0:T(8,128)}, f32[2,16,1024]{2,1,0:T(8,128)}) custom-call(s32[2]{0:T(128)S(1)} %copy-done.9, f32[656,128]{1,0:T(8,128)S(1)} %collective-permute-done.2.refs_1_, f32[656,128]{1,0:T(8,128)S(1)} %collective-permute-done.3.refs_2_, ...), custom_call_target="tpu_custom_call" | custom-call | tf_op jit(solution)/shard_map/pallas_call | solution.py:637
Async XLA Ops:
  0.6 9.0 %copy-start.8 = (s32[16,1024]{1,0:T(8,128)S(1)}, s32[16,1024]{1,0:T(8,128)}, u32[]{:S(2)}) copy-start(s32[16,1024]{1,0:T(8,128)} %wet.3) | copy-start | bytes 196612
  0.6 8.9 %copy-start.7 = (f32[16,1024]{1,0:T(8,128)S(1)}, f32[16,1024]{1,0:T(8,128)}, u32[]{:S(2)}) copy-start(f32[16,1024]{1,0:T(8,128)} %depth.3) | copy-start | bytes 196612
  0.7 8.9 %copy-start.2 = (f32[2,16,1024]{2,1,0:T(8,128)S(1)}, f32[2,16,1024]{2,1,0:T(8,128)}, u32[]{:S(2)}) copy-start(f32[2,16,1024]{2,1,0:T(8,128)} %momentum.3) | copy-start | bytes 393220
  0.7 8.9 %copy-start.6 = (f32[16,1024]{1,0:T(8,128)S(1)}, f32[16,1024]{1,0:T(8,128)}, u32[]{:S(2)}) copy-start(f32[16,1024]{1,0:T(8,128)} %surface.3) | copy-start | bytes 196612
  0.7 8.9 %copy-start.5 = (f32[2,96,128]{2,1,0:T(8,128)S(1)}, f32[2,96,128]{2,1,0:T(8,128)}, u32[]{:S(2)}) copy-start(f32[2,96,128]{2,1,0:T(8,128)} %shear.3) | copy-start | bytes 294916
  0.7 8.9 %copy-start.4 = (f32[2,96,128]{2,1,0:T(8,128)S(1)}, f32[2,96,128]{2,1,0:T(8,128)}, u32[]{:S(2)}) copy-start(f32[2,96,128]{2,1,0:T(8,128)} %first.3) | copy-start | bytes 294916
  0.7 8.9 %copy-start.3 = (f32[2,96,128]{2,1,0:T(8,128)S(1)}, f32[2,96,128]{2,1,0:T(8,128)}, u32[]{:S(2)}) copy-start(f32[2,96,128]{2,1,0:T(8,128)} %buoyancy.3) | copy-start | bytes 294916
  0.7 8.9 %copy-start = (f32[6,2,96,128]{3,2,1,0:T(8,128)S(1)}, f32[6,2,96,128]{3,2,1,0:T(8,128)}, u32[]{:S(2)}) copy-start(f32[6,2,96,128]{3,2,1,0:T(8,128)} %stress.3) | copy-start | bytes 1769476
  0.7 8.9 %copy-start.1 = (f32[3,2,96,128]{3,2,1,0:T(8,128)S(1)}, f32[3,2,96,128]{3,2,1,0:T(8,128)}, u32[]{:S(2)}) copy-start(f32[3,2,96,128]{3,2,1,0:T(8,128)} %motion.3) | copy-start | bytes 884740
  1.3 8.3 %copy-start.9 = (s32[2]{0:T(128)S(1)}, s32[2]{0:T(128)}, u32[]{:S(2)}) copy-start(s32[2]{0:T(128)} %pad_add_fusion.parity.refs_0_) | copy-start | bytes 28
  4.0 3.0 %collective-permute-start = (f32[96,128]{1,0:T(8,128)}, f32[96,128]{1,0:T(8,128)S(1)}, u32[]{:S(2)}, u32[]{:S(2)}) collective-permute-start(f32[96,128]{1,0:T(8,128)} %get-tuple-element.29), channel_id=1, source_target_pairs={{0,1},{1,0},{2,3},{3,2},{4,5},{5,4},{6,7},{7,6},{8,9},{9,8},{10,11... | collective-permute-start | bytes 147464 | tf_op jit(solution)/shard_map/ppermute | solution.py:621
  4.0 5.6 %collective-permute-start.1 = (f32[96,128]{1,0:T(8,128)}, f32[96,128]{1,0:T(8,128)S(1)}, u32[]{:S(2)}, u32[]{:S(2)}) collective-permute-start(f32[96,128]{1,0:T(8,128)} %get-tuple-element.30), channel_id=1, source_target_pairs={{1,2},{2,1},{3,4},{4,3},{5,6},{6,5},{9,10},{10,9},{11,12},{12,11},... | collective-permute-start | bytes 147464 | tf_op jit(solution)/shard_map/ppermute | solution.py:622
  12.4 10.4 %collective-permute-start.2 = (f32[656,128]{1,0:T(8,128)S(1)}, f32[656,128]{1,0:T(8,128)S(1)}, u32[]{:S(2)}, u32[]{:S(2)}) collective-permute-start(f32[656,128]{1,0:T(8,128)S(1)} %get-tuple-element.31), channel_id=1, source_target_pairs={{0,8},{8,0},{16,24},{24,16},{32,40},{40,32},{48,56},{56,48},{64,72... | collective-permute-start | bytes 1007624 | tf_op jit(solution)/shard_map/ppermute | solution.py:621
  14.1 24.7 %collective-permute-start.3 = (f32[656,128]{1,0:T(8,128)S(1)}, f32[656,128]{1,0:T(8,128)S(1)}, u32[]{:S(2)}, u32[]{:S(2)}) collective-permute-start(f32[656,128]{1,0:T(8,128)S(1)} %get-tuple-element.32), channel_id=1, source_target_pairs={{8,16},{16,8},{24,32},{32,24},{40,48},{48,40},{56,64},{64,56},{72,... | collective-permute-start | bytes 1007624 | tf_op jit(solution)/shard_map/ppermute | solution.py:622
  42.5 7.6 %collective-permute-start.4 = (f32[440,128]{1,0:T(8,128)S(1)}, f32[440,128]{1,0:T(8,128)S(1)}, u32[]{:S(2)}, u32[]{:S(2)}) collective-permute-start(f32[440,128]{1,0:T(8,128)S(1)} %get-tuple-element.38), channel_id=1, source_target_pairs={{0,8},{8,0},{16,24},{24,16},{32,40},{40,32},{48,56},{56,48},{64,72... | collective-permute-start | bytes 675848 | tf_op jit(solution)/shard_map/ppermute | solution.py:621
  42.6 17.5 %collective-permute-start.5 = (f32[440,128]{1,0:T(8,128)S(1)}, f32[440,128]{1,0:T(8,128)S(1)}, u32[]{:S(2)}, u32[]{:S(2)}) collective-permute-start(f32[440,128]{1,0:T(8,128)S(1)} %get-tuple-element.39), channel_id=1, source_target_pairs={{8,16},{16,8},{24,32},{32,24},{40,48},{48,40},{56,64},{64,56},{72,... | collective-permute-start | bytes 675848 | tf_op jit(solution)/shard_map/ppermute | solution.py:622
  63.6 6.7 %collective-permute-start.6 = (f32[440,128]{1,0:T(8,128)S(1)}, f32[440,128]{1,0:T(8,128)S(1)}, u32[]{:S(2)}, u32[]{:S(2)}) collective-permute-start(f32[440,128]{1,0:T(8,128)S(1)} %get-tuple-element.44), channel_id=1, source_target_pairs={{0,8},{8,0},{16,24},{24,16},{32,40},{40,32},{48,56},{56,48},{64,72... | collective-permute-start | bytes 675848 | tf_op jit(solution)/shard_map/ppermute | solution.py:621
  63.7 16.6 %collective-permute-start.7 = (f32[440,128]{1,0:T(8,128)S(1)}, f32[440,128]{1,0:T(8,128)S(1)}, u32[]{:S(2)}, u32[]{:S(2)}) collective-permute-start(f32[440,128]{1,0:T(8,128)S(1)} %get-tuple-element.45), channel_id=1, source_target_pairs={{8,16},{16,8},{24,32},{32,24},{40,48},{48,40},{56,64},{64,56},{72,... | collective-permute-start | bytes 675848 | tf_op jit(solution)/shard_map/ppermute | solution.py:622
  83.8 9.8 %collective-permute-start.8 = (f32[800,128]{1,0:T(8,128)S(1)}, f32[800,128]{1,0:T(8,128)S(1)}, u32[]{:S(2)}, u32[]{:S(2)}) collective-permute-start(f32[800,128]{1,0:T(8,128)S(1)} %get-tuple-element.49), channel_id=1, source_target_pairs={{0,8},{8,0},{16,24},{24,16},{32,40},{40,32},{48,56},{56,48},{64,72... | collective-permute-start | bytes 1228808 | tf_op jit(solution)/shard_map/ppermute | solution.py:621
  83.9 19.9 %collective-permute-start.9 = (f32[800,128]{1,0:T(8,128)S(1)}, f32[800,128]{1,0:T(8,128)S(1)}, u32[]{:S(2)}, u32[]{:S(2)}) collective-permute-start(f32[800,128]{1,0:T(8,128)S(1)} %get-tuple-element.50), channel_id=1, source_target_pairs={{8,16},{16,8},{24,32},{32,24},{40,48},{48,40},{56,64},{64,56},{72,... | collective-permute-start | bytes 1228808 | tf_op jit(solution)/shard_map/ppermute | solution.py:622

commit v5 on v4

--- a/solution.py
+++ b/solution.py
@@ -6,6 +6,7 @@
 from jax.experimental import pallas as pl
 from jax.experimental.pallas import tpu as pltpu
 from jax.sharding import PartitionSpec as P
+
 
 STEPS = 4
 NSUB = 4
@@ -125,6 +126,14 @@
             self.put(at + 8 * k, values[0][:, :LANES], values[1][:, :LANES])
         self.put(at + 8 * slabs, *tails)
 
+    def put_tail(self, at, slabs, right, left):
+        lane = iota((8, LANES), 1)
+        tails = [jnp.zeros((8, LANES), jnp.float32) for _ in range(2)]
+        for k in range(slabs):
+            here = (lane >= 8 * k) & (lane < 8 * k + 8)
+            for i, value in enumerate((right(k), left(k))):
+                tails[i] = jnp.where(here, roll(value[:, LANES:], 4 + 8 * k, 1), tails[i])
+        self.put(at, *tails)
 
     def put_halves(self, at, units):
         low = iota((8, LANES), 0) < 4
@@ -167,12 +176,21 @@
 
 
 def payload_rows(slabs, kind):
-    part, _, _, more = offsets(slabs)
+    _, _, _, more = offsets(slabs)
     return {
-        "first": more + part + 8 * ((FLOOR_UNITS + TILES + 1) // 2),
+        "first": more + 24,
         "usual": more,
         "last": more + 8 * (UNITS + FLOOR_UNITS),
     }[kind]
+
+
+def floor_units(depth, wet):
+    face = wet * roll(wet, -1, 0)
+    return [(value[0:8], value[8:16]) for value in (depth, wet, face)]
+
+
+def static_rows(slabs):
+    return 8 * slabs + 8 * 3 * (TILES - 1) // 2
 
 
 def finish(out, slabs, motion, stress, buoyancy, ocean, floor, mean_row, kind):
@@ -232,12 +250,9 @@
         lanes = slice(LANES * i, LANES * i + LANES)
         out.put(extra_at + 8 * i, top[:, lanes], mean_row[:, lanes])
     if kind == "first":
-        out.put_solid(more_at, slabs, get(buoyancy, 0, 1), get(buoyancy, 0, 0))
-        faces = []
-        for t in range(TILES):
-            wet = floor[1, t, :, :]
-            faces.append(((wet * roll(wet, -1, 0))[0:8], wet[8:16]))
-        out.put_halves(more_at + part, units(floor, 2) + faces)
+        out.put_tail(more_at, slabs, get(buoyancy, 0, 1), get(buoyancy, 0, 0))
+        last = TILES - 1
+        out.put_halves(more_at + 8, floor_units(floor[0, last, :, :], floor[1, last, :, :]))
     if kind == "last":
         for i, (lower, upper) in enumerate(units(ocean, 3) + units(floor, 2)):
             value = jnp.where(low, upper, lower)
@@ -245,9 +260,10 @@
 
 
 def pack_y_kernel(
-    parity, motion, stress, buoyancy, first, shear, surface, momentum, depth, wet, one, two
+    motion, stress, buoyancy, first, shear, surface, momentum, depth, wet, one, two,
+    static_one, static_two,
 ):
-    even = parity[1] == 0
+    even = lax.rem(lax.axis_index("gy"), 2) == 0
     out = Sender(even, one, two)
     slabs = motion.shape[2] // 8
     lane = iota((8, LANES), 1)
@@ -287,6 +303,14 @@
                 count, at = 0, at + 8
     if count:
         out.put(at, right, left)
+    out = Sender(lax.rem(lax.axis_index("gx"), 2) == 0, static_one, static_two)
+    for k in range(slabs):
+        out.put(8 * k, buoyancy[1, 8 * k : 8 * k + 8, :], buoyancy[0, 8 * k : 8 * k + 8, :])
+    units = []
+    for t in range(TILES - 1):
+        lanes = slice(LANES * t, LANES * t + LANES)
+        units += floor_units(depth[:, lanes], wet[:, lanes].astype(jnp.float32))
+    out.put_halves(8 * slabs, units)
 
 
 def pack_y_rows(slabs):
@@ -294,10 +318,10 @@
 
 
 def start_kernel(
-    parity, motion, stress, buoyancy, first, shear, surface, momentum, depth, wet, one, two,
+    motion, stress, buoyancy, first, shear, surface, momentum, depth, wet, one, two,
     motion_out, stress_out, solid_out, ocean_out, floor_out, send_one, send_two,
 ):
-    inbox = Receiver(parity[1] == 0, one, two)
+    inbox = Receiver(lax.rem(lax.axis_index("gy"), 2) == 0, one, two)
     slabs = motion.shape[2] // 8
     lane = iota((8, LANES), 1)
     fields = [(motion, f, motion_out, f) for f in range(3)]
@@ -344,7 +368,7 @@
             count += 1
             if count == 4:
                 count, at = 0, at + 8
-    out = Sender(parity[0] == 0, send_one, send_two)
+    out = Sender(lax.rem(lax.axis_index("gx"), 2) == 0, send_one, send_two)
     finish(out, slabs, motion_out, stress_out, solid_out, ocean_out, floor_out, None, "first")
 
 
@@ -406,9 +430,9 @@
 
 
 def ocean_part(
-    inbox, base, slabs, motion, ocean, floor, wide, first, coef, height, flow, side, row_left
+    inbox, bases, slabs, motion, ocean, floor, wide, first, coef, height, flow, side, row_left
 ):
-    part, ocean_at, _, more_at = offsets(slabs)
+    _, ocean_at, _, more_at = offsets(slabs)
     low = iota((8, LANES), 0) < 4
     groups = 4 if wide else 3
 
@@ -420,13 +444,18 @@
             target[t, PAD + 28 : PAD + 36, :] = far
         target[t, PAD + 20 : PAD + 28, :] = near
 
+    def floor_halves(f, t):
+        if t < TILES - 1:
+            return bases[0].halves(8 * slabs, 3 * t + f)
+        return bases[1].halves(more_at + 8, f)
+
     if first or wide:
         for t in range(TILES):
             for f, target in ((1, flow.at[0, 0]), (0, height)):
-                near, top = base.halves(more_at + part, f * TILES + t)
+                near, top = floor_halves(f, t)
                 far = inbox.right(more_at + 8 * (UNITS + f * TILES + t)) if wide else None
                 place(target, t, floor[f, t, :, :], near, top, far)
-        after = lambda t: base.halves(more_at + part, 2 * TILES + t)[0]
+        after = lambda t: floor_halves(2, t)[0]
         coefficients(coef, flow.at[0], height, None if wide else after)
     spread_left, spread_last = upsampled([row_left, motion[2, 1, 0:1, :]])
     for t in range(TILES):
@@ -486,14 +515,14 @@
 
 
 def step_kernel(last, is_first, edge, *refs):
-    parity, refs = refs[0], list(refs[1:])
+    refs = list(refs)
 
     def take(count):
         taken = refs[:count]
         del refs[:count]
         return taken
 
-    base_one, base_two = take(2)
+    static_one, static_two, base_one, base_two = take(4)
     one, two = (base_one, base_two) if is_first else take(2)
     motion, stress, solid, ocean, floor = take(5)
     ready = not (is_first or last)
@@ -508,8 +537,8 @@
     height, flow, side, speed = take(4)
     slabs = motion.shape[2] // 8
     part, _, extra_at, more_at = offsets(slabs)
-    even = parity[0] == 0
-    base = Receiver(even, base_one, base_two)
+    even = lax.rem(lax.axis_index("gx"), 2) == 0
+    bases = [Receiver(even, static_one, static_two), Receiver(even, base_one, base_two)]
     inbox = Receiver(even, one, two)
 
     def extra_row(take):
@@ -518,7 +547,7 @@
     row_left = extra_row(inbox.left)
     loaded = None if is_first else -LOAD_GAIN * extra_row(inbox.right)
     ocean_part(
-        inbox, base, slabs, motion, ocean, floor, last, is_first, coef, height, flow, side, row_left
+        inbox, bases, slabs, motion, ocean, floor, last, is_first, coef, height, flow, side, row_left
     )
     blocks = 3 if last else 2
     sums = [[] for _ in range(blocks)]
@@ -558,8 +587,10 @@
         xx = [stress[0, 0, z, :], stress[0, 1, z, :], inbox.solid(1, 2 * part, k, slabs)]
         xy = [inbox.solid(-1, part, k, slabs), stress[3, 0, z, :], stress[3, 1, z, :]]
         xz = [inbox.solid(-1, 2 * part, k, slabs), stress[4, 0, z, :], stress[4, 1, z, :]]
-        rate_left = SOLID_STEP * base.solid(-1, more_at, k, slabs)
-        rate_right = SOLID_STEP * base.solid(1, more_at, k, slabs)
+        tail_left = roll(bases[1].left(more_at), -(4 + 8 * k), 1)
+        tail_right = roll(bases[1].right(more_at), -(4 + 8 * k), 1)
+        rate_left = SOLID_STEP * jnp.concatenate([bases[0].left(8 * k), tail_left], axis=1)
+        rate_right = SOLID_STEP * jnp.concatenate([bases[0].right(8 * k), tail_right], axis=1)
         speed[0, 2, z, :] = inbox.solid(-1, 0, k, slabs) + rate_left * xx[0]
         speed[1, 2, z, :] = inbox.solid(1, 0, k, slabs) - rate_right * xy[2]
         speed[2, 2, z, :] = inbox.solid(1, part, k, slabs) - rate_right * xz[2]
@@ -632,8 +663,7 @@
         return jax.ShapeDtypeStruct(shape, f32)
 
     def call(kernel, outs, args, scratch=(), grant=VMEM_LIMIT):
-        specs = [pl.BlockSpec(memory_space=pltpu.SMEM)]
-        specs += [pl.BlockSpec(memory_space=pltpu.VMEM)] * (len(args) - 1)
+        specs = [pl.BlockSpec(memory_space=pltpu.VMEM)] * len(args)
         return pl.pallas_call(
             kernel,
             out_shape=outs,
@@ -644,7 +674,6 @@
             interpret=INTERPRET,
         )(*args)
 
-    parity = jnp.stack([lax.axis_index("gx") % 2, lax.axis_index("gy") % 2]).astype(jnp.int32)
     own = (
         motion, stress, buoyancy, lame_first, lame_shear, surface, momentum, bathymetry, wet_mask,
     )
@@ -655,11 +684,16 @@
         array(3, TILES, 16, LANES),
         array(2, TILES, 16, LANES),
     )
-    packed = (array(pack_y_rows(slabs), LANES),) * 2
-    received = exchanged(*call(pack_y_kernel, packed, (parity, *own), grant=LOADER_LIMIT), "gy")
+    packed = (
+        *(array(pack_y_rows(slabs), LANES),) * 2,
+        *(array(static_rows(slabs), LANES),) * 2,
+    )
+    *send, static_one, static_two = call(pack_y_kernel, packed, own, grant=LOADER_LIMIT)
+    received = exchanged(*send, "gy")
+    static = exchanged(static_one, static_two, "gx")
     packed = (array(payload_rows(slabs, "first"), LANES),) * 2
     motion, stress, solid, ocean, floor, *send = call(
-        start_kernel, (*wide, *packed), (parity, *own, *received)
+        start_kernel, (*wide, *packed), (*own, *received)
     )
     base = coef = None
     for step in range(STEPS):
@@ -678,11 +712,11 @@
         outs = (*state, array(3, TILES, 16, LANES), array(rows, LANES), array(rows, LANES))
         fixed = (motion, stress, solid, ocean, floor)
         if first:
-            base = received
-            inputs = (parity, *base, *fixed)
+            base = (*static, *received)
+            inputs = (*base, *fixed)
             outs = (*outs, array(*table))
         elif last:
-            inputs = (parity, *base, *received, *fixed)
+            inputs = (*base, *received, *fixed)
             scratch = [pltpu.VMEM(table, f32), *scratch]
             outs = (
                 array(3, 2, depth_cells, LANES),
@@ -691,7 +725,7 @@
                 array(2, 16, 8 * LANES),
             )
         else:
-            inputs = (parity, *base, *received, *fixed, coef)
+            inputs = (*base, *received, *fixed, coef)
         kernel = functools.partial(step_kernel, last, first, edge)
         results = call(kernel, outs, inputs, scratch)
         if first:

time: 108 us -> 109 us (level)
  starting transfers between devices: 24.6 us -> 40.1 us
  waiting for transfers between devices: 61.6 us -> 50.3 us
  Pallas kernels: 19.6 us -> 17 us
    ppermute x5 -> x6, starting transfers between devices: 22.7 us -> 38 us  [exchanged(): lax.ppermute(second, axis, swap(size, 1))]
    ppermute x5 -> x6, waiting for transfers between devices: 12.8 us -> 2.49 us  [exchanged(): lax.ppermute(first, axis, swap(size, 0))]
    pallas_call x6, Pallas kernels: 19.6 us -> 17 us  [call(): pl.pallas_call(kernel, out_shape=outs, in_specs=specs, out_specs=tuple((p...]
    ppermute x5 -> x6, waiting for transfers between devices: 48.8 us -> 47.8 us  [exchanged(): lax.ppermute(second, axis, swap(size, 1))]
  transfers between devices with their start and end apart: 10 -> 12, of which waited for: 9 -> 7; matrix products, arithmetic and copies ran while one was open for 0% -> 0% of each run, Pallas kernels for 0% -> 0%
where the time goes in v5:
time: 109 us; the launch traced here: 108 us
  waiting for transfers between devices  50.3 us (46%)
  starting transfers between devices  40.1 us (37%)
  Pallas kernels  17 us (16%)
    ppermute x6, waiting for transfers between devices, exchanged(): lax.ppermute(second, axis, swap(size, 1))  47.8 us
    ppermute x6, starting transfers between devices, exchanged(): lax.ppermute(second, axis, swap(size, 1))  38 us
    pallas_call x6, Pallas kernels, call(): pl.pallas_call(kernel, out_shape=outs, in_specs=specs, out_specs=tuple((p...  17 us
    ppermute x6, waiting for transfers between devices, exchanged(): lax.ppermute(first, axis, swap(size, 0))  2.49 us
  transfers between devices with their start and end apart: 12, of which 7 were waited for; matrix products, arithmetic and copies ran while one was open for 0% of the time, Pallas kernels for 0%

profile of v5, /device:TPU:192, one launch (start us, length us, event | category | flops | bytes accessed | tf_op | source)
XLA Modules:
  0.0 108.4 jit_solution(16373954408605802421)
XLA Ops:
  0.6 0.0 copy-start.8
  0.6 0.0 copy-start.7
  0.7 0.0 copy-start.2
  0.7 0.0 copy-start.6
  0.7 0.0 copy-start.5
  0.7 0.0 copy-start.4
  0.7 0.0 copy-start.3
  0.7 0.0 copy-start
  0.7 0.0 copy-start.1
  0.7 2.8 %shard_map.120 = (f32[96,128]{1,0:T(8,128)}, f32[96,128]{1,0:T(8,128)}, f32[192,128]{1,0:T(8,128)}, f32[192,128]{1,0:T(8,128)}) custom-call(f32[3,2,96,128]{3,2,1,0:T(8,128)} %motion.3, f32[6,2,96,128]{3,2,1,0:T(8,128)} %stress.3, f32[2,96,128]{2,1,0:T(8,128)} %buoyancy.3, f32[2,96,128]{2,1,0:T(8,128)} %first.3, f32[2,96,128]{2,1,0:T(8,128)} %shear.3, ...), custom_call_target="tpu_custom_call" | custom-call | tf_op jit(solution)/shard_map/pallas_call | solution.py:667
  3.5 0.1 collective-permute-start.2
  3.6 3.0 %collective-permute-start.3 = (f32[96,128]{1,0:T(8,128)}, f32[96,128]{1,0:T(8,128)S(1)}, u32[]{:S(2)}, u32[]{:S(2)}) collective-permute-start(f32[96,128]{1,0:T(8,128)} %get-tuple-element.34), channel_id=1, source_target_pairs={{1,2},{2,1},{3,4},{4,3},{5,6},{6,5},{9,10},{10,9},{11,12},{12,11},... | collective-permute-start | bytes 147464 | tf_op jit(solution)/shard_map/ppermute | solution.py:653
  6.6 0.0 collective-permute-done.2.one
  6.6 2.6 %collective-permute-done.3.two = f32[96,128]{1,0:T(8,128)S(1)} collective-permute-done((f32[96,128]{1,0:T(8,128)}, f32[96,128]{1,0:T(8,128)S(1)}, u32[]{:S(2)}, u32[]{:S(2)}) %collective-permute-start.3) | collective-permute-done | bytes 49184 | tf_op jit(solution)/shard_map/ppermute | solution.py:653
  9.2 0.0 copy-done.8
  9.2 0.0 copy-done.7
  9.3 0.0 copy-done.6
  9.3 0.0 copy-done.5
  9.3 0.0 copy-done.4
  9.3 0.0 copy-done.3
  9.3 0.0 copy-done
  9.3 0.0 copy-done.1
  9.3 2.2 %shard_map.121 = (f32[3,2,96,256]{3,2,1,0:T(8,128)S(1)}, f32[6,2,96,256]{3,2,1,0:T(8,128)S(1)}, f32[3,2,96,256]{3,2,1,0:T(8,128)S(1)}, f32[3,9,16,128]{3,2,1,0:T...) custom-call(f32[3,2,96,128]{3,2,1,0:T(8,128)S(1)} %copy-done.1, ...), custom_call_target="tpu_custom_call" | custom-call | tf_op jit(solution)/shard_map/pallas_call | solution.py:667
  11.5 1.7 %collective-permute-start.4 = (f32[464,128]{1,0:T(8,128)S(1)}, f32[464,128]{1,0:T(8,128)S(1)}, u32[]{:S(2)}, u32[]{:S(2)}) collective-permute-start(f32[464,128]{1,0:T(8,128)S(1)} %get-tuple-element.35), channel_id=1, source_target_pairs={{0,8},{8,0},{16,24},{24,16},{32,40},{40,32},{48,56},{56,48},{64,72... | collective-permute-start | bytes 712712 | tf_op jit(solution)/shard_map/ppermute | solution.py:652
  13.2 6.3 %collective-permute-start.5 = (f32[464,128]{1,0:T(8,128)S(1)}, f32[464,128]{1,0:T(8,128)S(1)}, u32[]{:S(2)}, u32[]{:S(2)}) collective-permute-start(f32[464,128]{1,0:T(8,128)S(1)} %get-tuple-element.36), channel_id=1, source_target_pairs={{8,16},{16,8},{24,32},{32,24},{40,48},{48,40},{56,64},{64,56},{72,... | collective-permute-start | bytes 712712 | tf_op jit(solution)/shard_map/ppermute | solution.py:653
  19.4 0.0 copy-done.10
  19.4 0.1 collective-permute-start
  19.5 7.7 %collective-permute-start.1 = (f32[192,128]{1,0:T(8,128)S(1)}, f32[192,128]{1,0:T(8,128)S(1)}, u32[]{:S(2)}, u32[]{:S(2)}) collective-permute-start(f32[192,128]{1,0:T(8,128)S(1)} %copy-done.9), channel_id=1, source_target_pairs={{8,16},{16,8},{24,32},{32,24},{40,48},{48,40},{56,64},{64,56},{72,... | collective-permute-start | bytes 294920 | tf_op jit(solution)/shard_map/ppermute | solution.py:653
  27.3 0.0 collective-permute-done.refs_0_
  27.3 10.6 %collective-permute-done.1.refs_1_ = f32[192,128]{1,0:T(8,128)S(1)} collective-permute-done((f32[192,128]{1,0:T(8,128)S(1)}, f32[192,128]{1,0:T(8,128)S(1)}, u32[]{:S(2)}, u32[]{:S(2)}) %collective-permute-start.1) | collective-permute-done | bytes 98336 | tf_op jit(solution)/shard_map/ppermute | solution.py:653
  37.8 0.0 collective-permute-done.4.refs_2_
  37.8 0.0 collective-permute-done.5.refs_3_
  37.8 3.3 %shard_map.122 = (f32[3,2,96,256]{3,2,1,0:T(8,128)S(1)}, f32[6,2,96,256]{3,2,1,0:T(8,128)S(1)}, f32[3,9,16,128]{3,2,1,0:T(8,128)S(1)}, f32[440,128]{1,0:T(8,128)...) custom-call(f32[192,128]{1,0:T(8,128)S(1)} %collective-permute-done.refs_0_, ...), custom_call_target="tpu_custom_call" | custom-call | tf_op jit(solution)/shard_map/pallas_call | solution.py:667
  41.1 0.1 collective-permute-start.6
  41.2 5.3 %collective-permute-start.7 = (f32[440,128]{1,0:T(8,128)S(1)}, f32[440,128]{1,0:T(8,128)S(1)}, u32[]{:S(2)}, u32[]{:S(2)}) collective-permute-start(f32[440,128]{1,0:T(8,128)S(1)} %get-tuple-element.43), channel_id=1, source_target_pairs={{8,16},{16,8},{24,32},{32,24},{40,48},{48,40},{56,64},{64,56},{72,... | collective-permute-start | bytes 675848 | tf_op jit(solution)/shard_map/ppermute | solution.py:653
  46.5 1.4 %collective-permute-done.6.refs_4_ = f32[440,128]{1,0:T(8,128)S(1)} collective-permute-done((f32[440,128]{1,0:T(8,128)S(1)}, f32[440,128]{1,0:T(8,128)S(1)}, u32[]{:S(2)}, u32[]{:S(2)}) %collective-permute-start.6) | collective-permute-done | bytes 225312 | tf_op jit(solution)/shard_map/ppermute | solution.py:652
  48.0 10.0 %collective-permute-done.7.refs_5_ = f32[440,128]{1,0:T(8,128)S(1)} collective-permute-done((f32[440,128]{1,0:T(8,128)S(1)}, f32[440,128]{1,0:T(8,128)S(1)}, u32[]{:S(2)}, u32[]{:S(2)}) %collective-permute-start.7) | collective-permute-done | bytes 225312 | tf_op jit(solution)/shard_map/ppermute | solution.py:653
  58.0 3.0 %shard_map.123 = (f32[3,2,96,256]{3,2,1,0:T(8,128)S(1)}, f32[6,2,96,256]{3,2,1,0:T(8,128)S(1)}, f32[3,9,16,128]{3,2,1,0:T(8,128)S(1)}, f32[440,128]{1,0:T(8,128)S(1)}, f32[440,128]{1,0:T(8,128)S(1)}) custom-call(f32[192,128]{1,0:T(8,128)S(1)} %collective-permute-done.refs_0_, f32[192,128]{1,0:T(8,128)S(1)} %collective-permute-done.1.refs_1_, ...), custom_call_target="tpu_custom_call" | custom-call | tf_op jit(solution)/shard_map/pallas_call | solution.py:667
  61.0 0.1 collective-permute-start.8
  61.1 7.3 %collective-permute-start.9 = (f32[440,128]{1,0:T(8,128)S(1)}, f32[440,128]{1,0:T(8,128)S(1)}, u32[]{:S(2)}, u32[]{:S(2)}) collective-permute-start(f32[440,128]{1,0:T(8,128)S(1)} %get-tuple-element.49), channel_id=1, source_target_pairs={{8,16},{16,8},{24,32},{32,24},{40,48},{48,40},{56,64},{64,56},{72,... | collective-permute-start | bytes 675848 | tf_op jit(solution)/shard_map/ppermute | solution.py:653
  68.4 0.0 collective-permute-done.8.refs_4_
  68.4 9.1 %collective-permute-done.9.refs_5_ = f32[440,128]{1,0:T(8,128)S(1)} collective-permute-done((f32[440,128]{1,0:T(8,128)S(1)}, f32[440,128]{1,0:T(8,128)S(1)}, u32[]{:S(2)}, u32[]{:S(2)}) %collective-permute-start.9) | collective-permute-done | bytes 225312 | tf_op jit(solution)/shard_map/ppermute | solution.py:653
  77.5 2.9 %shard_map.124 = (f32[3,2,96,256]{3,2,1,0:T(8,128)S(1)}, f32[6,2,96,256]{3,2,1,0:T(8,128)S(1)}, f32[3,9,16,128]{3,2,1,0:T(8,128)S(1)}, f32[800,128]{1,0:T(8,128)S(1)}, f32[800,128]{1,0:T(8,128)S(1)}) custom-call(f32[192,128]{1,0:T(8,128)S(1)} %collective-permute-done.refs_0_, f32[192,128]{1,0:T(8,128)S(1)} %collective-permute-done.1.refs_1_, ...), custom_call_target="tpu_custom_call" | custom-call | tf_op jit(solution)/shard_map/pallas_call | solution.py:667
  80.3 0.1 collective-permute-start.10
  80.4 8.4 %collective-permute-start.11 = (f32[800,128]{1,0:T(8,128)S(1)}, f32[800,128]{1,0:T(8,128)S(1)}, u32[]{:S(2)}, u32[]{:S(2)}) collective-permute-start(f32[800,128]{1,0:T(8,128)S(1)} %get-tuple-element.54), channel_id=1, source_target_pairs={{8,16},{16,8},{24,32},{32,24},{40,48},{48,40},{56,64},{64,56},{72,... | collective-permute-start | bytes 1228808 | tf_op jit(solution)/shard_map/ppermute | solution.py:653
  88.8 1.0 collective-permute-done.10.refs_4_
  89.9 15.5 %collective-permute-done.11.refs_5_ = f32[800,128]{1,0:T(8,128)S(1)} collective-permute-done((f32[800,128]{1,0:T(8,128)S(1)}, f32[800,128]{1,0:T(8,128)S(1)}, u32[]{:S(2)}, u32[]{:S(2)}) %collective-permute-start.11) | collective-permute-done | bytes 409632 | tf_op jit(solution)/shard_map/ppermute | solution.py:653
  105.4 3.0 %shard_map.125 = (f32[3,2,96,128]{3,2,1,0:T(8,128)}, f32[6,2,96,128]{3,2,1,0:T(8,128)}, f32[16,1024]{1,0:T(8,128)}, f32[2,16,1024]{2,1,0:T(8,128)}) custom-call(f32[192,128]{1,0:T(8,128)S(1)} %collective-permute-done.refs_0_, f32[192,128]{1,0:T(8,128)S(1)} %collective-permute-done.1.refs_1_, f32[464,128]{1,0:T(8,128)S(1)} %collective-permute-done.4.refs_2_, ...), custom_call_target="tpu_custom_call" | custom-call | tf_op jit(solution)/shard_map/pallas_call | solution.py:667
  (4 shorter events, 0.0 us)
Async XLA Ops:
  0.6 8.6 %copy-start.8 = (s32[16,1024]{1,0:T(8,128)S(1)}, s32[16,1024]{1,0:T(8,128)}, u32[]{:S(2)}) copy-start(s32[16,1024]{1,0:T(8,128)} %wet.3) | copy-start | bytes 196612
  0.6 8.6 %copy-start.7 = (f32[16,1024]{1,0:T(8,128)S(1)}, f32[16,1024]{1,0:T(8,128)}, u32[]{:S(2)}) copy-start(f32[16,1024]{1,0:T(8,128)} %depth.3) | copy-start | bytes 196612
  0.7 8.6 %copy-start.2 = (f32[2,16,1024]{2,1,0:T(8,128)S(1)}, f32[2,16,1024]{2,1,0:T(8,128)}, u32[]{:S(2)}) copy-start(f32[2,16,1024]{2,1,0:T(8,128)} %momentum.3) | copy-start | bytes 393220
  0.7 8.6 %copy-start.6 = (f32[16,1024]{1,0:T(8,128)S(1)}, f32[16,1024]{1,0:T(8,128)}, u32[]{:S(2)}) copy-start(f32[16,1024]{1,0:T(8,128)} %surface.3) | copy-start | bytes 196612
  0.7 8.6 %copy-start.5 = (f32[2,96,128]{2,1,0:T(8,128)S(1)}, f32[2,96,128]{2,1,0:T(8,128)}, u32[]{:S(2)}) copy-start(f32[2,96,128]{2,1,0:T(8,128)} %shear.3) | copy-start | bytes 294916
  0.7 8.6 %copy-start.4 = (f32[2,96,128]{2,1,0:T(8,128)S(1)}, f32[2,96,128]{2,1,0:T(8,128)}, u32[]{:S(2)}) copy-start(f32[2,96,128]{2,1,0:T(8,128)} %first.3) | copy-start | bytes 294916
  0.7 8.6 %copy-start.3 = (f32[2,96,128]{2,1,0:T(8,128)S(1)}, f32[2,96,128]{2,1,0:T(8,128)}, u32[]{:S(2)}) copy-start(f32[2,96,128]{2,1,0:T(8,128)} %buoyancy.3) | copy-start | bytes 294916
  0.7 8.6 %copy-start = (f32[6,2,96,128]{3,2,1,0:T(8,128)S(1)}, f32[6,2,96,128]{3,2,1,0:T(8,128)}, u32[]{:S(2)}) copy-start(f32[6,2,96,128]{3,2,1,0:T(8,128)} %stress.3) | copy-start | bytes 1769476
  0.7 8.6 %copy-start.1 = (f32[3,2,96,128]{3,2,1,0:T(8,128)S(1)}, f32[3,2,96,128]{3,2,1,0:T(8,128)}, u32[]{:S(2)}) copy-start(f32[3,2,96,128]{3,2,1,0:T(8,128)} %motion.3) | copy-start | bytes 884740
  3.5 15.9 %copy-start.10 = (f32[192,128]{1,0:T(8,128)S(1)}, f32[192,128]{1,0:T(8,128)}, u32[]{:S(2)}) copy-start(f32[192,128]{1,0:T(8,128)} %get-tuple-element.31) | copy-start | bytes 294916
  3.5 16.0 %copy-start.9 = (f32[192,128]{1,0:T(8,128)S(1)}, f32[192,128]{1,0:T(8,128)}, u32[]{:S(2)}) copy-start(f32[192,128]{1,0:T(8,128)} %get-tuple-element.32) | copy-start | bytes 294916
  3.5 3.1 %collective-permute-start.2 = (f32[96,128]{1,0:T(8,128)}, f32[96,128]{1,0:T(8,128)S(1)}, u32[]{:S(2)}, u32[]{:S(2)}) collective-permute-start(f32[96,128]{1,0:T(8,128)} %get-tuple-element.33), channel_id=1, source_target_pairs={{0,1},{1,0},{2,3},{3,2},{4,5},{5,4},{6,7},{7,6},{8,9},{9,8},{10,11... | collective-permute-start | bytes 147464 | tf_op jit(solution)/shard_map/ppermute | solution.py:652
  3.6 5.6 %collective-permute-start.3 = (f32[96,128]{1,0:T(8,128)}, f32[96,128]{1,0:T(8,128)S(1)}, u32[]{:S(2)}, u32[]{:S(2)}) collective-permute-start(f32[96,128]{1,0:T(8,128)} %get-tuple-element.34), channel_id=1, source_target_pairs={{1,2},{2,1},{3,4},{4,3},{5,6},{6,5},{9,10},{10,9},{11,12},{12,11},... | collective-permute-start | bytes 147464 | tf_op jit(solution)/shard_map/ppermute | solution.py:653
  11.5 26.3 %collective-permute-start.4 = (f32[464,128]{1,0:T(8,128)S(1)}, f32[464,128]{1,0:T(8,128)S(1)}, u32[]{:S(2)}, u32[]{:S(2)}) collective-permute-start(f32[464,128]{1,0:T(8,128)S(1)} %get-tuple-element.35), channel_id=1, source_target_pairs={{0,8},{8,0},{16,24},{24,16},{32,40},{40,32},{48,56},{56,48},{64,72... | collective-permute-start | bytes 712712 | tf_op jit(solution)/shard_map/ppermute | solution.py:652
  13.2 24.7 %collective-permute-start.5 = (f32[464,128]{1,0:T(8,128)S(1)}, f32[464,128]{1,0:T(8,128)S(1)}, u32[]{:S(2)}, u32[]{:S(2)}) collective-permute-start(f32[464,128]{1,0:T(8,128)S(1)} %get-tuple-element.36), channel_id=1, source_target_pairs={{8,16},{16,8},{24,32},{32,24},{40,48},{48,40},{56,64},{64,56},{72,... | collective-permute-start | bytes 712712 | tf_op jit(solution)/shard_map/ppermute | solution.py:653
  19.4 7.8 %collective-permute-start = (f32[192,128]{1,0:T(8,128)S(1)}, f32[192,128]{1,0:T(8,128)S(1)}, u32[]{:S(2)}, u32[]{:S(2)}) collective-permute-start(f32[192,128]{1,0:T(8,128)S(1)} %copy-done.10), channel_id=1, source_target_pairs={{0,8},{8,0},{16,24},{24,16},{32,40},{40,32},{48,56},{56,48},{64,72... | collective-permute-start | bytes 294920 | tf_op jit(solution)/shard_map/ppermute | solution.py:652
  19.5 18.3 %collective-permute-start.1 = (f32[192,128]{1,0:T(8,128)S(1)}, f32[192,128]{1,0:T(8,128)S(1)}, u32[]{:S(2)}, u32[]{:S(2)}) collective-permute-start(f32[192,128]{1,0:T(8,128)S(1)} %copy-done.9), channel_id=1, source_target_pairs={{8,16},{16,8},{24,32},{32,24},{40,48},{48,40},{56,64},{64,56},{72,... | collective-permute-start | bytes 294920 | tf_op jit(solution)/shard_map/ppermute | solution.py:653
  41.1 6.9 %collective-permute-start.6 = (f32[440,128]{1,0:T(8,128)S(1)}, f32[440,128]{1,0:T(8,128)S(1)}, u32[]{:S(2)}, u32[]{:S(2)}) collective-permute-start(f32[440,128]{1,0:T(8,128)S(1)} %get-tuple-element.42), channel_id=1, source_target_pairs={{0,8},{8,0},{16,24},{24,16},{32,40},{40,32},{48,56},{56,48},{64,72... | collective-permute-start | bytes 675848 | tf_op jit(solution)/shard_map/ppermute | solution.py:652
  41.2 16.8 %collective-permute-start.7 = (f32[440,128]{1,0:T(8,128)S(1)}, f32[440,128]{1,0:T(8,128)S(1)}, u32[]{:S(2)}, u32[]{:S(2)}) collective-permute-start(f32[440,128]{1,0:T(8,128)S(1)} %get-tuple-element.43), channel_id=1, source_target_pairs={{8,16},{16,8},{24,32},{32,24},{40,48},{48,40},{56,64},{64,56},{72,... | collective-permute-start | bytes 675848 | tf_op jit(solution)/shard_map/ppermute | solution.py:653
  61.0 7.4 %collective-permute-start.8 = (f32[440,128]{1,0:T(8,128)S(1)}, f32[440,128]{1,0:T(8,128)S(1)}, u32[]{:S(2)}, u32[]{:S(2)}) collective-permute-start(f32[440,128]{1,0:T(8,128)S(1)} %get-tuple-element.48), channel_id=1, source_target_pairs={{0,8},{8,0},{16,24},{24,16},{32,40},{40,32},{48,56},{56,48},{64,72... | collective-permute-start | bytes 675848 | tf_op jit(solution)/shard_map/ppermute | solution.py:652
  61.1 16.4 %collective-permute-start.9 = (f32[440,128]{1,0:T(8,128)S(1)}, f32[440,128]{1,0:T(8,128)S(1)}, u32[]{:S(2)}, u32[]{:S(2)}) collective-permute-start(f32[440,128]{1,0:T(8,128)S(1)} %get-tuple-element.49), channel_id=1, source_target_pairs={{8,16},{16,8},{24,32},{32,24},{40,48},{48,40},{56,64},{64,56},{72,... | collective-permute-start | bytes 675848 | tf_op jit(solution)/shard_map/ppermute | solution.py:653
  80.3 9.5 %collective-permute-start.10 = (f32[800,128]{1,0:T(8,128)S(1)}, f32[800,128]{1,0:T(8,128)S(1)}, u32[]{:S(2)}, u32[]{:S(2)}) collective-permute-start(f32[800,128]{1,0:T(8,128)S(1)} %get-tuple-element.53), channel_id=1, source_target_pairs={{0,8},{8,0},{16,24},{24,16},{32,40},{40,32},{48,56},{56,48},{64,72... | collective-permute-start | bytes 1228808 | tf_op jit(solution)/shard_map/ppermute | solution.py:652
  80.4 25.0 %collective-permute-start.11 = (f32[800,128]{1,0:T(8,128)S(1)}, f32[800,128]{1,0:T(8,128)S(1)}, u32[]{:S(2)}, u32[]{:S(2)}) collective-permute-start(f32[800,128]{1,0:T(8,128)S(1)} %get-tuple-element.54), channel_id=1, source_target_pairs={{8,16},{16,8},{24,32},{32,24},{40,48},{48,40},{56,64},{64,56},{72,... | collective-permute-start | bytes 1228808 | tf_op jit(solution)/shard_map/ppermute | solution.py:653

commit v6 on v4

--- a/solution.py
+++ b/solution.py
@@ -245,9 +245,9 @@
 
 
 def pack_y_kernel(
-    parity, motion, stress, buoyancy, first, shear, surface, momentum, depth, wet, one, two
+    motion, stress, buoyancy, first, shear, surface, momentum, depth, wet, one, two
 ):
-    even = parity[1] == 0
+    even = lax.rem(lax.axis_index("gy"), 2) == 0
     out = Sender(even, one, two)
     slabs = motion.shape[2] // 8
     lane = iota((8, LANES), 1)
@@ -294,10 +294,10 @@
 
 
 def start_kernel(
-    parity, motion, stress, buoyancy, first, shear, surface, momentum, depth, wet, one, two,
+    motion, stress, buoyancy, first, shear, surface, momentum, depth, wet, one, two,
     motion_out, stress_out, solid_out, ocean_out, floor_out, send_one, send_two,
 ):
-    inbox = Receiver(parity[1] == 0, one, two)
+    inbox = Receiver(lax.rem(lax.axis_index("gy"), 2) == 0, one, two)
     slabs = motion.shape[2] // 8
     lane = iota((8, LANES), 1)
     fields = [(motion, f, motion_out, f) for f in range(3)]
@@ -344,7 +344,7 @@
             count += 1
             if count == 4:
                 count, at = 0, at + 8
-    out = Sender(parity[0] == 0, send_one, send_two)
+    out = Sender(lax.rem(lax.axis_index("gx"), 2) == 0, send_one, send_two)
     finish(out, slabs, motion_out, stress_out, solid_out, ocean_out, floor_out, None, "first")
 
 
@@ -486,7 +486,7 @@
 
 
 def step_kernel(last, is_first, edge, *refs):
-    parity, refs = refs[0], list(refs[1:])
+    refs = list(refs)
 
     def take(count):
         taken = refs[:count]
@@ -508,7 +508,7 @@
     height, flow, side, speed = take(4)
     slabs = motion.shape[2] // 8
     part, _, extra_at, more_at = offsets(slabs)
-    even = parity[0] == 0
+    even = lax.rem(lax.axis_index("gx"), 2) == 0
     base = Receiver(even, base_one, base_two)
     inbox = Receiver(even, one, two)
 
@@ -632,8 +632,7 @@
         return jax.ShapeDtypeStruct(shape, f32)
 
     def call(kernel, outs, args, scratch=(), grant=VMEM_LIMIT):
-        specs = [pl.BlockSpec(memory_space=pltpu.SMEM)]
-        specs += [pl.BlockSpec(memory_space=pltpu.VMEM)] * (len(args) - 1)
+        specs = [pl.BlockSpec(memory_space=pltpu.VMEM)] * len(args)
         return pl.pallas_call(
             kernel,
             out_shape=outs,
@@ -644,7 +643,6 @@
             interpret=INTERPRET,
         )(*args)
 
-    parity = jnp.stack([lax.axis_index("gx") % 2, lax.axis_index("gy") % 2]).astype(jnp.int32)
     own = (
         motion, stress, buoyancy, lame_first, lame_shear, surface, momentum, bathymetry, wet_mask,
     )
@@ -656,10 +654,10 @@
         array(2, TILES, 16, LANES),
     )
     packed = (array(pack_y_rows(slabs), LANES),) * 2
-    received = exchanged(*call(pack_y_kernel, packed, (parity, *own), grant=LOADER_LIMIT), "gy")
+    received = exchanged(*call(pack_y_kernel, packed, own, grant=LOADER_LIMIT), "gy")
     packed = (array(payload_rows(slabs, "first"), LANES),) * 2
     motion, stress, solid, ocean, floor, *send = call(
-        start_kernel, (*wide, *packed), (parity, *own, *received)
+        start_kernel, (*wide, *packed), (*own, *received)
     )
     base = coef = None
     for step in range(STEPS):
@@ -679,10 +677,10 @@
         fixed = (motion, stress, solid, ocean, floor)
         if first:
             base = received
-            inputs = (parity, *base, *fixed)
+            inputs = (*base, *fixed)
             outs = (*outs, array(*table))
         elif last:
-            inputs = (parity, *base, *received, *fixed)
+            inputs = (*base, *received, *fixed)
             scratch = [pltpu.VMEM(table, f32), *scratch]
             outs = (
                 array(3, 2, depth_cells, LANES),
@@ -691,7 +689,7 @@
                 array(2, 16, 8 * LANES),
             )
         else:
-            inputs = (parity, *base, *received, *fixed, coef)
+            inputs = (*base, *received, *fixed, coef)
         kernel = functools.partial(step_kernel, last, first, edge)
         results = call(kernel, outs, inputs, scratch)
         if first:

time: 108 us -> 104 us (0.963)
  Pallas kernels: 19.6 us -> 17 us
    pallas_call x6, Pallas kernels: 19.6 us -> 17 us  [call(): pl.pallas_call(kernel, out_shape=outs, in_specs=specs, out_specs=tuple((p...]
where the time goes in v6:
time: 104 us
  waiting for transfers between devices  61.6 us (59%)
  starting transfers between devices  24.6 us (24%)
  Pallas kernels  17 us (16%)
    ppermute x5, waiting for transfers between devices, exchanged(): lax.ppermute(second, axis, swap(size, 1))  48.8 us
    ppermute x5, starting transfers between devices, exchanged(): lax.ppermute(second, axis, swap(size, 1))  22.7 us
    pallas_call x6, Pallas kernels, call(): pl.pallas_call(kernel, out_shape=outs, in_specs=specs, out_specs=tuple((p...  17 us
    ppermute x5, waiting for transfers between devices, exchanged(): lax.ppermute(first, axis, swap(size, 0))  12.8 us
  transfers between devices with their start and end apart: 10, of which 9 were waited for; matrix products, arithmetic and copies ran while one was open for 0% of the time, Pallas kernels for 0%

profile of v6, /device:TPU:192, one launch (start us, length us, event | category | flops | bytes accessed | tf_op | source)
XLA Modules:
  0.0 104.1 jit_solution(18437299172715785051)
XLA Ops:
  0.6 0.0 copy-start.8
  0.6 0.0 copy-start.7
  0.7 0.0 copy-start.2
  0.7 0.0 copy-start.6
  0.7 0.0 copy-start.5
  0.7 0.0 copy-start.4
  0.7 0.0 copy-start.3
  0.7 0.0 copy-start
  0.7 0.0 copy-start.1
  0.7 2.7 %shard_map.120 = (f32[96,128]{1,0:T(8,128)}, f32[96,128]{1,0:T(8,128)}) custom-call(f32[3,2,96,128]{3,2,1,0:T(8,128)} %motion.3, f32[6,2,96,128]{3,2,1,0:T(8,128)} %stress.3, f32[2,96,128]{2,1,0:T(8,128)} %buoyancy.3, f32[2,96,128]{2,1,0:T(8,128)} %first.3, f32[2,96,128]{2,1,0:T(8,128)} %shear.3, f32[16,1024]{1,0:T(8,128)} %surface.3, ...), custom_call_target="tpu_custom_call" | custom-call | tf_op jit(solution)/shard_map/pallas_call | solution.py:636
  3.5 0.0 collective-permute-start
  3.5 3.0 %collective-permute-start.1 = (f32[96,128]{1,0:T(8,128)}, f32[96,128]{1,0:T(8,128)S(1)}, u32[]{:S(2)}, u32[]{:S(2)}) collective-permute-start(f32[96,128]{1,0:T(8,128)} %get-tuple-element.30), channel_id=1, source_target_pairs={{1,2},{2,1},{3,4},{4,3},{5,6},{6,5},{9,10},{10,9},{11,12},{12,11},... | collective-permute-start | bytes 147464 | tf_op jit(solution)/shard_map/ppermute | solution.py:622
  6.5 0.0 collective-permute-done.one
  6.5 2.6 %collective-permute-done.1.two = f32[96,128]{1,0:T(8,128)S(1)} collective-permute-done((f32[96,128]{1,0:T(8,128)}, f32[96,128]{1,0:T(8,128)S(1)}, u32[]{:S(2)}, u32[]{:S(2)}) %collective-permute-start.1) | collective-permute-done | bytes 49184 | tf_op jit(solution)/shard_map/ppermute | solution.py:622
  9.1 0.0 copy-done.8
  9.1 0.0 copy-done.7
  9.1 0.0 copy-done.2
  9.1 0.0 copy-done.6
  9.1 0.0 copy-done.5
  9.1 0.0 copy-done.4
  9.1 0.0 copy-done.3
  9.1 0.0 copy-done
  9.1 0.0 copy-done.1
  9.1 2.2 %shard_map.121 = (f32[3,2,96,256]{3,2,1,0:T(8,128)S(1)}, f32[6,2,96,256]{3,2,1,0:T(8,128)S(1)}, f32[3,2,96,256]{3,2,1,0:T(8,128)S(1)}, f32[3,9,16,128]{3,2,1,0:T...) custom-call(f32[3,2,96,128]{3,2,1,0:T(8,128)S(1)} %copy-done.1, ...), custom_call_target="tpu_custom_call" | custom-call | tf_op jit(solution)/shard_map/pallas_call | solution.py:636
  11.3 1.7 %collective-permute-start.2 = (f32[656,128]{1,0:T(8,128)S(1)}, f32[656,128]{1,0:T(8,128)S(1)}, u32[]{:S(2)}, u32[]{:S(2)}) collective-permute-start(f32[656,128]{1,0:T(8,128)S(1)} %get-tuple-element.31), channel_id=1, source_target_pairs={{0,8},{8,0},{16,24},{24,16},{32,40},{40,32},{48,56},{56,48},{64,72... | collective-permute-start | bytes 1007624 | tf_op jit(solution)/shard_map/ppermute | solution.py:621
  13.0 6.3 %collective-permute-start.3 = (f32[656,128]{1,0:T(8,128)S(1)}, f32[656,128]{1,0:T(8,128)S(1)}, u32[]{:S(2)}, u32[]{:S(2)}) collective-permute-start(f32[656,128]{1,0:T(8,128)S(1)} %get-tuple-element.32), channel_id=1, source_target_pairs={{8,16},{16,8},{24,32},{32,24},{40,48},{48,40},{56,64},{64,56},{72,... | collective-permute-start | bytes 1007624 | tf_op jit(solution)/shard_map/ppermute | solution.py:622
  19.3 2.5 %collective-permute-done.2.refs_0_ = f32[656,128]{1,0:T(8,128)S(1)} collective-permute-done((f32[656,128]{1,0:T(8,128)S(1)}, f32[656,128]{1,0:T(8,128)S(1)}, u32[]{:S(2)}, u32[]{:S(2)}) %collective-permute-start.2) | collective-permute-done | bytes 335904 | tf_op jit(solution)/shard_map/ppermute | solution.py:621
  21.7 16.0 %collective-permute-done.3.refs_1_ = f32[656,128]{1,0:T(8,128)S(1)} collective-permute-done((f32[656,128]{1,0:T(8,128)S(1)}, f32[656,128]{1,0:T(8,128)S(1)}, u32[]{:S(2)}, u32[]{:S(2)}) %collective-permute-start.3) | collective-permute-done | bytes 335904 | tf_op jit(solution)/shard_map/ppermute | solution.py:622
  37.7 3.2 %shard_map.122 = (f32[3,2,96,256]{3,2,1,0:T(8,128)S(1)}, f32[6,2,96,256]{3,2,1,0:T(8,128)S(1)}, f32[3,9,16,128]{3,2,1,0:T(8,128)S(1)}, f32[440,128]{1,0:T(8,128)...) custom-call(f32[656,128]{1,0:T(8,128)S(1)} %collective-permute-done.2.refs_0_, ...), custom_call_target="tpu_custom_call" | custom-call | tf_op jit(solution)/shard_map/pallas_call | solution.py:636
  40.9 0.1 collective-permute-start.4
  41.0 4.5 %collective-permute-start.5 = (f32[440,128]{1,0:T(8,128)S(1)}, f32[440,128]{1,0:T(8,128)S(1)}, u32[]{:S(2)}, u32[]{:S(2)}) collective-permute-start(f32[440,128]{1,0:T(8,128)S(1)} %get-tuple-element.39), channel_id=1, source_target_pairs={{8,16},{16,8},{24,32},{32,24},{40,48},{48,40},{56,64},{64,56},{72,... | collective-permute-start | bytes 675848 | tf_op jit(solution)/shard_map/ppermute | solution.py:622
  45.5 3.0 %collective-permute-done.4.refs_2_ = f32[440,128]{1,0:T(8,128)S(1)} collective-permute-done((f32[440,128]{1,0:T(8,128)S(1)}, f32[440,128]{1,0:T(8,128)S(1)}, u32[]{:S(2)}, u32[]{:S(2)}) %collective-permute-start.4) | collective-permute-done | bytes 225312 | tf_op jit(solution)/shard_map/ppermute | solution.py:621
  48.5 10.0 %collective-permute-done.5.refs_3_ = f32[440,128]{1,0:T(8,128)S(1)} collective-permute-done((f32[440,128]{1,0:T(8,128)S(1)}, f32[440,128]{1,0:T(8,128)S(1)}, u32[]{:S(2)}, u32[]{:S(2)}) %collective-permute-start.5) | collective-permute-done | bytes 225312 | tf_op jit(solution)/shard_map/ppermute | solution.py:622
  58.5 3.0 %shard_map.123 = (f32[3,2,96,256]{3,2,1,0:T(8,128)S(1)}, f32[6,2,96,256]{3,2,1,0:T(8,128)S(1)}, f32[3,9,16,128]{3,2,1,0:T(8,128)S(1)}, f32[440,128]{1,0:T(8,128)S(1)}, f32[440,128]{1,0:T(8,128)S(1)}) custom-call(f32[656,128]{1,0:T(8,128)S(1)} %collective-permute-done.2.refs_0_, f32[656,128]{1,0:T(8,128)S(1)} %collective-permute-done.3.refs_1_, ...), custom_call_target="tpu_custom_call" | custom-call | tf_op jit(solution)/shard_map/pallas_call | solution.py:636
  61.5 0.1 collective-permute-start.6
  61.6 4.5 %collective-permute-start.7 = (f32[440,128]{1,0:T(8,128)S(1)}, f32[440,128]{1,0:T(8,128)S(1)}, u32[]{:S(2)}, u32[]{:S(2)}) collective-permute-start(f32[440,128]{1,0:T(8,128)S(1)} %get-tuple-element.45), channel_id=1, source_target_pairs={{8,16},{16,8},{24,32},{32,24},{40,48},{48,40},{56,64},{64,56},{72,... | collective-permute-start | bytes 675848 | tf_op jit(solution)/shard_map/ppermute | solution.py:622
  66.1 2.1 %collective-permute-done.6.refs_2_ = f32[440,128]{1,0:T(8,128)S(1)} collective-permute-done((f32[440,128]{1,0:T(8,128)S(1)}, f32[440,128]{1,0:T(8,128)S(1)}, u32[]{:S(2)}, u32[]{:S(2)}) %collective-permute-start.6) | collective-permute-done | bytes 225312 | tf_op jit(solution)/shard_map/ppermute | solution.py:621
  68.2 10.0 %collective-permute-done.7.refs_3_ = f32[440,128]{1,0:T(8,128)S(1)} collective-permute-done((f32[440,128]{1,0:T(8,128)S(1)}, f32[440,128]{1,0:T(8,128)S(1)}, u32[]{:S(2)}, u32[]{:S(2)}) %collective-permute-start.7) | collective-permute-done | bytes 225312 | tf_op jit(solution)/shard_map/ppermute | solution.py:622
  78.2 2.9 %shard_map.124 = (f32[3,2,96,256]{3,2,1,0:T(8,128)S(1)}, f32[6,2,96,256]{3,2,1,0:T(8,128)S(1)}, f32[3,9,16,128]{3,2,1,0:T(8,128)S(1)}, f32[800,128]{1,0:T(8,128)S(1)}, f32[800,128]{1,0:T(8,128)S(1)}) custom-call(f32[656,128]{1,0:T(8,128)S(1)} %collective-permute-done.2.refs_0_, f32[656,128]{1,0:T(8,128)S(1)} %collective-permute-done.3.refs_1_, ...), custom_call_target="tpu_custom_call" | custom-call | tf_op jit(solution)/shard_map/pallas_call | solution.py:636
  81.1 0.1 collective-permute-start.8
  81.2 4.5 %collective-permute-start.9 = (f32[800,128]{1,0:T(8,128)S(1)}, f32[800,128]{1,0:T(8,128)S(1)}, u32[]{:S(2)}, u32[]{:S(2)}) collective-permute-start(f32[800,128]{1,0:T(8,128)S(1)} %get-tuple-element.50), channel_id=1, source_target_pairs={{8,16},{16,8},{24,32},{32,24},{40,48},{48,40},{56,64},{64,56},{72,... | collective-permute-start | bytes 1228808 | tf_op jit(solution)/shard_map/ppermute | solution.py:622
  85.7 5.2 %collective-permute-done.8.refs_2_ = f32[800,128]{1,0:T(8,128)S(1)} collective-permute-done((f32[800,128]{1,0:T(8,128)S(1)}, f32[800,128]{1,0:T(8,128)S(1)}, u32[]{:S(2)}, u32[]{:S(2)}) %collective-permute-start.8) | collective-permute-done | bytes 409632 | tf_op jit(solution)/shard_map/ppermute | solution.py:621
  90.9 10.2 %collective-permute-done.9.refs_3_ = f32[800,128]{1,0:T(8,128)S(1)} collective-permute-done((f32[800,128]{1,0:T(8,128)S(1)}, f32[800,128]{1,0:T(8,128)S(1)}, u32[]{:S(2)}, u32[]{:S(2)}) %collective-permute-start.9) | collective-permute-done | bytes 409632 | tf_op jit(solution)/shard_map/ppermute | solution.py:622
  101.1 3.0 %shard_map.125 = (f32[3,2,96,128]{3,2,1,0:T(8,128)}, f32[6,2,96,128]{3,2,1,0:T(8,128)}, f32[16,1024]{1,0:T(8,128)}, f32[2,16,1024]{2,1,0:T(8,128)}) custom-call(f32[656,128]{1,0:T(8,128)S(1)} %collective-permute-done.2.refs_0_, f32[656,128]{1,0:T(8,128)S(1)} %collective-permute-done.3.refs_1_, f32[800,128]{1,0:T(8,128)S(1)} %collective-permute-done.8.refs_2_, ...), custom_call_target="tpu_custom_call" | custom-call | tf_op jit(solution)/shard_map/pallas_call | solution.py:636
Async XLA Ops:
  0.6 8.4 %copy-start.8 = (s32[16,1024]{1,0:T(8,128)S(1)}, s32[16,1024]{1,0:T(8,128)}, u32[]{:S(2)}) copy-start(s32[16,1024]{1,0:T(8,128)} %wet.3) | copy-start | bytes 196612
  0.6 8.4 %copy-start.7 = (f32[16,1024]{1,0:T(8,128)S(1)}, f32[16,1024]{1,0:T(8,128)}, u32[]{:S(2)}) copy-start(f32[16,1024]{1,0:T(8,128)} %depth.3) | copy-start | bytes 196612
  0.7 8.4 %copy-start.2 = (f32[2,16,1024]{2,1,0:T(8,128)S(1)}, f32[2,16,1024]{2,1,0:T(8,128)}, u32[]{:S(2)}) copy-start(f32[2,16,1024]{2,1,0:T(8,128)} %momentum.3) | copy-start | bytes 393220
  0.7 8.4 %copy-start.6 = (f32[16,1024]{1,0:T(8,128)S(1)}, f32[16,1024]{1,0:T(8,128)}, u32[]{:S(2)}) copy-start(f32[16,1024]{1,0:T(8,128)} %surface.3) | copy-start | bytes 196612
  0.7 8.4 %copy-start.5 = (f32[2,96,128]{2,1,0:T(8,128)S(1)}, f32[2,96,128]{2,1,0:T(8,128)}, u32[]{:S(2)}) copy-start(f32[2,96,128]{2,1,0:T(8,128)} %shear.3) | copy-start | bytes 294916
  0.7 8.4 %copy-start.4 = (f32[2,96,128]{2,1,0:T(8,128)S(1)}, f32[2,96,128]{2,1,0:T(8,128)}, u32[]{:S(2)}) copy-start(f32[2,96,128]{2,1,0:T(8,128)} %first.3) | copy-start | bytes 294916
  0.7 8.4 %copy-start.3 = (f32[2,96,128]{2,1,0:T(8,128)S(1)}, f32[2,96,128]{2,1,0:T(8,128)}, u32[]{:S(2)}) copy-start(f32[2,96,128]{2,1,0:T(8,128)} %buoyancy.3) | copy-start | bytes 294916
  0.7 8.4 %copy-start = (f32[6,2,96,128]{3,2,1,0:T(8,128)S(1)}, f32[6,2,96,128]{3,2,1,0:T(8,128)}, u32[]{:S(2)}) copy-start(f32[6,2,96,128]{3,2,1,0:T(8,128)} %stress.3) | copy-start | bytes 1769476
  0.7 8.4 %copy-start.1 = (f32[3,2,96,128]{3,2,1,0:T(8,128)S(1)}, f32[3,2,96,128]{3,2,1,0:T(8,128)}, u32[]{:S(2)}) copy-start(f32[3,2,96,128]{3,2,1,0:T(8,128)} %motion.3) | copy-start | bytes 884740
  3.5 3.0 %collective-permute-start = (f32[96,128]{1,0:T(8,128)}, f32[96,128]{1,0:T(8,128)S(1)}, u32[]{:S(2)}, u32[]{:S(2)}) collective-permute-start(f32[96,128]{1,0:T(8,128)} %get-tuple-element.29), channel_id=1, source_target_pairs={{0,1},{1,0},{2,3},{3,2},{4,5},{5,4},{6,7},{7,6},{8,9},{9,8},{10,11... | collective-permute-start | bytes 147464 | tf_op jit(solution)/shard_map/ppermute | solution.py:621
  3.5 5.6 %collective-permute-start.1 = (f32[96,128]{1,0:T(8,128)}, f32[96,128]{1,0:T(8,128)S(1)}, u32[]{:S(2)}, u32[]{:S(2)}) collective-permute-start(f32[96,128]{1,0:T(8,128)} %get-tuple-element.30), channel_id=1, source_target_pairs={{1,2},{2,1},{3,4},{4,3},{5,6},{6,5},{9,10},{10,9},{11,12},{12,11},... | collective-permute-start | bytes 147464 | tf_op jit(solution)/shard_map/ppermute | solution.py:622
  11.3 10.4 %collective-permute-start.2 = (f32[656,128]{1,0:T(8,128)S(1)}, f32[656,128]{1,0:T(8,128)S(1)}, u32[]{:S(2)}, u32[]{:S(2)}) collective-permute-start(f32[656,128]{1,0:T(8,128)S(1)} %get-tuple-element.31), channel_id=1, source_target_pairs={{0,8},{8,0},{16,24},{24,16},{32,40},{40,32},{48,56},{56,48},{64,72... | collective-permute-start | bytes 1007624 | tf_op jit(solution)/shard_map/ppermute | solution.py:621
  13.0 24.7 %collective-permute-start.3 = (f32[656,128]{1,0:T(8,128)S(1)}, f32[656,128]{1,0:T(8,128)S(1)}, u32[]{:S(2)}, u32[]{:S(2)}) collective-permute-start(f32[656,128]{1,0:T(8,128)S(1)} %get-tuple-element.32), channel_id=1, source_target_pairs={{8,16},{16,8},{24,32},{32,24},{40,48},{48,40},{56,64},{64,56},{72,... | collective-permute-start | bytes 1007624 | tf_op jit(solution)/shard_map/ppermute | solution.py:622
  40.9 7.6 %collective-permute-start.4 = (f32[440,128]{1,0:T(8,128)S(1)}, f32[440,128]{1,0:T(8,128)S(1)}, u32[]{:S(2)}, u32[]{:S(2)}) collective-permute-start(f32[440,128]{1,0:T(8,128)S(1)} %get-tuple-element.38), channel_id=1, source_target_pairs={{0,8},{8,0},{16,24},{24,16},{32,40},{40,32},{48,56},{56,48},{64,72... | collective-permute-start | bytes 675848 | tf_op jit(solution)/shard_map/ppermute | solution.py:621
  41.0 17.5 %collective-permute-start.5 = (f32[440,128]{1,0:T(8,128)S(1)}, f32[440,128]{1,0:T(8,128)S(1)}, u32[]{:S(2)}, u32[]{:S(2)}) collective-permute-start(f32[440,128]{1,0:T(8,128)S(1)} %get-tuple-element.39), channel_id=1, source_target_pairs={{8,16},{16,8},{24,32},{32,24},{40,48},{48,40},{56,64},{64,56},{72,... | collective-permute-start | bytes 675848 | tf_op jit(solution)/shard_map/ppermute | solution.py:622
  61.5 6.7 %collective-permute-start.6 = (f32[440,128]{1,0:T(8,128)S(1)}, f32[440,128]{1,0:T(8,128)S(1)}, u32[]{:S(2)}, u32[]{:S(2)}) collective-permute-start(f32[440,128]{1,0:T(8,128)S(1)} %get-tuple-element.44), channel_id=1, source_target_pairs={{0,8},{8,0},{16,24},{24,16},{32,40},{40,32},{48,56},{56,48},{64,72... | collective-permute-start | bytes 675848 | tf_op jit(solution)/shard_map/ppermute | solution.py:621
  61.6 16.6 %collective-permute-start.7 = (f32[440,128]{1,0:T(8,128)S(1)}, f32[440,128]{1,0:T(8,128)S(1)}, u32[]{:S(2)}, u32[]{:S(2)}) collective-permute-start(f32[440,128]{1,0:T(8,128)S(1)} %get-tuple-element.45), channel_id=1, source_target_pairs={{8,16},{16,8},{24,32},{32,24},{40,48},{48,40},{56,64},{64,56},{72,... | collective-permute-start | bytes 675848 | tf_op jit(solution)/shard_map/ppermute | solution.py:622
  81.1 9.8 %collective-permute-start.8 = (f32[800,128]{1,0:T(8,128)S(1)}, f32[800,128]{1,0:T(8,128)S(1)}, u32[]{:S(2)}, u32[]{:S(2)}) collective-permute-start(f32[800,128]{1,0:T(8,128)S(1)} %get-tuple-element.49), channel_id=1, source_target_pairs={{0,8},{8,0},{16,24},{24,16},{32,40},{40,32},{48,56},{56,48},{64,72... | collective-permute-start | bytes 1228808 | tf_op jit(solution)/shard_map/ppermute | solution.py:621
  81.2 19.9 %collective-permute-start.9 = (f32[800,128]{1,0:T(8,128)S(1)}, f32[800,128]{1,0:T(8,128)S(1)}, u32[]{:S(2)}, u32[]{:S(2)}) collective-permute-start(f32[800,128]{1,0:T(8,128)S(1)} %get-tuple-element.50), channel_id=1, source_target_pairs={{8,16},{16,8},{24,32},{32,24},{40,48},{48,40},{56,64},{64,56},{72,... | collective-permute-start | bytes 1228808 | tf_op jit(solution)/shard_map/ppermute | solution.py:622
